TPU v7x, 32 devices: a whole 2x2x4 slice. The times are simulated.
32 devices in a mesh: section: 16 (over z, y, core), mp: 2 (over x).
Axes of the slice: x: 2, y: 2, z: 4, core: 2. Of those that a mesh axis runs over, the one named last changes fastest.
Arguments:
- gate_weight: bfloat16 [2, 2048, 5632], P(None, 'section', 'mp'), may hold values from -6 to 6
- up_weight: bfloat16 [2, 2048, 5632], P(None, 'section', 'mp'), may hold values from -6 to 6
- hidden_map: int32 [2048], replicated, may hold values from 0 to 2047, as said below
- ffn_map: int32 [5376], replicated, may hold values from 0 to 5631, as said below
Outputs:
- grown_gate: bfloat16 [2, 2, 2048, 11008], P(None, None, 'section', 'mp')
- grown_up: bfloat16 [2, 2, 2048, 11008], P(None, None, 'section', 'mp')
Inputs may be any that keep to these rules, and one draw needn't show every extreme that they name: `hidden_map`: entry i names the old unit copied by new unit 2048 + i. Within each aligned block of 128 entries, at most 8 entries name units of any one block of 128 old units, and some block of old units is named exactly 8 times. `ffn_map`: entry j names the FFN unit of the next layer copied by added unit j % 2688 of FFN block j // 2688. Within each aligned block of 2688 entries, at most 1344 entries name units of any one block of 2816 old FFN units, and in each aligned block some block of old units is named exactly 1344 times.
All inputs are finite; a program needn't handle non-finite values.
Results may differ from a plain program's by a relative error of at most 0.001.
Values may be sent and summed in bfloat16 or wider, within the bound.
No kernel may reach another device: no remote copies, remote signals or barrier semaphores. Data moves between devices by JAX's collectives and lax.ppermute only.
A program may use at most 64 MiB of HBM per device.

v0:
```python
import jax
import jax.numpy as jnp
from jax import lax
from jax.sharding import PartitionSpec as P


def local(gate_weight, up_weight, hidden_map, ffn_map):
    layers, shard_rows, narrow = gate_weight.shape
    blocks = lax.axis_size("section")
    splits = lax.axis_size("mp")
    section_rank = lax.axis_index("section")
    column_rank = lax.axis_index("mp")
    d_old = shard_rows * blocks
    extra_dev = ffn_map.shape[0] // splits
    route_cap = max(1, shard_rows // blocks)
    next_pick = jnp.minimum(jnp.arange(layers, dtype=jnp.int32) + 1, layers - 1) - 1
    counts = (
        jax.ops.segment_sum(jnp.ones((d_old,), jnp.float32), hidden_map, num_segments=d_old) + 1.0
    )
    own_rows = section_rank * shard_rows + jnp.arange(shard_rows, dtype=jnp.int32)
    copied = lax.dynamic_slice_in_dim(hidden_map, section_rank * shard_rows, shard_rows)
    mine_extra = lax.dynamic_slice_in_dim(ffn_map, column_rank * extra_dev, extra_dev)
    table = hidden_map.reshape(blocks, shard_rows)
    owner = table // shard_rows
    wanted = owner == section_rank
    order = jnp.cumsum(wanted.astype(jnp.int32), axis=1) - 1
    slot_ids = jnp.arange(route_cap, dtype=jnp.int32)
    selected = wanted[:, None, :] & (order[:, None, :] == slot_ids[None, :, None])
    sent_rows = jnp.sum(jnp.where(selected, (table % shard_rows)[:, None, :], 0), axis=2).reshape(
        -1
    )
    mine_owner = copied // shard_rows
    row_ids = jnp.arange(shard_rows, dtype=jnp.int32)
    earlier = row_ids[None, :] < row_ids[:, None]
    rank_among = jnp.sum(
        (earlier & (mine_owner[None, :] == mine_owner[:, None])).astype(jnp.int32), axis=1
    )
    landing = mine_owner * route_cap + rank_among
    pair = (gate_weight, up_weight)
    later = tuple((portion[1:] for portion in pair))
    rows_here = pair[0].shape[1]

    def pick_columns(carried, pieces):
        amount = pieces[0].shape[2]
        inside = (mine_extra >= 0) & (mine_extra < amount)
        bounded = jnp.clip(mine_extra, 0, amount - 1)
        return tuple(
            (
                jnp.where(inside, jnp.take(portion, bounded, axis=2), current)
                for current, portion in zip(carried, pieces)
            )
        )

    empty_extra = jnp.zeros((layers - 1, rows_here, extra_dev), jnp.bfloat16)
    extras = pick_columns(
        (empty_extra, empty_extra),
        (
            lax.all_gather(later[0], "mp", axis=2, tiled=True),
            lax.all_gather(later[1], "mp", axis=2, tiled=True),
        ),
    )
    own_gate, own_up = tuple(
        (
            jnp.concatenate([portion, added[next_pick]], axis=2)
            for portion, added in zip(pair, extras)
        )
    )
    arrived = (
        lax.all_to_all(
            jnp.take(own_gate, sent_rows, axis=1),
            "section",
            split_axis=1,
            concat_axis=1,
            tiled=True,
        ),
        lax.all_to_all(
            jnp.take(own_up, sent_rows, axis=1), "section", split_axis=1, concat_axis=1, tiled=True
        ),
    )
    grown_gate = jnp.stack([own_gate, jnp.take(arrived[0], landing, axis=1)], axis=1)
    grown_up = jnp.stack([own_up, jnp.take(arrived[1], landing, axis=1)], axis=1)
    divisor = jnp.stack([counts[own_rows], counts[copied]])[None, :, :, None]
    return (
        (grown_gate.astype(jnp.float32) / divisor).astype(jnp.bfloat16),
        (grown_up.astype(jnp.float32) / divisor).astype(jnp.bfloat16),
    )


def solution(mesh):
    in_specs = (P(None, "section", "mp"), P(None, "section", "mp"), P(), P())
    out_specs = (P(None, None, "section", "mp"), P(None, None, "section", "mp"))
    return jax.shard_map(local, mesh=mesh, in_specs=in_specs, out_specs=out_specs, check_vma=False)
```

profile of v0, /device:TPU:13, one launch (start us, length us, event | category | flops | bytes accessed | tf_op | source)
XLA Modules:
  0.0 311.3 jit_solution(16628258519334611870)
XLA Ops:
  7.2 0.0 slice-start
  7.2 0.0 all-gather.3.cloned.1.call-start
  7.2 1.2 slice.6
  8.4 0.0 copy-start.3
  8.5 1.1 copy.26
  9.6 0.0 all-gather.3.cloned.1.call-update
  9.6 0.0 all-gather.5.cloned.1.call-start
  9.7 0.0 slice-done
  9.7 1.1 copy.27
  10.8 0.0 all-gather.5.cloned.1.call-update
  10.8 0.0 copy-done.3
  10.8 0.0 copy-start.4
  10.9 0.0 copy-start.5
  10.9 0.0 copy-start.6
  10.9 1.5 copy.20
  12.4 0.0 copy-done.4
  12.4 1.5 copy.23
  13.9 0.0 copy-done.5
  13.9 0.3 reduce_window_sum.11
  14.2 0.3 select_reduce_fusion
  14.5 0.1 reshape.175
  14.7 0.0 copy-done.6
  14.7 0.1 compare_and_fusion
  14.8 22.0 %all-gather.3.cloned.1.call-done = bf16[1,128,5632]{1,2,0:T(8,128)(2,1)} async-done(((bf16[1,128,2816]{1,2,0:T(8,128)(2,1)}), bf16[1,128,5632]{1,2,0:T(8,128)(2,1)}) %all-gather.3.cloned.1.call-update) | async-done | bytes 1441808 | tf_op jit(solution)/shard_map/all_gather | solution.py:58
  36.8 7.8 %gather_fusion.2 = bf16[2688,128]{1,0:T(8,128)(2,1)} fusion(bf16[128,5632]{0,1:T(8,128)(2,1)} %bitcast.69, s32[3072]{0:T(1024)S(1)} %pad_clamp_fusion), kind=kCustom, calls=%fused_computation.clone | custom fusion | bytes 1387008 | tf_op jit(solution)/shard_map/jit(_take)/gather | solution.py:49
  44.6 20.0 %all-gather.5.cloned.1.call-done = bf16[1,128,5632]{1,2,0:T(8,128)(2,1)} async-done(((bf16[1,128,2816]{1,2,0:T(8,128)(2,1)}), bf16[1,128,5632]{1,2,0:T(8,128)(2,1)}) %all-gather.5.cloned.1.call-update) | async-done | bytes 1441808 | tf_op jit(solution)/shard_map/all_gather | solution.py:59
  64.6 7.5 %gather_fusion.5 = bf16[2688,128]{1,0:T(8,128)(2,1)} fusion(bf16[128,5632]{0,1:T(8,128)(2,1)} %bitcast.70, s32[3072]{0:T(1024)S(1)} %pad_clamp_fusion), kind=kCustom, calls=%fused_computation.2.clone | custom fusion | bytes 1387008 | tf_op jit(solution)/shard_map/jit(_take)/gather | solution.py:49
  72.2 4.4 %fusion.7 = (bf16[128,2688]{0,1:T(8,128)(2,1)}, bf16[128,2688]{0,1:T(8,128)(2,1)}) fusion(bf16[2688,128]{1,0:T(8,128)(2,1)} %gather_fusion.5, pred[2688]{0:T(1024)(128)(4,1)S(1)} %get-tuple-element.12, pred[2688]{0:T(1024)(128)(4,1)S(1)} %get-tuple-element.14, bf16[2688,128]{1,0:T(8,128)(2,1)} %gather_fusion.2), kind=kLoop, calls=%fused_computation.25 | loop fusion | flops 1376256 | bytes 2757888 | tf_op jit(solution)/shard_map/gather | solution.py:64
  76.6 2.2 copy.22
  78.8 2.2 copy.19
  81.0 1.8 broadcast.225
  82.8 0.0 copy-start
  82.9 1.1 copy-done
  83.9 4.1 %pad_maximum_fusion.1 = bf16[2,128,5504]{2,0,1:T(2,128)(2,1)} fusion(bf16[2,128,2688]{2,0,1:T(2,128)(2,1)S(1)} %broadcast.225, bf16[2,128,2816]{2,0,1:T(2,128)(2,1)S(1)} %copy.23), kind=kLoop, calls=%fused_computation.18 | loop fusion | flops 5636096 | bytes 5636096 | tf_op jit(solution)/shard_map/concatenate | solution.py:64
  88.0 11.9 %gather_fusion.6 = bf16[128,2,5504]{2,1,0:T(2,128)(2,1)} fusion(bf16[2,128,5504]{2,0,1:T(2,128)(2,1)} %pad_maximum_fusion.1, s32[1024]{0:T(1024)S(1)} %pad_clamp_fusion.4), kind=kCustom, calls=%fused_computation.4.clone | custom fusion | bytes 5636608 | tf_op jit(solution)/shard_map/jit(_take)/gather | solution.py:77
  100.0 1.8 broadcast.224
  101.8 0.0 copy-start.1
  101.8 1.1 copy-done.1
  102.9 4.1 %pad_maximum_fusion = bf16[2,128,5504]{2,0,1:T(2,128)(2,1)} fusion(bf16[2,128,2688]{2,0,1:T(2,128)(2,1)S(1)} %broadcast.224, bf16[2,128,2816]{2,0,1:T(2,128)(2,1)S(1)} %copy.20), kind=kLoop, calls=%fused_computation.17 | loop fusion | flops 5636096 | bytes 5636096 | tf_op jit(solution)/shard_map/concatenate | solution.py:64
  107.0 11.6 %gather_fusion.3 = bf16[128,2,5504]{2,1,0:T(2,128)(2,1)} fusion(bf16[2,128,5504]{2,0,1:T(2,128)(2,1)} %pad_maximum_fusion, s32[1024]{0:T(1024)S(1)} %pad_clamp_fusion.4), kind=kCustom, calls=%fused_computation.1.clone | custom fusion | bytes 5636608 | tf_op jit(solution)/shard_map/jit(_take)/gather | solution.py:70
  118.6 9.4 %fusion.3 = (bf16[2,128,5504]{2,0,1:T(2,128)(2,1)S(1)}, bf16[2,128,5504]{2,0,1:T(2,128)(2,1)}) fusion(bf16[128,2,5504]{2,1,0:T(2,128)(2,1)} %gather_fusion.6, pred[128]{0:T(512)(128)(4,1)S(1)} %compare_and_fusion.3, bf16[128,2,5504]{2,1,0:T(2,128)(2,1)} %gather_fusion.3), kind=kLoop, calls=%fused_computation.20 | loop fusion | flops 2818048 | bytes 11272320 | tf_op jit(solution)/shard_map/jit(_take)/select_n | solution.py:77
  128.0 69.1 %all_to_all.10 = bf16[2,128,5504]{2,0,1:T(2,128)(2,1)} all-to-all(bf16[2,128,5504]{2,0,1:T(2,128)(2,1)S(1)} %get-tuple-element.23), channel_id=1, replica_groups=mesh['section'=16,'mp'=2] {'section'}, dimensions={1} | all-to-all | bytes 5636096 | tf_op jit(solution)/shard_map/all_to_all | solution.py:76
  197.1 5.6 %all-to-all-start = ((bf16[2,128,5504]{2,0,1:T(2,128)(2,1)}), bf16[2,128,5504]{2,0,1:T(2,128)(2,1)}, u32[]{:S(2)}, u32[]{:S(2)}) async-start(bf16[2,128,5504]{2,0,1:T(2,128)(2,1)} %get-tuple-element.24), calls=%async_computation | async-start | bytes 5636096 | tf_op jit(solution)/shard_map/all_to_all | solution.py:69
  202.8 11.7 %scatter_fusion = f32[2048]{0:T(1024)S(1)} fusion(f32[2048]{0:T(1024)S(1)} %broadcast_in_dim.63, s32[2048]{0:T(1024)S(1)} %copy-done.5, f32[2048]{0:T(1024)S(1)} %broadcast_in_dim.63), kind=kCustom, calls=%fused_computation.8 | custom fusion | flops 2048 | bytes 32768 | tf_op jit(solution)/shard_map/scatter-add | solution.py:18
  214.5 0.1 compare_select_fusion.4
  214.6 1.4 gather_fusion.1
  216.0 1.1 gather_fusion
  217.2 0.2 convert_reduce_fusion
  217.4 0.0 copy-start.2
  217.4 5.5 %fusion.20 = bf16[2,1,128,5504]{3,0,2,1:T(2,128)(2,1)} fusion(bf16[2,128,2688]{2,0,1:T(2,128)(2,1)} %copy-done, bf16[2,128,2816]{2,0,1:T(2,128)(2,1)S(1)} %copy.23), kind=kLoop, calls=%fused_computation.69 | loop fusion | flops 5636096 | bytes 5636096 | tf_op jit(solution)/shard_map/stack | solution.py:81
  222.9 0.0 copy-done.2
  222.9 4.1 %fusion.19 = bf16[2,1,128,5504]{3,0,2,1:T(2,128)(2,1)} fusion(bf16[2,128,2688]{2,0,1:T(2,128)(2,1)S(1)} %copy-done.2, bf16[2,128,2816]{2,0,1:T(2,128)(2,1)S(1)} %copy.20), kind=kLoop, calls=%fused_computation.68 | loop fusion | flops 5636096 | bytes 5636096 | tf_op jit(solution)/shard_map/stack | solution.py:80
  227.0 11.1 %gather_fusion.7 = bf16[128,2,5504]{2,1,0:T(2,128)(2,1)S(1)} fusion(bf16[2,128,5504]{2,0,1:T(2,128)(2,1)} %all_to_all.10, s32[1024]{0:T(1024)S(1)} %pad_clamp_fusion.3), kind=kCustom, calls=%fused_computation.5.clone | custom fusion | bytes 5636608 | tf_op jit(solution)/shard_map/jit(_take)/gather | solution.py:81
  238.2 27.6 %all-to-all-done = bf16[2,128,5504]{2,0,1:T(2,128)(2,1)} async-done(((bf16[2,128,5504]{2,0,1:T(2,128)(2,1)}), bf16[2,128,5504]{2,0,1:T(2,128)(2,1)}, u32[]{:S(2)}, u32[]{:S(2)}) %all-to-all-start) | async-done | bytes 2818080 | tf_op jit(solution)/shard_map/all_to_all | solution.py:69
  265.7 11.7 %gather_fusion.4 = bf16[128,2,5504]{2,1,0:T(2,128)(2,1)} fusion(bf16[2,128,5504]{2,0,1:T(2,128)(2,1)} %all-to-all-done, s32[1024]{0:T(1024)S(1)} %pad_clamp_fusion.3), kind=kCustom, calls=%fused_computation.3.clone | custom fusion | bytes 5636608 | tf_op jit(solution)/shard_map/jit(_take)/gather | solution.py:80
  277.4 7.0 %fusion.5 = (bf16[2,1,128,5504]{3,0,2,1:T(2,128)(2,1)S(1)}, bf16[2,1,128,5504]{3,0,2,1:T(2,128)(2,1)S(1)}) fusion(bf16[128,2,5504]{2,1,0:T(2,128)(2,1)S(1)} %gather_fusion.7, pred[128]{0:T(512)(128)(4,1)S(1)} %get-tuple-element.8, bf16[128,2,5504]{2,1,0:T(2,128)(2,1)} %gather_fusion.4), kind=kLoop, calls=%fused_computation.22 | loop fusion | flops 2818048 | bytes 11272320 | tf_op jit(solution)/shard_map/stack | solution.py:81
  284.4 13.7 %fusion = (bf16[2,2,128,5504]{3,0,2,1:T(2,128)(2,1)S(1)}, bf16[2,2,128,5504]{3,0,2,1:T(2,128)(2,1)S(1)}) fusion(bf16[2,1,128,5504]{3,0,2,1:T(2,128)(2,1)S(1)} %get-tuple-element.21, bf16[2,1,128,5504]{3,0,2,1:T(2,128)(2,1)} %fusion.20, f32[2,128]{1,0:T(2,128)S(1)} %pad_maximum_fusion.2, bf16[2,1,128,5504]{3,0,2,1:T(2,128)(2,1)S(1)} %get-tuple-element.22, ...), kind=kLoop, calls=%fused_computation.10 | loop fusion | flops 22544384 | bytes 22545408 | tf_op jit(solution)/shard_map/convert_element_type | solution.py:85
  298.1 3.0 copy.25
  301.2 3.0 copy.24
  (13 shorter events, 0.1 us)
Async XLA Ops:
  7.2 2.5 slice-start
  7.2 29.6 %all-gather.3.cloned.1.call-start = ((), (), s32[]{:S(2)}) async-start(), calls=%async_computation.2 | async-start | bytes 2162688 | tf_op jit(solution)/shard_map/all_gather | solution.py:58
  8.4 2.4 copy-start.3
  9.6 55.0 %all-gather.5.cloned.1.call-start = ((), (), s32[]{:S(2)}) async-start(), calls=%async_computation.3 | async-start | bytes 2162688 | tf_op jit(solution)/shard_map/all_gather | solution.py:59
  10.8 1.5 copy-start.4
  10.9 3.0 copy-start.5
  10.9 3.8 %copy-start.6 = (s32[5376]{0:T(1024)S(1)}, s32[5376]{0:T(1024)}, u32[]{:S(2)}) copy-start(s32[5376]{0:T(1024)} %param.11) | copy-start | bytes 64516
  82.8 1.1 copy-start
  101.8 1.1 copy-start.1
  197.1 68.6 %all-to-all-start = ((bf16[2,128,5504]{2,0,1:T(2,128)(2,1)}), bf16[2,128,5504]{2,0,1:T(2,128)(2,1)}, u32[]{:S(2)}, u32[]{:S(2)}) async-start(bf16[2,128,5504]{2,0,1:T(2,128)(2,1)} %get-tuple-element.24), calls=%async_computation | async-start | bytes 5636096 | tf_op jit(solution)/shard_map/all_to_all | solution.py:69
  217.4 5.6 %copy-start.2 = (bf16[2,128,2688]{2,0,1:T(2,128)(2,1)S(1)}, bf16[2,128,2688]{2,0,1:T(2,128)(2,1)}, u32[]{:S(2)}) copy-start(bf16[2,128,2688]{2,0,1:T(2,128)(2,1)} %copy-done.1) | copy-start | bytes 4128772
Sparse Core Ops, SparseCore 0:
  10.1 26.6 all-gather.2
  38.9 25.6 all-gather.4
where the time goes:
time: 316 us; the launch traced here: 311 us
  local copies, waits for them, and re-layouts  87.2 us (28%)
  waiting for transfers between devices  69.6 us (22%)
  blocking collectives  69.1 us (22%)
  other arithmetic  65.1 us (21%)
  between operations  14.6 us (5%)
  starting transfers between devices  5.71 us (2%)
    all_to_all x1, blocking collectives, local(): lax.all_to_all(jnp.take(own_up, sent_rows, axis=1), 'section', split_axis...  69.1 us
    all_to_all x1, waiting for transfers between devices, local(): lax.all_to_all(jnp.take(own_gate, sent_rows, axis=1), 'section', split_ax...  27.6 us
    all_gather x1, waiting for transfers between devices, local(): lax.all_gather(later[0], 'mp', axis=2, tiled=True)  22 us
    all_gather x1, waiting for transfers between devices, local(): lax.all_gather(later[1], 'mp', axis=2, tiled=True)  20 us
    gather x2, local copies, waits for them, and re-layouts, pick_columns(): jnp.take(portion, bounded, axis=2)  15.3 us
    convert_element_type x1, other arithmetic, local(): (grown_up.astype(jnp.float32) / divisor).astype(jnp.bfloat16)  13.7 us
    unnamed x20, local copies, waits for them, and re-layouts  13.6 us
    another operation x2, other arithmetic, local(): jnp.stack([own_up, jnp.take(arrived[1], landing, axis=1)], axis=1)  12.5 us
  transfers between devices with their start and end apart: 3, of which 3 were waited for; matrix products, arithmetic and copies ran while one was open for 15% of the time, Pallas kernels for 0%

commit v1 on v0

--- a/solution.py
+++ b/solution.py
@@ -1,11 +1,589 @@
+import functools
+
 import jax
 import jax.numpy as jnp
 from jax import lax
+from jax.experimental import pallas as pl
+from jax.experimental.pallas import tpu as pltpu
 from jax.sharding import PartitionSpec as P
 
 
-def local(gate_weight, up_weight, hidden_map, ffn_map):
-    layers, shard_rows, narrow = gate_weight.shape
+F32 = jnp.float32
+BF16 = jnp.bfloat16
+I32 = jnp.int32
+VMEM = pl.BlockSpec(memory_space=pltpu.VMEM)
+HBM = pl.BlockSpec(memory_space=pl.ANY)
+K_CHUNK = 256
+PARAMS = pltpu.CompilerParams(vmem_limit_bytes=32 << 20)
+
+
+def iota(shape, axis):
+    return lax.broadcasted_iota(I32, shape, axis)
+
+
+def count_of(table, ids):
+    total = jnp.zeros((ids.shape[0], table.shape[1]), F32)
+    for block in range(table.shape[0]):
+        total += jnp.where(table[block : block + 1, :] == ids, 1.0, 0.0)
+    return 1.0 + jnp.sum(total, axis=1, keepdims=True)
+
+
+def pick_matrix(table, me, cap, key_ref, within_ref, targets):
+    blocks, rows = table.shape
+    owner = lax.div(table, jnp.full_like(table, rows))
+    within_ref[...] = table - owner * rows
+    wanted = owner == me
+    before = (iota((rows, rows), 0) < iota((rows, rows), 1)).astype(F32).astype(BF16)
+    order = jnp.dot(wanted.astype(F32).astype(BF16), before, preferred_element_type=F32)
+    key_ref[...] = jnp.where(wanted, order.astype(I32), -1)
+    slot = iota((cap, rows), 0)
+    parts = []
+    for target in targets:
+        line = pl.ds(target, 1)
+        parts.append(jnp.where(key_ref[line, :] == slot, within_ref[line, :], 0).astype(F32))
+    row_of = jnp.sum(jnp.concatenate(parts, axis=0), axis=1, keepdims=True).astype(I32)
+    pick = (iota((blocks * cap, rows), 1) == row_of).astype(F32).astype(BF16)
+    return pick, count_of(table, row_of + me * rows)
+
+
+def land_matrix(mine, blocks, cap):
+    rows = mine.shape[1]
+    across, down = iota((rows, rows), 1), iota((rows, rows), 0)
+    column = jnp.sum(
+        jnp.where(across == down, mine, 0).astype(F32), axis=1, keepdims=True
+    ).astype(I32)
+    owner_row = lax.div(mine, jnp.full_like(mine, rows))
+    owner = lax.div(column, jnp.full_like(column, rows))
+    earlier = (across < down) & (owner == owner_row)
+    rank = jnp.sum(jnp.where(earlier, 1.0, 0.0), axis=1, keepdims=True).astype(I32)
+    return (iota((rows, blocks * cap), 1) == owner * cap + rank).astype(F32).astype(BF16)
+
+
+def onehot_dot(left, index_row, extent):
+    total = None
+    for start in range(0, extent, K_CHUNK):
+        size = min(K_CHUNK, extent - start)
+        mask = iota((size, index_row.shape[1]), 0) == index_row - start
+        term = jnp.dot(
+            left[:, start : start + size],
+            mask.astype(F32).astype(BF16),
+            preferred_element_type=F32,
+        )
+        total = term if total is None else total + term
+    return total
+
+
+def send_kernel(layer, cap, halves, table_ref, gate_ref, up_ref, *refs):
+    *sent_refs, map_ref, in_ref, held_ref, key_ref, within_ref, map_sem, in_sems, out_sems = refs
+    blocks = table_ref.shape[0]
+    map_load = pltpu.make_async_copy(table_ref, map_ref, map_sem)
+    map_load.start()
+    narrow = gate_ref.shape[2]
+    steps = in_sems.shape[1]
+    width = narrow // steps
+    me = lax.axis_index("section")
+    loads = []
+    for side, ref in enumerate((gate_ref, up_ref)):
+        for step in range(steps):
+            at = side * narrow + step * width
+            loads.append(
+                pltpu.make_async_copy(
+                    ref.at[layer, :, pl.ds(step * width, width)],
+                    in_ref.at[:, pl.ds(at, width)],
+                    in_sems.at[side, step],
+                )
+            )
+            loads[-1].start()
+    if halves:
+        half = blocks // 2
+        base = lax.div(me, half) * half
+        targets = [base + p for p in range(half)] + [me ^ p for p in range(half, blocks)]
+    else:
+        targets = list(range(blocks))
+    map_load.wait()
+    pick, count = pick_matrix(map_ref[...], me, cap, key_ref, within_ref, targets)
+    scale = 1.0 / count
+    stores = []
+    for number, load in enumerate(loads):
+        at = number * width
+        load.wait()
+        rows = jnp.dot(pick, in_ref[:, at : at + width], preferred_element_type=F32)
+        held_ref[:, at : at + width] = (rows * scale).astype(BF16)
+        first = 0
+        for piece, ref in enumerate(sent_refs):
+            count_here = ref.shape[0]
+            stores.append(
+                pltpu.make_async_copy(
+                    held_ref.at[pl.ds(first, count_here), pl.ds(at, width)],
+                    ref.at[:, pl.ds(at, width)],
+                    out_sems.at[number, piece],
+                )
+            )
+            stores[-1].start()
+            first += count_here
+    for store in stores:
+        store.wait()
+
+
+def send_rows(table, gate, up, layer, cap, halves):
+    _, rows, narrow = gate.shape
+    blocks = table.shape[0]
+    steps = 2
+    if halves:
+        counts = [blocks // 2 * cap] + [cap] * (blocks // 2)
+    else:
+        counts = [blocks * cap]
+    return pl.pallas_call(
+        functools.partial(send_kernel, layer, cap, halves),
+        out_shape=[jax.ShapeDtypeStruct((count, 2 * narrow), BF16) for count in counts],
+        in_specs=[HBM] * 3,
+        out_specs=[HBM] * len(counts),
+        scratch_shapes=[
+            pltpu.VMEM((blocks, rows), I32),
+            pltpu.VMEM((rows, 2 * narrow), BF16),
+            pltpu.VMEM((blocks * cap, 2 * narrow), BF16),
+            pltpu.VMEM((blocks, rows), I32),
+            pltpu.VMEM((blocks, rows), I32),
+            pltpu.SemaphoreType.DMA(()),
+            pltpu.SemaphoreType.DMA((2, steps)),
+            pltpu.SemaphoreType.DMA((2 * steps, len(counts))),
+        ],
+        cost_estimate=pl.CostEstimate(
+            flops=4 * blocks * cap * rows * narrow,
+            bytes_accessed=8 * rows * narrow,
+            transcendentals=0,
+        ),
+    )(table, gate, up)
+
+
+def load_weights(layers, gate_ref, up_ref, in_ref, sems):
+    loads = []
+    for at, layer in enumerate(layers):
+        for side, ref in enumerate((gate_ref, up_ref)):
+            loads.append(
+                pltpu.make_async_copy(ref.at[layer], in_ref.at[at, side], sems.at[at, side])
+            )
+            loads[-1].start()
+    return loads
+
+
+def own_kernel(table_ref, ids_ref, gate_ref, up_ref, out_ref, in_ref, own_ref, sems):
+    layers, rows, narrow = gate_ref.shape
+    loads = load_weights([layers - 1], gate_ref, up_ref, in_ref, sems)
+    me = lax.axis_index("section")
+    scale = 1.0 / count_of(table_ref[...], iota((rows, 1), 0) + me * rows)
+    for side, load in enumerate(loads):
+        load.wait()
+        own_ref[side * rows : (side + 1) * rows] = (in_ref[0, side].astype(F32) * scale).astype(BF16)
+    for s in range(ids_ref.shape[0]):
+        out_ref[s] = onehot_dot(own_ref, ids_ref[s : s + 1, :], narrow).astype(BF16)
+
+
+def own_rows(table, ids, gate, up):
+    _, rows, narrow = gate.shape
+    turns, width = ids.shape
+    return pl.pallas_call(
+        own_kernel,
+        out_shape=jax.ShapeDtypeStruct((turns, 2 * rows, width), BF16),
+        in_specs=[VMEM, VMEM, HBM, HBM],
+        out_specs=VMEM,
+        scratch_shapes=[
+            pltpu.VMEM((1, 2, rows, narrow), BF16),
+            pltpu.VMEM((2 * rows, narrow), BF16),
+            pltpu.SemaphoreType.DMA((1, 2)),
+        ],
+        cost_estimate=pl.CostEstimate(
+            flops=4 * rows * narrow * width * turns,
+            bytes_accessed=8 * rows * narrow,
+            transcendentals=0,
+        ),
+        name="own_rows",
+    )(table, ids, gate, up)
+
+
+def land_kernel(cap, table_ref, land_ref):
+    mine = table_ref[pl.ds(lax.axis_index("section"), 1), :]
+    land_ref[...] = land_matrix(mine, table_ref.shape[0], cap)
+
+
+def land_rows(table, cap):
+    blocks, rows = table.shape
+    return pl.pallas_call(
+        functools.partial(land_kernel, cap),
+        out_shape=jax.ShapeDtypeStruct((rows, blocks * cap), BF16),
+        in_specs=[VMEM],
+        out_specs=VMEM,
+        compiler_params=PARAMS,
+        name="land_rows",
+    )(table)
+
+
+def arrive_kernel(land_ref, ids_ref, *refs):
+    *came_refs, rows_ref, out_ref, held_ref, sems = refs
+    narrow = rows_ref.shape[1]
+    rows = land_ref.shape[0]
+    cap = came_refs[1].shape[0]
+    half = len(came_refs) - 1
+    me = lax.axis_index("section")
+    starts = [lax.div(me, half) * half] + [me ^ p for p in range(half, 2 * half)]
+    loads = []
+    for piece, (ref, start) in enumerate(zip(came_refs, starts)):
+        where = pl.ds(pl.multiple_of(start * cap, cap), ref.shape[0])
+        loads.append(pltpu.make_async_copy(ref, held_ref.at[where, :], sems.at[piece]))
+        loads[-1].start()
+    for load in loads:
+        load.wait()
+    for side in range(2):
+        rows_ref[side * rows : (side + 1) * rows] = jnp.dot(
+            land_ref[...],
+            held_ref[:, side * narrow : (side + 1) * narrow],
+            preferred_element_type=F32,
+        ).astype(BF16)
+    for s in range(ids_ref.shape[0]):
+        out_ref[s] = onehot_dot(rows_ref, ids_ref[s : s + 1, :], narrow).astype(BF16)
+
+
+def arrive_rows(land, ids, came):
+    rows, slots = land.shape
+    narrow = came[0].shape[1] // 2
+    turns, width = ids.shape
+    return pl.pallas_call(
+        arrive_kernel,
+        out_shape=(
+            jax.ShapeDtypeStruct((2 * rows, narrow), BF16),
+            jax.ShapeDtypeStruct((turns, 2 * rows, width), BF16),
+        ),
+        in_specs=[VMEM, VMEM] + [HBM] * len(came),
+        out_specs=(VMEM,) * 2,
+        scratch_shapes=[
+            pltpu.VMEM((slots, 2 * narrow), BF16),
+            pltpu.SemaphoreType.DMA((len(came),)),
+        ],
+        compiler_params=PARAMS,
+        cost_estimate=pl.CostEstimate(
+            flops=4 * rows * narrow * width * turns,
+            bytes_accessed=8 * rows * narrow,
+            transcendentals=0,
+        ),
+        name="arrive_rows",
+    )(land, ids, *came)
+
+
+def near_kernel(rows_ref, ids_ref, out_ref):
+    for start, size in column_tiles(ids_ref.shape[1]):
+        out_ref[:, start : start + size] = onehot_dot(
+            rows_ref, ids_ref[:, start : start + size], rows_ref.shape[1]
+        ).astype(BF16)
+
+
+def near_columns(rows, ids):
+    count, narrow = rows.shape
+    extra = ids.shape[1]
+    return pl.pallas_call(
+        near_kernel,
+        out_shape=jax.ShapeDtypeStruct((count, extra), BF16),
+        in_specs=[VMEM] * 2,
+        out_specs=VMEM,
+        compiler_params=PARAMS,
+        cost_estimate=pl.CostEstimate(
+            flops=2 * count * narrow * extra,
+            bytes_accessed=2 * count * (narrow + extra),
+            transcendentals=0,
+        ),
+    )(rows, ids)
+
+
+def column_tiles(extent):
+    pieces = -(-extent // 1408)
+    size = extent // pieces // 256 * 256 or extent
+    starts = [size * piece for piece in range(pieces)]
+    return [
+        (start, (extent if start == starts[-1] else start + size) - start) for start in starts
+    ]
+
+
+def put_extras(half, narrow, near, far_ref, ids_ref, outs, held_ref, sems):
+    rows = held_ref.shape[0] // len(outs)
+    layers = outs[0].shape[0]
+    copies = []
+    for step, (start, size) in enumerate(column_tiles(held_ref.shape[1])):
+        total = None
+        for s in range(ids_ref.shape[0]):
+            far = onehot_dot(far_ref.at[s], ids_ref[s : s + 1, start : start + size], far_ref.shape[2])
+            total = far if total is None else total + far
+        held_ref[:, start : start + size] = (total + near(start, size)).astype(BF16)
+        for layer in range(layers):
+            for side, out in enumerate(outs):
+                copies.append(
+                    pltpu.make_async_copy(
+                        held_ref.at[pl.ds(side * rows, rows), pl.ds(start, size)],
+                        out.at[layer, half, :, pl.ds(narrow + start, size)],
+                        sems.at[step, layer, side],
+                    )
+                )
+                copies[-1].start()
+    return copies
+
+
+def first_kernel(
+    table_ref, near_ids_ref, far_ref, far_ids_ref, gate_ref, up_ref, gate_out, up_out,
+    in_ref, base_ref, held_ref, in_sems, base_sems, sems,
+):
+    layers, rows, narrow = gate_ref.shape
+    order = list(range(layers))[::-1]
+    loads = load_weights(order, gate_ref, up_ref, in_ref, in_sems)
+    scale = 1.0 / count_of(
+        table_ref[...], iota((rows, 1), 0) + lax.axis_index("section") * rows
+    )
+    outs = (gate_out, up_out)
+    copies = []
+    for number, load in enumerate(loads):
+        at, side = number // 2, number % 2
+        load.wait()
+        here = pl.ds(side * rows, rows)
+        base_ref[at, here] = (in_ref[at, side].astype(F32) * scale).astype(BF16)
+        copies.append(
+            pltpu.make_async_copy(
+                base_ref.at[at, here],
+                outs[side].at[order[at], 0, :, pl.ds(0, narrow)],
+                base_sems.at[at, side],
+            )
+        )
+        copies[-1].start()
+
+    def near(start, size):
+        return onehot_dot(base_ref.at[0], near_ids_ref[:, start : start + size], narrow)
+
+    copies += put_extras(0, narrow, near, far_ref, far_ids_ref, outs, held_ref, sems)
+    for copy in copies:
+        copy.wait()
+
+
+def first_half(table, near_ids, far, far_ids, gate, up, out_type):
+    layers, rows, narrow = gate.shape
+    extra = near_ids.shape[1]
+    return pl.pallas_call(
+        first_kernel,
+        out_shape=(out_type, out_type),
+        in_specs=[VMEM] * 4 + [HBM] * 2,
+        out_specs=(HBM, HBM),
+        scratch_shapes=[
+            pltpu.VMEM((layers, 2, rows, narrow), BF16),
+            pltpu.VMEM((layers, 2 * rows, narrow), BF16),
+            pltpu.VMEM((2 * rows, extra), BF16),
+            pltpu.SemaphoreType.DMA((layers, 2)),
+            pltpu.SemaphoreType.DMA((layers, 2)),
+            pltpu.SemaphoreType.DMA((len(column_tiles(extra)), layers, 2)),
+        ],
+        compiler_params=PARAMS,
+        cost_estimate=pl.CostEstimate(
+            flops=4 * rows * (narrow + far.shape[2] * far.shape[0]) * extra,
+            bytes_accessed=8 * layers * rows * (narrow + extra),
+            transcendentals=0,
+        ),
+        name="first_half",
+    )(table, near_ids, far, far_ids, gate, up)
+
+
+def second_kernel(
+    rows_ref, near_ref, far_ref, ids_ref, gate_in, up_in, gate_out, up_out,
+    held_ref, base_sems, sems,
+):
+    rows, narrow = rows_ref.shape[0] // 2, rows_ref.shape[1]
+    outs = (gate_out, up_out)
+    layers = gate_out.shape[0]
+    copies = []
+    for side, out in enumerate(outs):
+        copies.append(
+            pltpu.make_async_copy(
+                rows_ref.at[pl.ds(side * rows, rows), :],
+                out.at[layers - 1, 1, :, pl.ds(0, narrow)],
+                base_sems.at[side],
+            )
+        )
+        copies[-1].start()
+
+    def near(start, size):
+        return near_ref[:, start : start + size].astype(F32)
+
+    copies += put_extras(1, narrow, near, far_ref, ids_ref, outs, held_ref, sems)
+    for copy in copies:
+        copy.wait()
+
+
+def second_half(rows, near, far, ids, gate_out, up_out):
+    count, narrow = rows.shape
+    extra = near.shape[1]
+    layers = gate_out.shape[0]
+    out_type = jax.ShapeDtypeStruct(gate_out.shape, BF16)
+    return pl.pallas_call(
+        second_kernel,
+        out_shape=(out_type, out_type),
+        in_specs=[VMEM] * 4 + [HBM] * 2,
+        out_specs=(HBM, HBM),
+        input_output_aliases={4: 0, 5: 1},
+        scratch_shapes=[
+            pltpu.VMEM((count, extra), BF16),
+            pltpu.SemaphoreType.DMA((2,)),
+            pltpu.SemaphoreType.DMA((len(column_tiles(extra)), layers, 2)),
+        ],
+        compiler_params=PARAMS,
+        cost_estimate=pl.CostEstimate(
+            flops=2 * count * far.shape[2] * far.shape[0] * extra,
+            bytes_accessed=4 * count * (narrow + layers * extra),
+            transcendentals=0,
+        ),
+        name="second_half",
+    )(rows, near, far, ids, gate_out, up_out)
+
+
+def last_kernel(
+    land_ref, came_ref, gate_in, up_in, gate_out, up_out, in_ref, held_ref, in_sems, out_sems
+):
+    narrow = came_ref.shape[1] // 2
+    steps = in_sems.shape[1]
+    width = narrow // steps
+    loads, stores = [], []
+    for number in range(2 * steps):
+        columns = pl.ds(number * width, width)
+        loads.append(
+            pltpu.make_async_copy(
+                came_ref.at[:, columns],
+                in_ref.at[:, columns],
+                in_sems.at[number // steps, number % steps],
+            )
+        )
+        loads[-1].start()
+    for side, out in enumerate((gate_out, up_out)):
+        for step in range(steps):
+            at = side * narrow + step * width
+            loads[side * steps + step].wait()
+            held_ref[:, at : at + width] = jnp.dot(
+                land_ref[...], in_ref[:, at : at + width], preferred_element_type=F32
+            ).astype(BF16)
+            stores.append(
+                pltpu.make_async_copy(
+                    held_ref.at[:, pl.ds(at, width)],
+                    out.at[0, 1, :, pl.ds(step * width, width)],
+                    out_sems.at[side, step],
+                )
+            )
+            stores[-1].start()
+    for store in stores:
+        store.wait()
+
+
+def last_rows(land, came, gate_out, up_out):
+    rows, slots = land.shape
+    narrow = came.shape[1] // 2
+    steps = 2
+    out_type = jax.ShapeDtypeStruct(gate_out.shape, BF16)
+    return pl.pallas_call(
+        last_kernel,
+        out_shape=(out_type, out_type),
+        in_specs=[VMEM] + [HBM] * 3,
+        out_specs=(HBM, HBM),
+        input_output_aliases={2: 0, 3: 1},
+        scratch_shapes=[
+            pltpu.VMEM((slots, 2 * narrow), BF16),
+            pltpu.VMEM((rows, 2 * narrow), BF16),
+            pltpu.SemaphoreType.DMA((2, steps)),
+            pltpu.SemaphoreType.DMA((2, steps)),
+        ],
+        compiler_params=PARAMS,
+        cost_estimate=pl.CostEstimate(
+            flops=4 * rows * slots * narrow,
+            bytes_accessed=8 * rows * narrow,
+            transcendentals=0,
+        ),
+        name="last_rows",
+    )(land, came, gate_out, up_out)
+
+
+def column_plan(ffn_map, splits, narrow, width):
+    rank = lax.axis_index("mp")
+    extra = ffn_map.shape[0] // splits
+    table = ffn_map.reshape(splits, extra)
+    owner = table // narrow
+    within = table - owner * narrow
+
+    def line(array, at):
+        return lax.dynamic_index_in_dim(array, at, 0, keepdims=False)
+
+    my_owner, my_within = line(owner, rank), line(within, rank)
+    near = jnp.where(my_owner == rank, my_within, -1)[None, :]
+    turns = range(1, splits)
+    targets = [lax.rem(rank + turn, splits) for turn in turns]
+    origins = [lax.rem(rank + splits - turn, splits) for turn in turns]
+    hits = jnp.stack(
+        [line(owner, target) == rank for target in targets]
+        + [my_owner == origin for origin in origins]
+    )
+    order = jnp.where(hits, jnp.cumsum(hits.astype(I32), axis=1) - 1, -1)
+    slots = jnp.arange(width, dtype=I32)
+    sends = [
+        jnp.sum(
+            jnp.where(order[at][None, :] == slots[:, None], line(within, target)[None, :] + 1, 0),
+            axis=1,
+        )
+        - 1
+        for at, target in enumerate(targets)
+    ]
+    return near, jnp.stack(sends), order[splits - 1 :]
+
+
+def turn_around(sent, splits):
+    return jnp.stack(
+        [
+            lax.ppermute(sent[turn - 1], "mp", [(i, (i + turn) % splits) for i in range(splits)])
+            for turn in range(1, splits)
+        ]
+    )
+
+
+def tiled_local(gate_weight, up_weight, hidden_map, ffn_map):
+    layers, rows, narrow = gate_weight.shape
+    blocks = lax.axis_size("section")
+    splits = lax.axis_size("mp")
+    extra = ffn_map.shape[0] // splits
+    cap = rows // blocks
+    column_cap = extra // splits
+    width = -(-column_cap // 128) * 128
+    table = hidden_map.reshape(blocks, rows)
+    out_type = jax.ShapeDtypeStruct((layers, 2, rows, narrow + extra), BF16)
+
+    half = blocks // 2
+    groups = [list(range(half)), list(range(half, blocks))]
+
+    def swap_rows(sent, groups=None):
+        return lax.all_to_all(
+            sent, "section", split_axis=0, concat_axis=0, tiled=True, axis_index_groups=groups
+        )
+
+    def cross(sent, p):
+        return lax.ppermute(sent, "section", [(i, i ^ p) for i in range(blocks)])
+
+    sent_top = send_rows(table, gate_weight, up_weight, layers - 1, cap, True)
+    came_top = [cross(sent_top[1 + p], half + p) for p in range(half)]
+    came_top.insert(0, swap_rows(sent_top[0], groups))
+    sent_top = sent_top[0]
+    ffn_map, table = lax.optimization_barrier((ffn_map, sent_top, table))[::2]
+    near_ids, send_ids, far_ids = column_plan(ffn_map, splits, narrow, width)
+    own_sent = own_rows(table, send_ids, gate_weight, up_weight)
+    own_far = turn_around(own_sent, splits)
+    sent_low = send_rows(table, gate_weight, up_weight, 0, cap, False)[0]
+    came_low = swap_rows(sent_low)
+    land = land_rows(table, cap)
+    got, got_sent = arrive_rows(land, send_ids, came_top)
+    got_far = turn_around(got_sent, splits)
+    outs = first_half(table, near_ids, own_far, far_ids, gate_weight, up_weight, out_type)
+    got_near = near_columns(got, near_ids)
+    outs = second_half(got, got_near, got_far, far_ids, *outs)
+    return last_rows(land, came_low, *outs)
+
+
+def plain_local(gate_weight, up_weight, hidden_map, ffn_map):
+    layers, shard_rows, _ = gate_weight.shape
     blocks = lax.axis_size("section")
     splits = lax.axis_size("mp")
     section_rank = lax.axis_index("section")
@@ -86,6 +664,26 @@
     )
 
 
+def local(gate_weight, up_weight, hidden_map, ffn_map):
+    layers, rows, narrow = gate_weight.shape
+    blocks = lax.axis_size("section")
+    splits = lax.axis_size("mp")
+    extra = ffn_map.shape[0] // splits
+    whole_tiles = (
+        layers == 2
+        and splits > 1
+        and blocks > 1
+        and blocks & (blocks - 1) == 0
+        and rows % (8 * blocks) == 0
+        and rows % 16 == 0
+        and narrow % 256 == 0
+        and extra % 128 == 0
+        and extra % splits == 0
+    )
+    form = tiled_local if whole_tiles else plain_local
+    return form(gate_weight, up_weight, hidden_map, ffn_map)
+
+
 def solution(mesh):
     in_specs = (P(None, "section", "mp"), P(None, "section", "mp"), P(), P())
     out_specs = (P(None, None, "section", "mp"), P(None, None, "section", "mp"))

time: 316 us -> 118 us (0.37); the launches traced: 311 us -> 117 us
  local copies, waits for them, and re-layouts: 87.2 us -> 1.6 us
  blocking collectives: 69.1 us -> 0 us
  other arithmetic: 65.1 us -> 2.86 us
  Pallas kernels: 0 us -> 37.7 us
  waiting for transfers between devices: 69.6 us -> 43.3 us
  starting transfers between devices: 5.71 us -> 30.3 us
  between operations: 14.6 us -> 1.03 us
    gather x12 -> x0, local copies, waits for them, and re-layouts: 72.3 us -> none  [the longest x2 15.3 us: pick_columns(): jnp.take(portion, bounded, axis=2)]
    all_to_all x1 -> x0, blocking collectives: 69.1 us -> none  [local(): lax.all_to_all(jnp.take(own_up, sent_rows, axis=1), 'section', split_axis...]
    all_gather x2 -> x0, waiting for transfers between devices: 42 us -> none  [the longest x1 22 us: local(): lax.all_gather(later[0], 'mp', axis=2, tiled=True)]
    ppermute x0 -> x10, waiting for transfers between devices: none -> 39.8 us  [the longest x8 38.5 us: cross(): return lax.ppermute(sent, 'section', [(i, i ^ p) for i in range(blocks)])]
    pallas_call x0 -> x9, Pallas kernels: none -> 37.7 us  [the longest x1 10.4 us: first_half(): pl.pallas_call(first_kernel, out_shape=(out_type, out_type), in_specs=[VM...]
    all_to_all x1 -> x2, waiting for transfers between devices: 27.6 us -> 3.45 us  [swap_rows(): lax.all_to_all(sent, 'section', split_axis=0, concat_axis=0, tiled=True,...]
    ppermute x0 -> x10, starting transfers between devices: none -> 19 us  [the longest x8 16.4 us: cross(): return lax.ppermute(sent, 'section', [(i, i ^ p) for i in range(blocks)])]
    another operation x5 -> x2, other arithmetic: 16.9 us -> 0.79 us  [the longest x2 12.5 us: local(): jnp.stack([own_up, jnp.take(arrived[1], landing, axis=1)], axis=1)]
  transfers between devices with their start and end apart: 3 -> 12, of which waited for: 3 -> 9; matrix products, arithmetic and copies ran while one was open for 15% -> 4% of each run, Pallas kernels for 0% -> 27%
where the time goes in v1:
time: 118 us; the launch traced here: 117 us
  waiting for transfers between devices  43.3 us (37%)
  Pallas kernels  37.7 us (32%)
  starting transfers between devices  30.3 us (26%)
  other arithmetic  2.86 us (2%)
  local copies, waits for them, and re-layouts  1.6 us (1%)
    ppermute x8, waiting for transfers between devices, cross(): return lax.ppermute(sent, 'section', [(i, i ^ p) for i in range(blocks)])  38.5 us
    ppermute x8, starting transfers between devices, cross(): return lax.ppermute(sent, 'section', [(i, i ^ p) for i in range(blocks)])  16.4 us
    all_to_all x2, starting transfers between devices, swap_rows(): lax.all_to_all(sent, 'section', split_axis=0, concat_axis=0, tiled=True,...  11.3 us
    pallas_call x1, Pallas kernels, first_half(): pl.pallas_call(first_kernel, out_shape=(out_type, out_type), in_specs=[VM...  10.4 us
    pallas_call x2, Pallas kernels, send_rows(): pl.pallas_call(functools.partial(send_kernel, layer, cap, halves), out_sh...  7.01 us
    pallas_call x1, Pallas kernels, own_rows(): pl.pallas_call(own_kernel, out_shape=jax.ShapeDtypeStruct((turns, 2 * row...  5.41 us
    pallas_call x1, Pallas kernels, near_columns(): pl.pallas_call(near_kernel, out_shape=jax.ShapeDtypeStruct((count, extra)...  4.56 us
    pallas_call x1, Pallas kernels, arrive_rows(): pl.pallas_call(arrive_kernel, out_shape=(jax.ShapeDtypeStruct((2 * rows,...  4.12 us
  transfers between devices with their start and end apart: 12, of which 9 were waited for; matrix products, arithmetic and copies ran while one was open for 4% of the time, Pallas kernels for 27%

profile of v1, /device:TPU:13, one launch (start us, length us, event | category | flops | bytes accessed | tf_op | source)
XLA Modules:
  0.0 116.7 jit_solution(8712991266294853237)
XLA Ops:
  0.6 3.7 %shard_map.59 = (bf16[64,5632]{1,0:T(8,128)(2,1)}, bf16[8,5632]{1,0:T(8,128)(2,1)}, bf16[8,5632]{1,0:T(8,128)(2,1)}, bf16[8,5632]{1,0:T(8,128)(2,1)}, bf16[8,563...) custom-call(s32[16,128]{1,0:T(8,128)} %bitcast.19, ...), custom_call_target="tpu_custom_call" | custom-call | flops 184549376 | bytes 2883584 | tf_op jit(solution)/shard_map/pallas_call | solution.py:136
  4.3 4.5 %all-to-all-start.1 = ((bf16[8,8,5632]{2,1,0:T(8,128)(2,1)}), bf16[8,8,5632]{2,1,0:T(8,128)(2,1)S(1)}, u32[]{:S(2)}, u32[]{:S(2)}) async-start(bf16[8,8,5632]{2,1,0:T(8,128)(2,1)} %bitcast.27), calls=%async_computation.1 | async-start | bytes 1441792 | tf_op jit(solution)/shard_map/all_to_all | solution.py:559
  8.8 0.8 reshape.36
  9.6 0.1 multiply_subtract_fusion
  9.7 0.1 fusion
  9.8 0.6 reduce-window.6
  10.4 0.2 slice_reduce_fusion
  10.6 0.2 reduce-window.9
  10.8 3.3 %shard_map.60 = bf16[128,5632]{1,0:T(8,128)(2,1)} custom-call(s32[16,128]{1,0:T(8,128)} %bitcast.20, bf16[2,128,2816]{2,1,0:T(8,128)(2,1)} %gate_ref.7, bf16[2,128,2816]{2,1,0:T(8,128)(2,1)} %up_ref.7), custom_call_target="tpu_custom_call" | custom-call | flops 184549376 | bytes 2883584 | tf_op jit(solution)/shard_map/pallas_call | solution.py:136
  14.1 0.0 copy-start.11
  14.1 0.0 copy-start.10
  14.1 0.0 copy-start.9
  14.1 0.0 copy-start.8
  14.1 0.0 copy-start.7
  14.1 0.0 copy-start.6
  14.1 0.0 copy-start.5
  14.2 0.0 copy-start.4
  14.2 0.0 copy-start.2
  14.2 0.1 add_bitcast_fusion
  14.3 3.4 %all-to-all-done.1 = bf16[8,8,5632]{2,1,0:T(8,128)(2,1)S(1)} async-done(((bf16[8,8,5632]{2,1,0:T(8,128)(2,1)}), bf16[8,8,5632]{2,1,0:T(8,128)(2,1)S(1)}, u32[]{:S(2)}, u32[]{:S(2)}) %all-to-all-start.1) | async-done | bytes 720928 | tf_op jit(solution)/shard_map/all_to_all | solution.py:559
  17.7 6.8 %all-to-all-start = ((bf16[16,8,5632]{2,1,0:T(8,128)(2,1)}), bf16[16,8,5632]{2,1,0:T(8,128)(2,1)S(1)}, u32[]{:S(2)}, u32[]{:S(2)}) async-start(bf16[16,8,5632]{2,1,0:T(8,128)(2,1)} %bitcast.26), calls=%async_computation | async-start | bytes 2883584 | tf_op jit(solution)/shard_map/all_to_all | solution.py:559
  24.6 0.1 compare_select_fusion
  24.7 1.7 %select_reduce_fusion = s32[1408]{0:T(1024)S(1)} fusion(s32[2688]{0:T(1024)S(1)} %get-tuple-element.45, s32[2688]{0:T(1024)S(1)} %get-tuple-element.48), kind=kLoop, calls=%fused_computation | loop fusion | flops 11352704 | bytes 27136 | tf_op jit(solution)/shard_map/reduce_sum | solution.py:525
  26.4 0.6 sub.27.ids_ref
  27.0 5.4 %own_rows.1 = bf16[1,256,1408]{2,1,0:T(8,128)(2,1)} custom-call(s32[16,128]{1,0:T(8,128)} %bitcast.21, s32[1,1408]{1,0:T(1,128)} %sub.27.ids_ref, bf16[2,128,2816]{2,1,0:T(8,128)(2,1)} %gate_ref.7, bf16[2,128,2816]{2,1,0:T(8,128)(2,1)} %up_ref.7), custom_call_target="tpu_custom_call" | custom-call | flops 2030043136 | bytes 2883584 | tf_op jit(solution)/shard_map/own_rows/pallas_call | solution.py:185
  32.4 0.0 copy-start
  32.4 0.0 copy-start.1
  32.4 1.3 %collective-permute-start.9 = (bf16[256,1408]{1,0:T(8,128)(2,1)}, bf16[256,1408]{1,0:T(8,128)(2,1)S(1)}, u32[]{:S(2)}, u32[]{:S(2)}) collective-permute-start(bf16[256,1408]{1,0:T(8,128)(2,1)} %bitcast.31), channel_id=1, source_target_pairs={{0,1},{1,0},{2,3},{3,2},{4,5},{5,4},{6,7},{7,6},{8,9},{9,8},{10,11... | collective-permute-start | bytes 2162696 | tf_op jit(solution)/shard_map/ppermute | solution.py:538
  33.7 0.0 copy-done.11
  33.7 2.1 %collective-permute-start = (bf16[8,5632]{1,0:T(8,128)(2,1)S(1)}, bf16[8,5632]{1,0:T(8,128)(2,1)S(1)}, u32[]{:S(2)}, u32[]{:S(2)}) collective-permute-start(bf16[8,5632]{1,0:T(8,128)(2,1)S(1)} %copy-done.11), channel_id=1, source_target_pairs={{0,16},{2,18},{4,20},{6,22},{8,24},{10,26},{12,28},{14,30},{16,0},... | collective-permute-start | bytes 270344 | tf_op jit(solution)/shard_map/ppermute | solution.py:564
  35.8 0.0 copy-done.10
  35.8 1.1 collective-permute-start.1
  36.9 0.0 copy-done.9
  36.9 2.1 %collective-permute-start.2 = (bf16[8,5632]{1,0:T(8,128)(2,1)S(1)}, bf16[8,5632]{1,0:T(8,128)(2,1)S(1)}, u32[]{:S(2)}, u32[]{:S(2)}) collective-permute-start(bf16[8,5632]{1,0:T(8,128)(2,1)S(1)} %copy-done.9), channel_id=1, source_target_pairs={{0,20},{2,22},{4,16},{6,18},{8,28},{10,30},{12,24},{14,26},{16,4},... | collective-permute-start | bytes 270344 | tf_op jit(solution)/shard_map/ppermute | solution.py:564
  39.0 0.0 copy-done.8
  39.0 1.2 %collective-permute-start.3 = (bf16[8,5632]{1,0:T(8,128)(2,1)S(1)}, bf16[8,5632]{1,0:T(8,128)(2,1)S(1)}, u32[]{:S(2)}, u32[]{:S(2)}) collective-permute-start(bf16[8,5632]{1,0:T(8,128)(2,1)S(1)} %copy-done.8), channel_id=1, source_target_pairs={{0,22},{2,20},{4,18},{6,16},{8,30},{10,28},{12,26},{14,24},{16,6},... | collective-permute-start | bytes 270344 | tf_op jit(solution)/shard_map/ppermute | solution.py:564
  40.2 25.1 %collective-permute-done.refs_1_ = bf16[8,5632]{1,0:T(8,128)(2,1)S(1)} collective-permute-done((bf16[8,5632]{1,0:T(8,128)(2,1)S(1)}, bf16[8,5632]{1,0:T(8,128)(2,1)S(1)}, u32[]{:S(2)}, u32[]{:S(2)}) %collective-permute-start) | collective-permute-done | bytes 90144 | tf_op jit(solution)/shard_map/ppermute | solution.py:564
  65.3 0.0 copy-done.7
  65.3 1.3 %collective-permute-start.4 = (bf16[8,5632]{1,0:T(8,128)(2,1)S(1)}, bf16[8,5632]{1,0:T(8,128)(2,1)S(1)}, u32[]{:S(2)}, u32[]{:S(2)}) collective-permute-start(bf16[8,5632]{1,0:T(8,128)(2,1)S(1)} %copy-done.7), channel_id=1, source_target_pairs={{0,24},{2,26},{4,28},{6,30},{8,16},{10,18},{12,20},{14,22},{16,8},... | collective-permute-start | bytes 270344 | tf_op jit(solution)/shard_map/ppermute | solution.py:564
  66.6 0.6 collective-permute-done.1.refs_2_
  67.2 0.0 copy-done.6
  67.2 2.7 %collective-permute-start.5 = (bf16[8,5632]{1,0:T(8,128)(2,1)S(1)}, bf16[8,5632]{1,0:T(8,128)(2,1)S(1)}, u32[]{:S(2)}, u32[]{:S(2)}) collective-permute-start(bf16[8,5632]{1,0:T(8,128)(2,1)S(1)} %copy-done.6), channel_id=1, source_target_pairs={{0,26},{2,24},{4,30},{6,28},{8,18},{10,16},{12,22},{14,20},{16,10}... | collective-permute-start | bytes 270344 | tf_op jit(solution)/shard_map/ppermute | solution.py:564
  69.9 0.0 collective-permute-done.2.refs_3_
  69.9 0.0 copy-done.5
  69.9 0.5 collective-permute-start.6
  70.4 1.6 %collective-permute-done.3.refs_4_ = bf16[8,5632]{1,0:T(8,128)(2,1)S(1)} collective-permute-done((bf16[8,5632]{1,0:T(8,128)(2,1)S(1)}, bf16[8,5632]{1,0:T(8,128)(2,1)S(1)}, u32[]{:S(2)}, u32[]{:S(2)}) %collective-permute-start.3) | collective-permute-done | bytes 90144 | tf_op jit(solution)/shard_map/ppermute | solution.py:564
  72.0 0.0 copy-done.4
  72.0 5.5 %collective-permute-start.7 = (bf16[8,5632]{1,0:T(8,128)(2,1)S(1)}, bf16[8,5632]{1,0:T(8,128)(2,1)S(1)}, u32[]{:S(2)}, u32[]{:S(2)}) collective-permute-start(bf16[8,5632]{1,0:T(8,128)(2,1)S(1)} %copy-done.4), channel_id=1, source_target_pairs={{0,30},{2,28},{4,26},{6,24},{8,22},{10,20},{12,18},{14,16},{16,14}... | collective-permute-start | bytes 270344 | tf_op jit(solution)/shard_map/ppermute | solution.py:564
  77.5 0.0 copy-done.2
  77.5 0.2 land_rows.1.land_ref
  77.7 3.1 %collective-permute-done.4.refs_5_ = bf16[8,5632]{1,0:T(8,128)(2,1)S(1)} collective-permute-done((bf16[8,5632]{1,0:T(8,128)(2,1)S(1)}, bf16[8,5632]{1,0:T(8,128)(2,1)S(1)}, u32[]{:S(2)}, u32[]{:S(2)}) %collective-permute-start.4) | collective-permute-done | bytes 90144 | tf_op jit(solution)/shard_map/ppermute | solution.py:564
  80.8 5.0 %collective-permute-done.5.refs_6_ = bf16[8,5632]{1,0:T(8,128)(2,1)S(1)} collective-permute-done((bf16[8,5632]{1,0:T(8,128)(2,1)S(1)}, bf16[8,5632]{1,0:T(8,128)(2,1)S(1)}, u32[]{:S(2)}, u32[]{:S(2)}) %collective-permute-start.5) | collective-permute-done | bytes 90144 | tf_op jit(solution)/shard_map/ppermute | solution.py:564
  85.8 0.7 collective-permute-done.6.refs_7_
  86.6 2.2 %collective-permute-done.7.refs_8_ = bf16[8,5632]{1,0:T(8,128)(2,1)S(1)} collective-permute-done((bf16[8,5632]{1,0:T(8,128)(2,1)S(1)}, bf16[8,5632]{1,0:T(8,128)(2,1)S(1)}, u32[]{:S(2)}, u32[]{:S(2)}) %collective-permute-start.7) | collective-permute-done | bytes 90144 | tf_op jit(solution)/shard_map/ppermute | solution.py:564
  88.8 4.1 %arrive_rows.1 = (bf16[256,2816]{1,0:T(8,128)(2,1)S(1)}, bf16[1,256,1408]{2,1,0:T(8,128)(2,1)S(1)}) custom-call(bf16[128,128]{1,0:T(8,128)(2,1)S(1)} %land_rows.1.land_ref, s32[1,1408]{1,0:T(1,128)S(1)} %copy-done.3, bf16[64,5632]{1,0:T(8,128)(2,1)S(1)} %bitcast.18, bf16[8,5632]{1,0:T(8,128)(2,1)S(1)} %collective-permute-done.refs_1_, ...), custom_call_target="tpu_custom_call" | custom-call | flops 2030043136 | bytes 2883584 | tf_op jit(solution)/shard_map/arrive_rows/pallas_call | solution.py:250
  92.9 1.3 %collective-permute-start.8 = (bf16[256,1408]{1,0:T(8,128)(2,1)S(1)}, bf16[256,1408]{1,0:T(8,128)(2,1)S(1)}, u32[]{:S(2)}, u32[]{:S(2)}) collective-permute-start(bf16[256,1408]{1,0:T(8,128)(2,1)S(1)} %bitcast.25), channel_id=1, source_target_pairs={{0,1},{1,0},{2,3},{3,2},{4,5},{5,4},{6,7},{7,6},{8,9},{9,8},{10,11... | collective-permute-start | bytes 2162696 | tf_op jit(solution)/shard_map/ppermute | solution.py:538
  94.2 0.0 collective-permute-done.9
  94.2 0.0 copy-done
  94.2 10.4 %first_half.1 = (bf16[2,2,128,5504]{3,2,1,0:T(8,128)(2,1)}, bf16[2,2,128,5504]{3,2,1,0:T(8,128)(2,1)}) custom-call(s32[16,128]{1,0:T(8,128)S(1)} %bitcast.23, s32[1,2688]{1,0:T(1,128)S(1)} %get-tuple-element.44.ids_ref.near_ids_ref, bf16[1,256,1408]{2,1,0:T(8,128)(2,1)S(1)} %bitcast.24, s32[1,2688]{1,0:T(1,128)S(1)} %get-tuple-element.49.far_ids_ref.ids_ref, ...), custom_call_target="tpu_custom_call" | custom-call | flops 5813305344 | bytes 11272192 | tf_op jit(solution)/shard_map/first_half/pallas_call | solution.py:365
  104.6 4.6 %shard_map.61.near_ref = bf16[256,2688]{1,0:T(8,128)(2,1)S(1)} custom-call(bf16[256,2816]{1,0:T(8,128)(2,1)S(1)} %get-tuple-element.30.rows_ref, s32[1,2688]{1,0:T(1,128)S(1)} %get-tuple-element.44.ids_ref.near_ids_ref), custom_call_target="tpu_custom_call" | custom-call | flops 3875536896 | bytes 2818048 | tf_op jit(solution)/shard_map/pallas_call | solution.py:282
  109.2 1.4 %collective-permute-done.8 = bf16[256,1408]{1,0:T(8,128)(2,1)S(1)} collective-permute-done((bf16[256,1408]{1,0:T(8,128)(2,1)S(1)}, bf16[256,1408]{1,0:T(8,128)(2,1)S(1)}, u32[]{:S(2)}, u32[]{:S(2)}) %collective-permute-start.8) | collective-permute-done | bytes 720928 | tf_op jit(solution)/shard_map/ppermute | solution.py:538
  110.6 4.0 %second_half.1 = (bf16[2,2,128,5504]{3,2,1,0:T(8,128)(2,1)}, bf16[2,2,128,5504]{3,2,1,0:T(8,128)(2,1)}) custom-call(bf16[256,2816]{1,0:T(8,128)(2,1)S(1)} %get-tuple-element.30.rows_ref, bf16[256,2688]{1,0:T(8,128)(2,1)S(1)} %shard_map.61.near_ref, bf16[1,256,1408]{2,1,0:T(8,128)(2,1)S(1)} %bitcast.17, ...), custom_call_target="tpu_custom_call", output_to_operand_aliasing={{0}: (4, {}), {1}: (5, {})} | custom-call | flops 1937768448 | bytes 8388608 | tf_op jit(solution)/shard_map/second_half/pallas_call | solution.py:419
  114.6 0.0 all-to-all-done
  114.6 1.9 %last_rows.1 = (bf16[2,2,128,5504]{3,2,1,0:T(8,128)(2,1)}, bf16[2,2,128,5504]{3,2,1,0:T(8,128)(2,1)}) custom-call(bf16[128,128]{1,0:T(8,128)(2,1)S(1)} %land_rows.1.land_ref, bf16[128,5632]{1,0:T(8,128)(2,1)S(1)} %bitcast.16, bf16[2,2,128,5504]{3,2,1,0:T(8,128)(2,1)} %get-tuple-element.34.gate_in, ...), custom_call_target="tpu_custom_call", output_to_operand_aliasing={{0}: (2, {}), {1}: (3, {})} | custom-call | flops 184549376 | bytes 2883584 | tf_op jit(solution)/shard_map/last_rows/pallas_call | solution.py:481
  (6 shorter events, 0.1 us)
Async XLA Ops:
  4.3 13.4 %all-to-all-start.1 = ((bf16[8,8,5632]{2,1,0:T(8,128)(2,1)}), bf16[8,8,5632]{2,1,0:T(8,128)(2,1)S(1)}, u32[]{:S(2)}, u32[]{:S(2)}) async-start(bf16[8,8,5632]{2,1,0:T(8,128)(2,1)} %bitcast.27), calls=%async_computation.1 | async-start | bytes 1441792 | tf_op jit(solution)/shard_map/all_to_all | solution.py:559
  14.1 19.6 %copy-start.11 = (bf16[8,5632]{1,0:T(8,128)(2,1)S(1)}, bf16[8,5632]{1,0:T(8,128)(2,1)}, u32[]{:S(2)}) copy-start(bf16[8,5632]{1,0:T(8,128)(2,1)} %get-tuple-element.22) | copy-start | bytes 270340
  14.1 21.7 %copy-start.10 = (bf16[8,5632]{1,0:T(8,128)(2,1)S(1)}, bf16[8,5632]{1,0:T(8,128)(2,1)}, u32[]{:S(2)}) copy-start(bf16[8,5632]{1,0:T(8,128)(2,1)} %get-tuple-element.23) | copy-start | bytes 270340
  14.1 22.8 %copy-start.9 = (bf16[8,5632]{1,0:T(8,128)(2,1)S(1)}, bf16[8,5632]{1,0:T(8,128)(2,1)}, u32[]{:S(2)}) copy-start(bf16[8,5632]{1,0:T(8,128)(2,1)} %get-tuple-element.24) | copy-start | bytes 270340
  14.1 24.9 %copy-start.8 = (bf16[8,5632]{1,0:T(8,128)(2,1)S(1)}, bf16[8,5632]{1,0:T(8,128)(2,1)}, u32[]{:S(2)}) copy-start(bf16[8,5632]{1,0:T(8,128)(2,1)} %get-tuple-element.25) | copy-start | bytes 270340
  14.1 51.2 %copy-start.7 = (bf16[8,5632]{1,0:T(8,128)(2,1)S(1)}, bf16[8,5632]{1,0:T(8,128)(2,1)}, u32[]{:S(2)}) copy-start(bf16[8,5632]{1,0:T(8,128)(2,1)} %get-tuple-element.26) | copy-start | bytes 270340
  14.1 53.1 %copy-start.6 = (bf16[8,5632]{1,0:T(8,128)(2,1)S(1)}, bf16[8,5632]{1,0:T(8,128)(2,1)}, u32[]{:S(2)}) copy-start(bf16[8,5632]{1,0:T(8,128)(2,1)} %get-tuple-element.27) | copy-start | bytes 270340
  14.1 55.8 %copy-start.5 = (bf16[8,5632]{1,0:T(8,128)(2,1)S(1)}, bf16[8,5632]{1,0:T(8,128)(2,1)}, u32[]{:S(2)}) copy-start(bf16[8,5632]{1,0:T(8,128)(2,1)} %get-tuple-element.28) | copy-start | bytes 270340
  14.2 57.9 %copy-start.4 = (bf16[8,5632]{1,0:T(8,128)(2,1)S(1)}, bf16[8,5632]{1,0:T(8,128)(2,1)}, u32[]{:S(2)}) copy-start(bf16[8,5632]{1,0:T(8,128)(2,1)} %get-tuple-element.29) | copy-start | bytes 270340
  14.2 63.3 %copy-start.2 = (s32[2048]{0:T(1024)S(1)}, s32[2048]{0:T(1024)}, u32[]{:S(2)}) copy-start(s32[2048]{0:T(1024)} %param.6) | copy-start | bytes 24580
  17.7 96.9 %all-to-all-start = ((bf16[16,8,5632]{2,1,0:T(8,128)(2,1)}), bf16[16,8,5632]{2,1,0:T(8,128)(2,1)S(1)}, u32[]{:S(2)}, u32[]{:S(2)}) async-start(bf16[16,8,5632]{2,1,0:T(8,128)(2,1)} %bitcast.26), calls=%async_computation | async-start | bytes 2883584 | tf_op jit(solution)/shard_map/all_to_all | solution.py:559
  27.0 61.8 %copy-start.3 = (s32[1,1408]{1,0:T(1,128)S(1)}, s32[1,1408]{1,0:T(1,128)}, u32[]{:S(2)}) copy-start(s32[1,1408]{1,0:T(1,128)} %sub.27.ids_ref) | copy-start | bytes 16900
  32.4 61.8 %copy-start = (bf16[2,128,2816]{2,1,0:T(8,128)(2,1)S(1)}, bf16[2,128,2816]{2,1,0:T(8,128)(2,1)}, u32[]{:S(2)}) copy-start(bf16[2,128,2816]{2,1,0:T(8,128)(2,1)} %gate_ref.7) | copy-start | bytes 4325380
  32.4 61.8 %copy-start.1 = (bf16[2,128,2816]{2,1,0:T(8,128)(2,1)S(1)}, bf16[2,128,2816]{2,1,0:T(8,128)(2,1)}, u32[]{:S(2)}) copy-start(bf16[2,128,2816]{2,1,0:T(8,128)(2,1)} %up_ref.7) | copy-start | bytes 4325380
  32.4 61.8 %collective-permute-start.9 = (bf16[256,1408]{1,0:T(8,128)(2,1)}, bf16[256,1408]{1,0:T(8,128)(2,1)S(1)}, u32[]{:S(2)}, u32[]{:S(2)}) collective-permute-start(bf16[256,1408]{1,0:T(8,128)(2,1)} %bitcast.31), channel_id=1, source_target_pairs={{0,1},{1,0},{2,3},{3,2},{4,5},{5,4},{6,7},{7,6},{8,9},{9,8},{10,11... | collective-permute-start | bytes 2162696 | tf_op jit(solution)/shard_map/ppermute | solution.py:538
  33.7 31.6 %collective-permute-start = (bf16[8,5632]{1,0:T(8,128)(2,1)S(1)}, bf16[8,5632]{1,0:T(8,128)(2,1)S(1)}, u32[]{:S(2)}, u32[]{:S(2)}) collective-permute-start(bf16[8,5632]{1,0:T(8,128)(2,1)S(1)} %copy-done.11), channel_id=1, source_target_pairs={{0,16},{2,18},{4,20},{6,22},{8,24},{10,26},{12,28},{14,30},{16,0},... | collective-permute-start | bytes 270344 | tf_op jit(solution)/shard_map/ppermute | solution.py:564
  35.8 31.5 %collective-permute-start.1 = (bf16[8,5632]{1,0:T(8,128)(2,1)S(1)}, bf16[8,5632]{1,0:T(8,128)(2,1)S(1)}, u32[]{:S(2)}, u32[]{:S(2)}) collective-permute-start(bf16[8,5632]{1,0:T(8,128)(2,1)S(1)} %copy-done.10), channel_id=1, source_target_pairs={{0,18},{2,16},{4,22},{6,20},{8,26},{10,24},{12,30},{14,28},{16,2},... | collective-permute-start | bytes 270344 | tf_op jit(solution)/shard_map/ppermute | solution.py:564
  36.9 33.1 %collective-permute-start.2 = (bf16[8,5632]{1,0:T(8,128)(2,1)S(1)}, bf16[8,5632]{1,0:T(8,128)(2,1)S(1)}, u32[]{:S(2)}, u32[]{:S(2)}) collective-permute-start(bf16[8,5632]{1,0:T(8,128)(2,1)S(1)} %copy-done.9), channel_id=1, source_target_pairs={{0,20},{2,22},{4,16},{6,18},{8,28},{10,30},{12,24},{14,26},{16,4},... | collective-permute-start | bytes 270344 | tf_op jit(solution)/shard_map/ppermute | solution.py:564
  39.0 33.1 %collective-permute-start.3 = (bf16[8,5632]{1,0:T(8,128)(2,1)S(1)}, bf16[8,5632]{1,0:T(8,128)(2,1)S(1)}, u32[]{:S(2)}, u32[]{:S(2)}) collective-permute-start(bf16[8,5632]{1,0:T(8,128)(2,1)S(1)} %copy-done.8), channel_id=1, source_target_pairs={{0,22},{2,20},{4,18},{6,16},{8,30},{10,28},{12,26},{14,24},{16,6},... | collective-permute-start | bytes 270344 | tf_op jit(solution)/shard_map/ppermute | solution.py:564
  65.3 15.5 %collective-permute-start.4 = (bf16[8,5632]{1,0:T(8,128)(2,1)S(1)}, bf16[8,5632]{1,0:T(8,128)(2,1)S(1)}, u32[]{:S(2)}, u32[]{:S(2)}) collective-permute-start(bf16[8,5632]{1,0:T(8,128)(2,1)S(1)} %copy-done.7), channel_id=1, source_target_pairs={{0,24},{2,26},{4,28},{6,30},{8,16},{10,18},{12,20},{14,22},{16,8},... | collective-permute-start | bytes 270344 | tf_op jit(solution)/shard_map/ppermute | solution.py:564
  67.2 18.6 %collective-permute-start.5 = (bf16[8,5632]{1,0:T(8,128)(2,1)S(1)}, bf16[8,5632]{1,0:T(8,128)(2,1)S(1)}, u32[]{:S(2)}, u32[]{:S(2)}) collective-permute-start(bf16[8,5632]{1,0:T(8,128)(2,1)S(1)} %copy-done.6), channel_id=1, source_target_pairs={{0,26},{2,24},{4,30},{6,28},{8,18},{10,16},{12,22},{14,20},{16,10}... | collective-permute-start | bytes 270344 | tf_op jit(solution)/shard_map/ppermute | solution.py:564
  69.9 16.6 %collective-permute-start.6 = (bf16[8,5632]{1,0:T(8,128)(2,1)S(1)}, bf16[8,5632]{1,0:T(8,128)(2,1)S(1)}, u32[]{:S(2)}, u32[]{:S(2)}) collective-permute-start(bf16[8,5632]{1,0:T(8,128)(2,1)S(1)} %copy-done.5), channel_id=1, source_target_pairs={{0,28},{2,30},{4,24},{6,26},{8,20},{10,22},{12,16},{14,18},{16,12}... | collective-permute-start | bytes 270344 | tf_op jit(solution)/shard_map/ppermute | solution.py:564
  72.0 16.8 %collective-permute-start.7 = (bf16[8,5632]{1,0:T(8,128)(2,1)S(1)}, bf16[8,5632]{1,0:T(8,128)(2,1)S(1)}, u32[]{:S(2)}, u32[]{:S(2)}) collective-permute-start(bf16[8,5632]{1,0:T(8,128)(2,1)S(1)} %copy-done.4), channel_id=1, source_target_pairs={{0,30},{2,28},{4,26},{6,24},{8,22},{10,20},{12,18},{14,16},{16,14}... | collective-permute-start | bytes 270344 | tf_op jit(solution)/shard_map/ppermute | solution.py:564
  92.9 17.6 %collective-permute-start.8 = (bf16[256,1408]{1,0:T(8,128)(2,1)S(1)}, bf16[256,1408]{1,0:T(8,128)(2,1)S(1)}, u32[]{:S(2)}, u32[]{:S(2)}) collective-permute-start(bf16[256,1408]{1,0:T(8,128)(2,1)S(1)} %bitcast.25), channel_id=1, source_target_pairs={{0,1},{1,0},{2,3},{3,2},{4,5},{5,4},{6,7},{7,6},{8,9},{9,8},{10,11... | collective-permute-start | bytes 2162696 | tf_op jit(solution)/shard_map/ppermute | solution.py:538

commit v2 on v1

--- a/solution.py
+++ b/solution.py
@@ -73,132 +73,192 @@
     return total
 
 
-def send_kernel(layer, cap, halves, table_ref, gate_ref, up_ref, *refs):
-    *sent_refs, map_ref, in_ref, held_ref, key_ref, within_ref, map_sem, in_sems, out_sems = refs
-    blocks = table_ref.shape[0]
-    map_load = pltpu.make_async_copy(table_ref, map_ref, map_sem)
-    map_load.start()
+def load_weights(layers, gate_ref, up_ref, in_ref, sems):
     narrow = gate_ref.shape[2]
-    steps = in_sems.shape[1]
-    width = narrow // steps
-    me = lax.axis_index("section")
     loads = []
-    for side, ref in enumerate((gate_ref, up_ref)):
-        for step in range(steps):
-            at = side * narrow + step * width
+    for at, layer in enumerate(layers):
+        for side, ref in enumerate((gate_ref, up_ref)):
             loads.append(
                 pltpu.make_async_copy(
-                    ref.at[layer, :, pl.ds(step * width, width)],
-                    in_ref.at[:, pl.ds(at, width)],
-                    in_sems.at[side, step],
+                    ref.at[layer],
+                    in_ref.at[at, :, pl.ds(side * narrow, narrow)],
+                    sems.at[at, side],
                 )
             )
             loads[-1].start()
-    if halves:
-        half = blocks // 2
-        base = lax.div(me, half) * half
-        targets = [base + p for p in range(half)] + [me ^ p for p in range(half, blocks)]
-    else:
-        targets = list(range(blocks))
-    map_load.wait()
-    pick, count = pick_matrix(map_ref[...], me, cap, key_ref, within_ref, targets)
-    scale = 1.0 / count
+    return loads
+
+
+def put_slots(loads, pick, scale, in_ref, held_ref, sent_refs, sems):
+    width = held_ref.shape[1] // len(loads)
     stores = []
-    for number, load in enumerate(loads):
-        at = number * width
+    for side, load in enumerate(loads):
+        columns = pl.ds(side * width, width)
         load.wait()
-        rows = jnp.dot(pick, in_ref[:, at : at + width], preferred_element_type=F32)
-        held_ref[:, at : at + width] = (rows * scale).astype(BF16)
+        rows = jnp.dot(pick, in_ref[:, columns], preferred_element_type=F32)
+        held_ref[:, columns] = (rows * scale).astype(BF16)
         first = 0
         for piece, ref in enumerate(sent_refs):
-            count_here = ref.shape[0]
+            count = ref.shape[0]
             stores.append(
                 pltpu.make_async_copy(
-                    held_ref.at[pl.ds(first, count_here), pl.ds(at, width)],
-                    ref.at[:, pl.ds(at, width)],
-                    out_sems.at[number, piece],
+                    held_ref.at[pl.ds(first, count), columns],
+                    ref.at[:, columns],
+                    sems.at[side, piece],
                 )
             )
             stores[-1].start()
-            first += count_here
+            first += count
+    return stores
+
+
+def send_kernel(layer, cap, table_ref, gate_ref, up_ref, *refs):
+    *sent_refs, map_ref, in_ref, held_ref, key_ref, within_ref, map_sem, in_sems, out_sems = refs
+    map_load = pltpu.make_async_copy(table_ref, map_ref, map_sem)
+    map_load.start()
+    loads = load_weights([layer], gate_ref, up_ref, in_ref, in_sems)
+    me = lax.axis_index("section")
+    targets = [me ^ p for p in range(map_ref.shape[0])]
+    map_load.wait()
+    pick, count = pick_matrix(map_ref[...], me, cap, key_ref, within_ref, targets)
+    stores = put_slots(loads, pick, 1.0 / count, in_ref.at[0], held_ref, sent_refs, out_sems)
     for store in stores:
         store.wait()
 
 
-def send_rows(table, gate, up, layer, cap, halves):
+def send_rows(table, gate, up, layer, cap):
     _, rows, narrow = gate.shape
     blocks = table.shape[0]
-    steps = 2
-    if halves:
-        counts = [blocks // 2 * cap] + [cap] * (blocks // 2)
-    else:
-        counts = [blocks * cap]
     return pl.pallas_call(
-        functools.partial(send_kernel, layer, cap, halves),
-        out_shape=[jax.ShapeDtypeStruct((count, 2 * narrow), BF16) for count in counts],
+        functools.partial(send_kernel, layer, cap),
+        out_shape=[jax.ShapeDtypeStruct((cap, 2 * narrow), BF16)] * blocks,
         in_specs=[HBM] * 3,
-        out_specs=[HBM] * len(counts),
+        out_specs=[HBM] * blocks,
         scratch_shapes=[
             pltpu.VMEM((blocks, rows), I32),
-            pltpu.VMEM((rows, 2 * narrow), BF16),
+            pltpu.VMEM((1, rows, 2 * narrow), BF16),
             pltpu.VMEM((blocks * cap, 2 * narrow), BF16),
             pltpu.VMEM((blocks, rows), I32),
             pltpu.VMEM((blocks, rows), I32),
             pltpu.SemaphoreType.DMA(()),
-            pltpu.SemaphoreType.DMA((2, steps)),
-            pltpu.SemaphoreType.DMA((2 * steps, len(counts))),
+            pltpu.SemaphoreType.DMA((1, 2)),
+            pltpu.SemaphoreType.DMA((2, blocks)),
         ],
         cost_estimate=pl.CostEstimate(
             flops=4 * blocks * cap * rows * narrow,
             bytes_accessed=8 * rows * narrow,
             transcendentals=0,
         ),
+        name="send_rows",
     )(table, gate, up)
 
 
-def load_weights(layers, gate_ref, up_ref, in_ref, sems):
-    loads = []
-    for at, layer in enumerate(layers):
-        for side, ref in enumerate((gate_ref, up_ref)):
-            loads.append(
-                pltpu.make_async_copy(ref.at[layer], in_ref.at[at, side], sems.at[at, side])
+def running_order(hit):
+    lines, lanes = hit.shape
+    ones = hit.astype(F32)
+    before = (iota((lanes, lanes), 0) < iota((lanes, lanes), 1)).astype(F32).astype(BF16)
+    above = (iota((lines, lines), 1) < iota((lines, lines), 0)).astype(F32).astype(BF16)
+    sums = jnp.broadcast_to(jnp.sum(ones, axis=1, keepdims=True), (lines, lanes))
+    total = jnp.dot(ones.astype(BF16), before, preferred_element_type=F32) + jnp.dot(
+        above, sums.astype(BF16), preferred_element_type=F32
+    )
+    return jnp.where(hit, total.astype(I32), -1)
+
+
+def column_plan(narrow, map_ref, near_ref, send_ref, far_ref, splits):
+    rank = lax.axis_index("mp")
+    lines = map_ref.shape[0] // splits
+    lanes = map_ref.shape[1]
+    width = send_ref.shape[1]
+    blocks = [map_ref[split * lines : (split + 1) * lines, :] for split in range(splits)]
+
+    def block_of(index):
+        chosen = blocks[0]
+        for split in range(1, splits):
+            chosen = jnp.where(index == split, blocks[split], chosen)
+        owner = lax.div(chosen, jnp.full_like(chosen, narrow))
+        return owner, chosen - owner * narrow
+
+    def flatten(value, ref, at):
+        for line in range(lines):
+            ref[at : at + 1, line * lanes : (line + 1) * lanes] = value[line : line + 1, :]
+
+    owner, within = block_of(rank)
+    flatten(jnp.where(owner == rank, within, -1), near_ref, 0)
+    for turn in range(1, splits):
+        flatten(
+            running_order(owner == lax.rem(rank + splits - turn, splits)), far_ref, turn - 1
+        )
+        their_owner, their_within = block_of(lax.rem(rank + turn, splits))
+        key = running_order(their_owner == rank)
+        value = (their_within + 1).astype(F32)
+        for start in range(0, width, lanes):
+            slot = iota((lanes, lanes), 0) + start
+            held = jnp.zeros((lanes, lanes), F32)
+            for line in range(lines):
+                held = jnp.where(key[line : line + 1, :] == slot, value[line : line + 1, :], held)
+            column = jnp.sum(held, axis=1, keepdims=True)
+            diagonal = iota((lanes, lanes), 0) == iota((lanes, lanes), 1)
+            send_ref[turn - 1 : turn, start : start + lanes] = (
+                jnp.sum(jnp.where(diagonal, column, 0.0), axis=0, keepdims=True).astype(I32) - 1
             )
-            loads[-1].start()
-    return loads
-
-
-def own_kernel(table_ref, ids_ref, gate_ref, up_ref, out_ref, in_ref, own_ref, sems):
+
+
+def middle_kernel(
+    cap, splits, table_ref, map_ref, gate_ref, up_ref, turn_ref, near_ref, send_ref, far_ref, sent_ref,
+    in_ref, own_ref, held_ref, key_ref, within_ref, in_sems, out_sems,
+):
     layers, rows, narrow = gate_ref.shape
-    loads = load_weights([layers - 1], gate_ref, up_ref, in_ref, sems)
+    loads = load_weights([layers - 1, 0], gate_ref, up_ref, in_ref, in_sems)
     me = lax.axis_index("section")
-    scale = 1.0 / count_of(table_ref[...], iota((rows, 1), 0) + me * rows)
-    for side, load in enumerate(loads):
+    table = table_ref[...]
+    column_plan(narrow, map_ref, near_ref, send_ref, far_ref, splits)
+    scale = 1.0 / count_of(table, iota((rows, 1), 0) + me * rows)
+    pick, count = pick_matrix(table, me, cap, key_ref, within_ref, list(range(table.shape[0])))
+    stores = put_slots(
+        loads[2:], pick, 1.0 / count, in_ref.at[1], held_ref, (sent_ref,), out_sems
+    )
+    for side, load in enumerate(loads[:2]):
         load.wait()
-        own_ref[side * rows : (side + 1) * rows] = (in_ref[0, side].astype(F32) * scale).astype(BF16)
-    for s in range(ids_ref.shape[0]):
-        out_ref[s] = onehot_dot(own_ref, ids_ref[s : s + 1, :], narrow).astype(BF16)
-
-
-def own_rows(table, ids, gate, up):
+        columns = in_ref[0, :, side * narrow : (side + 1) * narrow]
+        own_ref[side * rows : (side + 1) * rows] = (columns.astype(F32) * scale).astype(BF16)
+    for s in range(splits - 1):
+        turn_ref[s] = onehot_dot(own_ref, send_ref[s : s + 1, :], narrow).astype(BF16)
+    for store in stores:
+        store.wait()
+
+
+def middle(table, columns, gate, up, cap, splits, width):
     _, rows, narrow = gate.shape
-    turns, width = ids.shape
+    blocks = table.shape[0]
+    extra = columns.size // splits
     return pl.pallas_call(
-        own_kernel,
-        out_shape=jax.ShapeDtypeStruct((turns, 2 * rows, width), BF16),
+        functools.partial(middle_kernel, cap, splits),
+        out_shape=(
+            jax.ShapeDtypeStruct((splits - 1, 2 * rows, width), BF16),
+            jax.ShapeDtypeStruct((1, extra), I32),
+            jax.ShapeDtypeStruct((splits - 1, width), I32),
+            jax.ShapeDtypeStruct((splits - 1, extra), I32),
+            jax.ShapeDtypeStruct((blocks * cap, 2 * narrow), BF16),
+        ),
         in_specs=[VMEM, VMEM, HBM, HBM],
-        out_specs=VMEM,
+        out_specs=(VMEM, VMEM, VMEM, VMEM, HBM),
         scratch_shapes=[
-            pltpu.VMEM((1, 2, rows, narrow), BF16),
+            pltpu.VMEM((2, rows, 2 * narrow), BF16),
             pltpu.VMEM((2 * rows, narrow), BF16),
-            pltpu.SemaphoreType.DMA((1, 2)),
+            pltpu.VMEM((blocks * cap, 2 * narrow), BF16),
+            pltpu.VMEM((blocks, rows), I32),
+            pltpu.VMEM((blocks, rows), I32),
+            pltpu.SemaphoreType.DMA((2, 2)),
+            pltpu.SemaphoreType.DMA((2, 1)),
         ],
         cost_estimate=pl.CostEstimate(
-            flops=4 * rows * narrow * width * turns,
-            bytes_accessed=8 * rows * narrow,
+            flops=4 * rows * narrow * width,
+            bytes_accessed=16 * rows * narrow,
             transcendentals=0,
         ),
-        name="own_rows",
-    )(table, ids, gate, up)
+        name="middle",
+    )(table, columns, gate, up)
 
 
 def land_kernel(cap, table_ref, land_ref):
@@ -222,10 +282,9 @@
     *came_refs, rows_ref, out_ref, held_ref, sems = refs
     narrow = rows_ref.shape[1]
     rows = land_ref.shape[0]
-    cap = came_refs[1].shape[0]
-    half = len(came_refs) - 1
+    cap = came_refs[0].shape[0]
     me = lax.axis_index("section")
-    starts = [lax.div(me, half) * half] + [me ^ p for p in range(half, 2 * half)]
+    starts = [me ^ p for p in range(len(came_refs))]
     loads = []
     for piece, (ref, start) in enumerate(zip(came_refs, starts)):
         where = pl.ds(pl.multiple_of(start * cap, cap), ref.shape[0])
@@ -341,7 +400,8 @@
         at, side = number // 2, number % 2
         load.wait()
         here = pl.ds(side * rows, rows)
-        base_ref[at, here] = (in_ref[at, side].astype(F32) * scale).astype(BF16)
+        columns = in_ref[at, :, side * narrow : (side + 1) * narrow]
+        base_ref[at, here] = (columns.astype(F32) * scale).astype(BF16)
         copies.append(
             pltpu.make_async_copy(
                 base_ref.at[at, here],
@@ -368,7 +428,7 @@
         in_specs=[VMEM] * 4 + [HBM] * 2,
         out_specs=(HBM, HBM),
         scratch_shapes=[
-            pltpu.VMEM((layers, 2, rows, narrow), BF16),
+            pltpu.VMEM((layers, rows, 2 * narrow), BF16),
             pltpu.VMEM((layers, 2 * rows, narrow), BF16),
             pltpu.VMEM((2 * rows, extra), BF16),
             pltpu.SemaphoreType.DMA((layers, 2)),
@@ -500,38 +560,6 @@
     )(land, came, gate_out, up_out)
 
 
-def column_plan(ffn_map, splits, narrow, width):
-    rank = lax.axis_index("mp")
-    extra = ffn_map.shape[0] // splits
-    table = ffn_map.reshape(splits, extra)
-    owner = table // narrow
-    within = table - owner * narrow
-
-    def line(array, at):
-        return lax.dynamic_index_in_dim(array, at, 0, keepdims=False)
-
-    my_owner, my_within = line(owner, rank), line(within, rank)
-    near = jnp.where(my_owner == rank, my_within, -1)[None, :]
-    turns = range(1, splits)
-    targets = [lax.rem(rank + turn, splits) for turn in turns]
-    origins = [lax.rem(rank + splits - turn, splits) for turn in turns]
-    hits = jnp.stack(
-        [line(owner, target) == rank for target in targets]
-        + [my_owner == origin for origin in origins]
-    )
-    order = jnp.where(hits, jnp.cumsum(hits.astype(I32), axis=1) - 1, -1)
-    slots = jnp.arange(width, dtype=I32)
-    sends = [
-        jnp.sum(
-            jnp.where(order[at][None, :] == slots[:, None], line(within, target)[None, :] + 1, 0),
-            axis=1,
-        )
-        - 1
-        for at, target in enumerate(targets)
-    ]
-    return near, jnp.stack(sends), order[splits - 1 :]
-
-
 def turn_around(sent, splits):
     return jnp.stack(
         [
@@ -552,26 +580,19 @@
     table = hidden_map.reshape(blocks, rows)
     out_type = jax.ShapeDtypeStruct((layers, 2, rows, narrow + extra), BF16)
 
-    half = blocks // 2
-    groups = [list(range(half)), list(range(half, blocks))]
-
-    def swap_rows(sent, groups=None):
-        return lax.all_to_all(
-            sent, "section", split_axis=0, concat_axis=0, tiled=True, axis_index_groups=groups
-        )
+    def swap_rows(sent):
+        return lax.all_to_all(sent, "section", split_axis=0, concat_axis=0, tiled=True)
 
     def cross(sent, p):
         return lax.ppermute(sent, "section", [(i, i ^ p) for i in range(blocks)])
 
-    sent_top = send_rows(table, gate_weight, up_weight, layers - 1, cap, True)
-    came_top = [cross(sent_top[1 + p], half + p) for p in range(half)]
-    came_top.insert(0, swap_rows(sent_top[0], groups))
-    sent_top = sent_top[0]
-    ffn_map, table = lax.optimization_barrier((ffn_map, sent_top, table))[::2]
-    near_ids, send_ids, far_ids = column_plan(ffn_map, splits, narrow, width)
-    own_sent = own_rows(table, send_ids, gate_weight, up_weight)
+    sent_top = send_rows(table, gate_weight, up_weight, layers - 1, cap)
+    came_top = [sent_top[0]] + [cross(sent_top[p], p) for p in range(1, blocks)]
+    columns = ffn_map.reshape(-1, 128)
+    own_sent, near_ids, send_ids, far_ids, sent_low = middle(
+        table, columns, gate_weight, up_weight, cap, splits, width
+    )
     own_far = turn_around(own_sent, splits)
-    sent_low = send_rows(table, gate_weight, up_weight, 0, cap, False)[0]
     came_low = swap_rows(sent_low)
     land = land_rows(table, cap)
     got, got_sent = arrive_rows(land, send_ids, came_top)

time: 118 us -> 109 us (0.924)
  waiting for transfers between devices: 43.3 us -> 34.5 us
  starting transfers between devices: 30.3 us -> 36.7 us
  other arithmetic: 2.86 us -> 0 us
  Pallas kernels: 37.7 us -> 34.9 us
    ppermute x8 -> x15, starting transfers between devices: 16.4 us -> 27.7 us  [cross(): return lax.ppermute(sent, 'section', [(i, i ^ p) for i in range(blocks)])]
    ppermute x8 -> x15, waiting for transfers between devices: 38.5 us -> 32.2 us  [cross(): return lax.ppermute(sent, 'section', [(i, i ^ p) for i in range(blocks)])]
    all_to_all x2 -> x1, starting transfers between devices: 11.3 us -> 6.53 us  [swap_rows(): lax.all_to_all(sent, 'section', split_axis=0, concat_axis=0, tiled=True)]
    all_to_all x2 -> x1, waiting for transfers between devices: 3.45 us -> 0.01 us  [swap_rows(): lax.all_to_all(sent, 'section', split_axis=0, concat_axis=0, tiled=True)]
    pallas_call x3 -> x2, Pallas kernels: 12.4 us -> 9.97 us  [the longest x1 6.75 us: middle(): pl.pallas_call(functools.partial(middle_kernel, cap, splits), out_shape=(...]
    reduce_sum x1 -> x0, other arithmetic: 1.69 us -> none  [column_plan(): jnp.sum(jnp.where(order[at][None, :] == slots[:, None], line(within, targ...]
  transfers between devices with their start and end apart: 12 -> 18, of which waited for: 9 -> 12; matrix products, arithmetic and copies ran while one was open for 4% -> 0% of each run, Pallas kernels for 27% -> 24%
where the time goes in v2:
time: 109 us; the launch traced here: 108 us
  starting transfers between devices  36.7 us (34%)
  Pallas kernels  34.9 us (32%)
  waiting for transfers between devices  34.5 us (32%)
    ppermute x15, waiting for transfers between devices, cross(): return lax.ppermute(sent, 'section', [(i, i ^ p) for i in range(blocks)])  32.2 us
    ppermute x15, starting transfers between devices, cross(): return lax.ppermute(sent, 'section', [(i, i ^ p) for i in range(blocks)])  27.7 us
    pallas_call x1, Pallas kernels, first_half(): pl.pallas_call(first_kernel, out_shape=(out_type, out_type), in_specs=[VM...  9.54 us
    pallas_call x1, Pallas kernels, middle(): pl.pallas_call(functools.partial(middle_kernel, cap, splits), out_shape=(...  6.75 us
    all_to_all x1, starting transfers between devices, swap_rows(): lax.all_to_all(sent, 'section', split_axis=0, concat_axis=0, tiled=True)  6.53 us
    pallas_call x1, Pallas kernels, arrive_rows(): pl.pallas_call(arrive_kernel, out_shape=(jax.ShapeDtypeStruct((2 * rows,...  4.95 us
    pallas_call x1, Pallas kernels, near_columns(): pl.pallas_call(near_kernel, out_shape=jax.ShapeDtypeStruct((count, extra)...  4.48 us
    pallas_call x1, Pallas kernels, second_half(): pl.pallas_call(second_kernel, out_shape=(out_type, out_type), in_specs=[V...  3.83 us
  transfers between devices with their start and end apart: 18, of which 12 were waited for; matrix products, arithmetic and copies ran while one was open for 0% of the time, Pallas kernels for 24%

profile of v2, /device:TPU:13, one launch (start us, length us, event | category | flops | bytes accessed | tf_op | source)
XLA Modules:
  0.0 108.0 jit_solution(2841187443248266418)
XLA Ops:
  0.6 0.0 copy-start.2
  0.6 6.8 %middle.1 = (bf16[1,256,1408]{2,1,0:T(8,128)(2,1)}, s32[1,2688]{1,0:T(1,128)}, s32[1,1408]{1,0:T(1,128)}, s32[1,2688]{1,0:T(1,128)}, bf16[128,5632]{1,0:T(8,128)(2,1)}) custom-call(s32[16,128]{1,0:T(8,128)} %bitcast.10, s32[42,128]{1,0:T(8,128)} %bitcast.18, bf16[2,128,2816]{2,1,0:T(8,128)(2,1)} %gate_ref.5, bf16[2,128,2816]{2,1,0:T(8,128)(2,1)} %up_ref.5), custom_call_target="tpu_custom_call" | custom-call | flops 2030043136 | bytes 5767168 | tf_op jit(solution)/shard_map/middle/pallas_call | solution.py:235
  7.4 0.0 copy-start.6
  7.4 6.5 %all-to-all-start = ((bf16[16,8,5632]{2,1,0:T(8,128)(2,1)}), bf16[16,8,5632]{2,1,0:T(8,128)(2,1)S(1)}, u32[]{:S(2)}, u32[]{:S(2)}) async-start(bf16[16,8,5632]{2,1,0:T(8,128)(2,1)} %bitcast.16), calls=%async_computation | async-start | bytes 2883584 | tf_op jit(solution)/shard_map/all_to_all | solution.py:584
  13.9 0.0 copy-start.5
  14.0 3.2 %send_rows.1 = (bf16[8,5632]{1,0:T(8,128)(2,1)}, bf16[8,5632]{1,0:T(8,128)(2,1)}, bf16[8,5632]{1,0:T(8,128)(2,1)}, bf16[8,5632]{1,0:T(8,128)(2,1)}, bf16[8,5632]...) custom-call(s32[16,128]{1,0:T(8,128)} %bitcast.11, ...), custom_call_target="tpu_custom_call" | custom-call | flops 184549376 | bytes 2883584 | tf_op jit(solution)/shard_map/send_rows/pallas_call | solution.py:132
  17.2 0.5 collective-permute-start
  17.6 0.3 collective-permute-start.1
  17.9 1.5 %collective-permute-start.2 = (bf16[8,5632]{1,0:T(8,128)(2,1)}, bf16[8,5632]{1,0:T(8,128)(2,1)S(1)}, u32[]{:S(2)}, u32[]{:S(2)}) collective-permute-start(bf16[8,5632]{1,0:T(8,128)(2,1)} %get-tuple-element.34), channel_id=1, source_target_pairs={{0,6},{2,4},{4,2},{6,0},{8,14},{10,12},{12,10},{14,8},{16,22},{18,... | collective-permute-start | bytes 270344 | tf_op jit(solution)/shard_map/ppermute | solution.py:587
  19.4 0.3 collective-permute-start.3
  19.7 1.5 %collective-permute-start.4 = (bf16[8,5632]{1,0:T(8,128)(2,1)}, bf16[8,5632]{1,0:T(8,128)(2,1)S(1)}, u32[]{:S(2)}, u32[]{:S(2)}) collective-permute-start(bf16[8,5632]{1,0:T(8,128)(2,1)} %get-tuple-element.36), channel_id=1, source_target_pairs={{0,10},{2,8},{4,14},{6,12},{8,2},{10,0},{12,6},{14,4},{16,26},{18,... | collective-permute-start | bytes 270344 | tf_op jit(solution)/shard_map/ppermute | solution.py:587
  21.1 0.0 collective-permute-done.refs_1_
  21.1 0.0 collective-permute-start.5
  21.1 1.7 %collective-permute-done.1.refs_2_ = bf16[8,5632]{1,0:T(8,128)(2,1)S(1)} collective-permute-done((bf16[8,5632]{1,0:T(8,128)(2,1)}, bf16[8,5632]{1,0:T(8,128)(2,1)S(1)}, u32[]{:S(2)}, u32[]{:S(2)}) %collective-permute-start.1) | collective-permute-done | bytes 90144 | tf_op jit(solution)/shard_map/ppermute | solution.py:587
  22.8 5.7 %collective-permute-start.6 = (bf16[8,5632]{1,0:T(8,128)(2,1)}, bf16[8,5632]{1,0:T(8,128)(2,1)S(1)}, u32[]{:S(2)}, u32[]{:S(2)}) collective-permute-start(bf16[8,5632]{1,0:T(8,128)(2,1)} %get-tuple-element.38), channel_id=1, source_target_pairs={{0,14},{2,12},{4,10},{6,8},{8,6},{10,4},{12,2},{14,0},{16,30},{18,... | collective-permute-start | bytes 270344 | tf_op jit(solution)/shard_map/ppermute | solution.py:587
  28.5 0.0 collective-permute-done.2.refs_3_
  28.6 2.7 %collective-permute-start.7 = (bf16[8,5632]{1,0:T(8,128)(2,1)}, bf16[8,5632]{1,0:T(8,128)(2,1)S(1)}, u32[]{:S(2)}, u32[]{:S(2)}) collective-permute-start(bf16[8,5632]{1,0:T(8,128)(2,1)} %get-tuple-element.39), channel_id=1, source_target_pairs={{0,16},{2,18},{4,20},{6,22},{8,24},{10,26},{12,28},{14,30},{16,0},... | collective-permute-start | bytes 270344 | tf_op jit(solution)/shard_map/ppermute | solution.py:587
  31.2 9.1 %collective-permute-done.3.refs_4_ = bf16[8,5632]{1,0:T(8,128)(2,1)S(1)} collective-permute-done((bf16[8,5632]{1,0:T(8,128)(2,1)}, bf16[8,5632]{1,0:T(8,128)(2,1)S(1)}, u32[]{:S(2)}, u32[]{:S(2)}) %collective-permute-start.3) | collective-permute-done | bytes 90144 | tf_op jit(solution)/shard_map/ppermute | solution.py:587
  40.4 2.6 %collective-permute-start.8 = (bf16[8,5632]{1,0:T(8,128)(2,1)}, bf16[8,5632]{1,0:T(8,128)(2,1)S(1)}, u32[]{:S(2)}, u32[]{:S(2)}) collective-permute-start(bf16[8,5632]{1,0:T(8,128)(2,1)} %get-tuple-element.40), channel_id=1, source_target_pairs={{0,18},{2,16},{4,22},{6,20},{8,26},{10,24},{12,30},{14,28},{16,2},... | collective-permute-start | bytes 270344 | tf_op jit(solution)/shard_map/ppermute | solution.py:587
  43.0 0.5 collective-permute-done.4.refs_5_
  43.5 0.3 collective-permute-start.9
  43.7 0.8 collective-permute-done.5.refs_6_
  44.6 3.8 %collective-permute-start.10 = (bf16[8,5632]{1,0:T(8,128)(2,1)}, bf16[8,5632]{1,0:T(8,128)(2,1)S(1)}, u32[]{:S(2)}, u32[]{:S(2)}) collective-permute-start(bf16[8,5632]{1,0:T(8,128)(2,1)} %get-tuple-element.42), channel_id=1, source_target_pairs={{0,22},{2,20},{4,18},{6,16},{8,30},{10,28},{12,26},{14,24},{16,6},... | collective-permute-start | bytes 270344 | tf_op jit(solution)/shard_map/ppermute | solution.py:587
  48.3 0.0 collective-permute-done.6.refs_7_
  48.3 1.2 %collective-permute-start.16 = (bf16[256,1408]{1,0:T(8,128)(2,1)}, bf16[256,1408]{1,0:T(8,128)(2,1)S(1)}, u32[]{:S(2)}, u32[]{:S(2)}) collective-permute-start(bf16[256,1408]{1,0:T(8,128)(2,1)} %bitcast.17), channel_id=1, source_target_pairs={{0,1},{1,0},{2,3},{3,2},{4,5},{5,4},{6,7},{7,6},{8,9},{9,8},{10,11... | collective-permute-start | bytes 2162696 | tf_op jit(solution)/shard_map/ppermute | solution.py:566
  49.6 1.7 %collective-permute-done.7.refs_8_ = bf16[8,5632]{1,0:T(8,128)(2,1)S(1)} collective-permute-done((bf16[8,5632]{1,0:T(8,128)(2,1)}, bf16[8,5632]{1,0:T(8,128)(2,1)S(1)}, u32[]{:S(2)}, u32[]{:S(2)}) %collective-permute-start.7) | collective-permute-done | bytes 90144 | tf_op jit(solution)/shard_map/ppermute | solution.py:587
  51.2 0.0 collective-permute-start.11
  51.2 5.8 %collective-permute-done.8.refs_9_ = bf16[8,5632]{1,0:T(8,128)(2,1)S(1)} collective-permute-done((bf16[8,5632]{1,0:T(8,128)(2,1)}, bf16[8,5632]{1,0:T(8,128)(2,1)S(1)}, u32[]{:S(2)}, u32[]{:S(2)}) %collective-permute-start.8) | collective-permute-done | bytes 90144 | tf_op jit(solution)/shard_map/ppermute | solution.py:587
  57.1 2.4 %collective-permute-start.12 = (bf16[8,5632]{1,0:T(8,128)(2,1)}, bf16[8,5632]{1,0:T(8,128)(2,1)S(1)}, u32[]{:S(2)}, u32[]{:S(2)}) collective-permute-start(bf16[8,5632]{1,0:T(8,128)(2,1)} %get-tuple-element.44), channel_id=1, source_target_pairs={{0,26},{2,24},{4,30},{6,28},{8,18},{10,16},{12,22},{14,20},{16,10}... | collective-permute-start | bytes 270344 | tf_op jit(solution)/shard_map/ppermute | solution.py:587
  59.5 0.0 collective-permute-done.9.refs_10_
  59.5 0.7 collective-permute-start.13
  60.2 1.6 %collective-permute-done.10.refs_11_ = bf16[8,5632]{1,0:T(8,128)(2,1)S(1)} collective-permute-done((bf16[8,5632]{1,0:T(8,128)(2,1)}, bf16[8,5632]{1,0:T(8,128)(2,1)S(1)}, u32[]{:S(2)}, u32[]{:S(2)}) %collective-permute-start.10) | collective-permute-done | bytes 90144 | tf_op jit(solution)/shard_map/ppermute | solution.py:587
  61.9 5.5 %collective-permute-start.14 = (bf16[8,5632]{1,0:T(8,128)(2,1)}, bf16[8,5632]{1,0:T(8,128)(2,1)S(1)}, u32[]{:S(2)}, u32[]{:S(2)}) collective-permute-start(bf16[8,5632]{1,0:T(8,128)(2,1)} %get-tuple-element.46), channel_id=1, source_target_pairs={{0,30},{2,28},{4,26},{6,24},{8,22},{10,20},{12,18},{14,16},{16,14}... | collective-permute-start | bytes 270344 | tf_op jit(solution)/shard_map/ppermute | solution.py:587
  67.4 0.0 copy-done.2
  67.4 0.2 land_rows.1.land_ref
  67.6 3.8 %collective-permute-done.11.refs_12_ = bf16[8,5632]{1,0:T(8,128)(2,1)S(1)} collective-permute-done((bf16[8,5632]{1,0:T(8,128)(2,1)}, bf16[8,5632]{1,0:T(8,128)(2,1)S(1)}, u32[]{:S(2)}, u32[]{:S(2)}) %collective-permute-start.11) | collective-permute-done | bytes 90144 | tf_op jit(solution)/shard_map/ppermute | solution.py:587
  71.4 2.8 %collective-permute-done.12.refs_13_ = bf16[8,5632]{1,0:T(8,128)(2,1)S(1)} collective-permute-done((bf16[8,5632]{1,0:T(8,128)(2,1)}, bf16[8,5632]{1,0:T(8,128)(2,1)S(1)}, u32[]{:S(2)}, u32[]{:S(2)}) %collective-permute-start.12) | collective-permute-done | bytes 90144 | tf_op jit(solution)/shard_map/ppermute | solution.py:587
  74.2 2.2 %collective-permute-done.13.refs_14_ = bf16[8,5632]{1,0:T(8,128)(2,1)S(1)} collective-permute-done((bf16[8,5632]{1,0:T(8,128)(2,1)}, bf16[8,5632]{1,0:T(8,128)(2,1)S(1)}, u32[]{:S(2)}, u32[]{:S(2)}) %collective-permute-start.13) | collective-permute-done | bytes 90144 | tf_op jit(solution)/shard_map/ppermute | solution.py:587
  76.3 2.2 %collective-permute-done.14.refs_15_ = bf16[8,5632]{1,0:T(8,128)(2,1)S(1)} collective-permute-done((bf16[8,5632]{1,0:T(8,128)(2,1)}, bf16[8,5632]{1,0:T(8,128)(2,1)S(1)}, u32[]{:S(2)}, u32[]{:S(2)}) %collective-permute-start.14) | collective-permute-done | bytes 90144 | tf_op jit(solution)/shard_map/ppermute | solution.py:587
  78.5 0.0 copy-done.6
  78.5 0.0 copy-start.4
  78.5 0.9 copy-done.4
  79.4 4.9 %arrive_rows.1 = (bf16[256,2816]{1,0:T(8,128)(2,1)S(1)}, bf16[1,256,1408]{2,1,0:T(8,128)(2,1)S(1)}) custom-call(bf16[128,128]{1,0:T(8,128)(2,1)S(1)} %land_rows.1.land_ref, s32[1,1408]{1,0:T(1,128)S(1)} %copy-done.6, bf16[8,5632]{1,0:T(8,128)(2,1)S(1)} %copy-done.4, bf16[8,5632]{1,0:T(8,128)(2,1)S(1)} %collective-permute-done.refs_1_, ...), custom_call_target="tpu_custom_call" | custom-call | flops 2030043136 | bytes 2883584 | tf_op jit(solution)/shard_map/arrive_rows/pallas_call | solution.py:309
  84.4 1.3 %collective-permute-start.15 = (bf16[256,1408]{1,0:T(8,128)(2,1)S(1)}, bf16[256,1408]{1,0:T(8,128)(2,1)S(1)}, u32[]{:S(2)}, u32[]{:S(2)}) collective-permute-start(bf16[256,1408]{1,0:T(8,128)(2,1)S(1)} %bitcast.15), channel_id=1, source_target_pairs={{0,1},{1,0},{2,3},{3,2},{4,5},{5,4},{6,7},{7,6},{8,9},{9,8},{10,11... | collective-permute-start | bytes 2162696 | tf_op jit(solution)/shard_map/ppermute | solution.py:566
  85.7 0.0 copy-done.5
  85.7 0.0 copy-start
  85.7 0.0 copy-start.1
  85.7 0.0 copy-start.3
  85.7 4.5 %shard_map.59.near_ref = bf16[256,2688]{1,0:T(8,128)(2,1)S(1)} custom-call(bf16[256,2816]{1,0:T(8,128)(2,1)S(1)} %get-tuple-element.47.rows_ref, s32[1,2688]{1,0:T(1,128)S(1)} %copy-done.5), custom_call_target="tpu_custom_call" | custom-call | flops 3875536896 | bytes 2818048 | tf_op jit(solution)/shard_map/pallas_call | solution.py:341
  90.2 0.0 collective-permute-done.16
  90.2 0.0 copy-done
  90.2 0.0 copy-done.1
  90.2 0.0 copy-done.3
  90.2 9.5 %first_half.1 = (bf16[2,2,128,5504]{3,2,1,0:T(8,128)(2,1)}, bf16[2,2,128,5504]{3,2,1,0:T(8,128)(2,1)}) custom-call(s32[16,128]{1,0:T(8,128)S(1)} %bitcast.13, s32[1,2688]{1,0:T(1,128)S(1)} %copy-done.5, bf16[1,256,1408]{2,1,0:T(8,128)(2,1)S(1)} %bitcast.14, s32[1,2688]{1,0:T(1,128)S(1)} %copy-done.3, bf16[2,128,2816]{2,1,0:T(8,128)(2,1)S(1)} %copy-done, ...), custom_call_target="tpu_custom_call" | custom-call | flops 5813305344 | bytes 11272192 | tf_op jit(solution)/shard_map/first_half/pallas_call | solution.py:425
  99.7 2.3 %collective-permute-done.15 = bf16[256,1408]{1,0:T(8,128)(2,1)S(1)} collective-permute-done((bf16[256,1408]{1,0:T(8,128)(2,1)S(1)}, bf16[256,1408]{1,0:T(8,128)(2,1)S(1)}, u32[]{:S(2)}, u32[]{:S(2)}) %collective-permute-start.15) | collective-permute-done | bytes 720928 | tf_op jit(solution)/shard_map/ppermute | solution.py:566
  102.0 3.8 %second_half.1 = (bf16[2,2,128,5504]{3,2,1,0:T(8,128)(2,1)}, bf16[2,2,128,5504]{3,2,1,0:T(8,128)(2,1)}) custom-call(bf16[256,2816]{1,0:T(8,128)(2,1)S(1)} %get-tuple-element.47.rows_ref, bf16[256,2688]{1,0:T(8,128)(2,1)S(1)} %shard_map.59.near_ref, bf16[1,256,1408]{2,1,0:T(8,128)(2,1)S(1)} %bitcast.9, ...), custom_call_target="tpu_custom_call", output_to_operand_aliasing={{0}: (4, {}), {1}: (5, {})} | custom-call | flops 1937768448 | bytes 8388608 | tf_op jit(solution)/shard_map/second_half/pallas_call | solution.py:479
  105.9 0.0 all-to-all-done
  105.9 2.0 %last_rows.1 = (bf16[2,2,128,5504]{3,2,1,0:T(8,128)(2,1)}, bf16[2,2,128,5504]{3,2,1,0:T(8,128)(2,1)}) custom-call(bf16[128,128]{1,0:T(8,128)(2,1)S(1)} %land_rows.1.land_ref, bf16[128,5632]{1,0:T(8,128)(2,1)S(1)} %bitcast.8, bf16[2,2,128,5504]{3,2,1,0:T(8,128)(2,1)} %get-tuple-element.54.gate_in, ...), custom_call_target="tpu_custom_call", output_to_operand_aliasing={{0}: (2, {}), {1}: (3, {})} | custom-call | flops 184549376 | bytes 2883584 | tf_op jit(solution)/shard_map/last_rows/pallas_call | solution.py:541
Async XLA Ops:
  0.6 66.7 %copy-start.2 = (s32[2048]{0:T(1024)S(1)}, s32[2048]{0:T(1024)}, u32[]{:S(2)}) copy-start(s32[2048]{0:T(1024)} %param.6) | copy-start | bytes 24580
  7.4 71.1 %copy-start.6 = (s32[1,1408]{1,0:T(1,128)S(1)}, s32[1,1408]{1,0:T(1,128)}, u32[]{:S(2)}) copy-start(s32[1,1408]{1,0:T(1,128)} %get-tuple-element.30.ids_ref) | copy-start | bytes 16900
  7.4 98.5 %all-to-all-start = ((bf16[16,8,5632]{2,1,0:T(8,128)(2,1)}), bf16[16,8,5632]{2,1,0:T(8,128)(2,1)S(1)}, u32[]{:S(2)}, u32[]{:S(2)}) async-start(bf16[16,8,5632]{2,1,0:T(8,128)(2,1)} %bitcast.16), calls=%async_computation | async-start | bytes 2883584 | tf_op jit(solution)/shard_map/all_to_all | solution.py:584
  13.9 71.7 %copy-start.5 = (s32[1,2688]{1,0:T(1,128)S(1)}, s32[1,2688]{1,0:T(1,128)}, u32[]{:S(2)}) copy-start(s32[1,2688]{1,0:T(1,128)} %get-tuple-element.48.ids_ref.near_ids_ref) | copy-start | bytes 32260
  17.2 4.0 %collective-permute-start = (bf16[8,5632]{1,0:T(8,128)(2,1)}, bf16[8,5632]{1,0:T(8,128)(2,1)S(1)}, u32[]{:S(2)}, u32[]{:S(2)}) collective-permute-start(bf16[8,5632]{1,0:T(8,128)(2,1)} %get-tuple-element.32), channel_id=1, source_target_pairs={{0,2},{2,0},{4,6},{6,4},{8,10},{10,8},{12,14},{14,12},{16,18},{18,... | collective-permute-start | bytes 270344 | tf_op jit(solution)/shard_map/ppermute | solution.py:587
  17.6 5.2 %collective-permute-start.1 = (bf16[8,5632]{1,0:T(8,128)(2,1)}, bf16[8,5632]{1,0:T(8,128)(2,1)S(1)}, u32[]{:S(2)}, u32[]{:S(2)}) collective-permute-start(bf16[8,5632]{1,0:T(8,128)(2,1)} %get-tuple-element.33), channel_id=1, source_target_pairs={{0,4},{2,6},{4,0},{6,2},{8,12},{10,14},{12,8},{14,10},{16,20},{18,... | collective-permute-start | bytes 270344 | tf_op jit(solution)/shard_map/ppermute | solution.py:587
  17.9 10.6 %collective-permute-start.2 = (bf16[8,5632]{1,0:T(8,128)(2,1)}, bf16[8,5632]{1,0:T(8,128)(2,1)S(1)}, u32[]{:S(2)}, u32[]{:S(2)}) collective-permute-start(bf16[8,5632]{1,0:T(8,128)(2,1)} %get-tuple-element.34), channel_id=1, source_target_pairs={{0,6},{2,4},{4,2},{6,0},{8,14},{10,12},{12,10},{14,8},{16,22},{18,... | collective-permute-start | bytes 270344 | tf_op jit(solution)/shard_map/ppermute | solution.py:587
  19.4 21.0 %collective-permute-start.3 = (bf16[8,5632]{1,0:T(8,128)(2,1)}, bf16[8,5632]{1,0:T(8,128)(2,1)S(1)}, u32[]{:S(2)}, u32[]{:S(2)}) collective-permute-start(bf16[8,5632]{1,0:T(8,128)(2,1)} %get-tuple-element.35), channel_id=1, source_target_pairs={{0,8},{2,10},{4,12},{6,14},{8,0},{10,2},{12,4},{14,6},{16,24},{18,... | collective-permute-start | bytes 270344 | tf_op jit(solution)/shard_map/ppermute | solution.py:587
  19.7 23.8 %collective-permute-start.4 = (bf16[8,5632]{1,0:T(8,128)(2,1)}, bf16[8,5632]{1,0:T(8,128)(2,1)S(1)}, u32[]{:S(2)}, u32[]{:S(2)}) collective-permute-start(bf16[8,5632]{1,0:T(8,128)(2,1)} %get-tuple-element.36), channel_id=1, source_target_pairs={{0,10},{2,8},{4,14},{6,12},{8,2},{10,0},{12,6},{14,4},{16,26},{18,... | collective-permute-start | bytes 270344 | tf_op jit(solution)/shard_map/ppermute | solution.py:587
  21.1 23.4 %collective-permute-start.5 = (bf16[8,5632]{1,0:T(8,128)(2,1)}, bf16[8,5632]{1,0:T(8,128)(2,1)S(1)}, u32[]{:S(2)}, u32[]{:S(2)}) collective-permute-start(bf16[8,5632]{1,0:T(8,128)(2,1)} %get-tuple-element.37), channel_id=1, source_target_pairs={{0,12},{2,14},{4,8},{6,10},{8,4},{10,6},{12,0},{14,2},{16,28},{18,... | collective-permute-start | bytes 270344 | tf_op jit(solution)/shard_map/ppermute | solution.py:587
  22.8 25.5 %collective-permute-start.6 = (bf16[8,5632]{1,0:T(8,128)(2,1)}, bf16[8,5632]{1,0:T(8,128)(2,1)S(1)}, u32[]{:S(2)}, u32[]{:S(2)}) collective-permute-start(bf16[8,5632]{1,0:T(8,128)(2,1)} %get-tuple-element.38), channel_id=1, source_target_pairs={{0,14},{2,12},{4,10},{6,8},{8,6},{10,4},{12,2},{14,0},{16,30},{18,... | collective-permute-start | bytes 270344 | tf_op jit(solution)/shard_map/ppermute | solution.py:587
  28.6 22.7 %collective-permute-start.7 = (bf16[8,5632]{1,0:T(8,128)(2,1)}, bf16[8,5632]{1,0:T(8,128)(2,1)S(1)}, u32[]{:S(2)}, u32[]{:S(2)}) collective-permute-start(bf16[8,5632]{1,0:T(8,128)(2,1)} %get-tuple-element.39), channel_id=1, source_target_pairs={{0,16},{2,18},{4,20},{6,22},{8,24},{10,26},{12,28},{14,30},{16,0},... | collective-permute-start | bytes 270344 | tf_op jit(solution)/shard_map/ppermute | solution.py:587
  40.4 16.7 %collective-permute-start.8 = (bf16[8,5632]{1,0:T(8,128)(2,1)}, bf16[8,5632]{1,0:T(8,128)(2,1)S(1)}, u32[]{:S(2)}, u32[]{:S(2)}) collective-permute-start(bf16[8,5632]{1,0:T(8,128)(2,1)} %get-tuple-element.40), channel_id=1, source_target_pairs={{0,18},{2,16},{4,22},{6,20},{8,26},{10,24},{12,30},{14,28},{16,2},... | collective-permute-start | bytes 270344 | tf_op jit(solution)/shard_map/ppermute | solution.py:587
  43.5 16.0 %collective-permute-start.9 = (bf16[8,5632]{1,0:T(8,128)(2,1)}, bf16[8,5632]{1,0:T(8,128)(2,1)S(1)}, u32[]{:S(2)}, u32[]{:S(2)}) collective-permute-start(bf16[8,5632]{1,0:T(8,128)(2,1)} %get-tuple-element.41), channel_id=1, source_target_pairs={{0,20},{2,22},{4,16},{6,18},{8,28},{10,30},{12,24},{14,26},{16,4},... | collective-permute-start | bytes 270344 | tf_op jit(solution)/shard_map/ppermute | solution.py:587
  44.6 17.3 %collective-permute-start.10 = (bf16[8,5632]{1,0:T(8,128)(2,1)}, bf16[8,5632]{1,0:T(8,128)(2,1)S(1)}, u32[]{:S(2)}, u32[]{:S(2)}) collective-permute-start(bf16[8,5632]{1,0:T(8,128)(2,1)} %get-tuple-element.42), channel_id=1, source_target_pairs={{0,22},{2,20},{4,18},{6,16},{8,30},{10,28},{12,26},{14,24},{16,6},... | collective-permute-start | bytes 270344 | tf_op jit(solution)/shard_map/ppermute | solution.py:587
  48.3 41.8 %collective-permute-start.16 = (bf16[256,1408]{1,0:T(8,128)(2,1)}, bf16[256,1408]{1,0:T(8,128)(2,1)S(1)}, u32[]{:S(2)}, u32[]{:S(2)}) collective-permute-start(bf16[256,1408]{1,0:T(8,128)(2,1)} %bitcast.17), channel_id=1, source_target_pairs={{0,1},{1,0},{2,3},{3,2},{4,5},{5,4},{6,7},{7,6},{8,9},{9,8},{10,11... | collective-permute-start | bytes 2162696 | tf_op jit(solution)/shard_map/ppermute | solution.py:566
  51.2 20.2 %collective-permute-start.11 = (bf16[8,5632]{1,0:T(8,128)(2,1)}, bf16[8,5632]{1,0:T(8,128)(2,1)S(1)}, u32[]{:S(2)}, u32[]{:S(2)}) collective-permute-start(bf16[8,5632]{1,0:T(8,128)(2,1)} %get-tuple-element.43), channel_id=1, source_target_pairs={{0,24},{2,26},{4,28},{6,30},{8,16},{10,18},{12,20},{14,22},{16,8},... | collective-permute-start | bytes 270344 | tf_op jit(solution)/shard_map/ppermute | solution.py:587
  57.1 17.1 %collective-permute-start.12 = (bf16[8,5632]{1,0:T(8,128)(2,1)}, bf16[8,5632]{1,0:T(8,128)(2,1)S(1)}, u32[]{:S(2)}, u32[]{:S(2)}) collective-permute-start(bf16[8,5632]{1,0:T(8,128)(2,1)} %get-tuple-element.44), channel_id=1, source_target_pairs={{0,26},{2,24},{4,30},{6,28},{8,18},{10,16},{12,22},{14,20},{16,10}... | collective-permute-start | bytes 270344 | tf_op jit(solution)/shard_map/ppermute | solution.py:587
  59.5 16.8 %collective-permute-start.13 = (bf16[8,5632]{1,0:T(8,128)(2,1)}, bf16[8,5632]{1,0:T(8,128)(2,1)S(1)}, u32[]{:S(2)}, u32[]{:S(2)}) collective-permute-start(bf16[8,5632]{1,0:T(8,128)(2,1)} %get-tuple-element.45), channel_id=1, source_target_pairs={{0,28},{2,30},{4,24},{6,26},{8,20},{10,22},{12,16},{14,18},{16,12}... | collective-permute-start | bytes 270344 | tf_op jit(solution)/shard_map/ppermute | solution.py:587
  61.9 16.6 %collective-permute-start.14 = (bf16[8,5632]{1,0:T(8,128)(2,1)}, bf16[8,5632]{1,0:T(8,128)(2,1)S(1)}, u32[]{:S(2)}, u32[]{:S(2)}) collective-permute-start(bf16[8,5632]{1,0:T(8,128)(2,1)} %get-tuple-element.46), channel_id=1, source_target_pairs={{0,30},{2,28},{4,26},{6,24},{8,22},{10,20},{12,18},{14,16},{16,14}... | collective-permute-start | bytes 270344 | tf_op jit(solution)/shard_map/ppermute | solution.py:587
  78.5 0.9 copy-start.4
  84.4 17.6 %collective-permute-start.15 = (bf16[256,1408]{1,0:T(8,128)(2,1)S(1)}, bf16[256,1408]{1,0:T(8,128)(2,1)S(1)}, u32[]{:S(2)}, u32[]{:S(2)}) collective-permute-start(bf16[256,1408]{1,0:T(8,128)(2,1)S(1)} %bitcast.15), channel_id=1, source_target_pairs={{0,1},{1,0},{2,3},{3,2},{4,5},{5,4},{6,7},{7,6},{8,9},{9,8},{10,11... | collective-permute-start | bytes 2162696 | tf_op jit(solution)/shard_map/ppermute | solution.py:566
  85.7 4.5 %copy-start = (bf16[2,128,2816]{2,1,0:T(8,128)(2,1)S(1)}, bf16[2,128,2816]{2,1,0:T(8,128)(2,1)}, u32[]{:S(2)}) copy-start(bf16[2,128,2816]{2,1,0:T(8,128)(2,1)} %gate_ref.5) | copy-start | bytes 4325380
  85.7 4.5 %copy-start.1 = (bf16[2,128,2816]{2,1,0:T(8,128)(2,1)S(1)}, bf16[2,128,2816]{2,1,0:T(8,128)(2,1)}, u32[]{:S(2)}) copy-start(bf16[2,128,2816]{2,1,0:T(8,128)(2,1)} %up_ref.5) | copy-start | bytes 4325380
  85.7 4.5 %copy-start.3 = (s32[1,2688]{1,0:T(1,128)S(1)}, s32[1,2688]{1,0:T(1,128)}, u32[]{:S(2)}) copy-start(s32[1,2688]{1,0:T(1,128)} %get-tuple-element.50.far_ids_ref.ids_ref) | copy-start | bytes 32260

commit v3 on v2

--- a/solution.py
+++ b/solution.py
@@ -158,18 +158,44 @@
     ones = hit.astype(F32)
     before = (iota((lanes, lanes), 0) < iota((lanes, lanes), 1)).astype(F32).astype(BF16)
     above = (iota((lines, lines), 1) < iota((lines, lines), 0)).astype(F32).astype(BF16)
-    sums = jnp.broadcast_to(jnp.sum(ones, axis=1, keepdims=True), (lines, lanes))
-    total = jnp.dot(ones.astype(BF16), before, preferred_element_type=F32) + jnp.dot(
-        above, sums.astype(BF16), preferred_element_type=F32
-    )
-    return jnp.where(hit, total.astype(I32), -1)
+    count = jnp.sum(ones, axis=1, keepdims=True)
+    ahead = jnp.dot(
+        above, jnp.broadcast_to(count, (lines, lanes)).astype(BF16), preferred_element_type=F32
+    )[:, :1]
+    inside = jnp.dot(ones.astype(BF16), before, preferred_element_type=F32)
+    return jnp.where(hit, inside, -1.0), ahead, count
+
+
+def slot_columns(inside, ahead, count, within, width):
+    lines, _ = inside.shape
+    slot = iota((lines, width), 1).astype(F32)
+    chosen = (slot >= ahead) & (slot < ahead + count)
+    spread = chosen.astype(F32).astype(BF16)
+    first = jnp.sum(jnp.where(chosen, ahead, 0.0), axis=0, keepdims=True)
+    used = jnp.sum(chosen.astype(F32), axis=0, keepdims=True)
+    high = lax.div(within, jnp.full_like(within, 256))
+    low = within - high * 256
+
+    def over_slots(value):
+        return lax.dot_general(
+            value.astype(F32).astype(BF16),
+            spread,
+            (((0,), (0,)), ((), ())),
+            preferred_element_type=F32,
+        )
+
+    order = slot[:1] - first
+    hit = over_slots(inside) == order
+    column = jnp.sum(
+        jnp.where(hit, over_slots(high) * 256.0 + over_slots(low), 0.0), axis=0, keepdims=True
+    )
+    return jnp.where(used > 0.0, column, -1.0).astype(I32)
 
 
 def column_plan(narrow, map_ref, near_ref, send_ref, far_ref, splits):
     rank = lax.axis_index("mp")
     lines = map_ref.shape[0] // splits
     lanes = map_ref.shape[1]
-    width = send_ref.shape[1]
     blocks = [map_ref[split * lines : (split + 1) * lines, :] for split in range(splits)]
 
     def block_of(index):
@@ -186,22 +212,14 @@
     owner, within = block_of(rank)
     flatten(jnp.where(owner == rank, within, -1), near_ref, 0)
     for turn in range(1, splits):
-        flatten(
-            running_order(owner == lax.rem(rank + splits - turn, splits)), far_ref, turn - 1
+        hit = owner == lax.rem(rank + splits - turn, splits)
+        inside, ahead, _ = running_order(hit)
+        flatten(jnp.where(hit, inside + ahead, -1.0).astype(I32), far_ref, turn - 1)
+        their_owner, their_within = block_of(lax.rem(rank + turn, splits))
+        inside, ahead, count = running_order(their_owner == rank)
+        send_ref[turn - 1 : turn, :] = slot_columns(
+            inside, ahead, count, their_within, send_ref.shape[1]
         )
-        their_owner, their_within = block_of(lax.rem(rank + turn, splits))
-        key = running_order(their_owner == rank)
-        value = (their_within + 1).astype(F32)
-        for start in range(0, width, lanes):
-            slot = iota((lanes, lanes), 0) + start
-            held = jnp.zeros((lanes, lanes), F32)
-            for line in range(lines):
-                held = jnp.where(key[line : line + 1, :] == slot, value[line : line + 1, :], held)
-            column = jnp.sum(held, axis=1, keepdims=True)
-            diagonal = iota((lanes, lanes), 0) == iota((lanes, lanes), 1)
-            send_ref[turn - 1 : turn, start : start + lanes] = (
-                jnp.sum(jnp.where(diagonal, column, 0.0), axis=0, keepdims=True).astype(I32) - 1
-            )
 
 
 def middle_kernel(
@@ -279,7 +297,7 @@
 
 
 def arrive_kernel(land_ref, ids_ref, *refs):
-    *came_refs, rows_ref, out_ref, held_ref, sems = refs
+    *came_refs, rows_ref, gate_ref, up_ref, held_ref, sems = refs
     narrow = rows_ref.shape[1]
     rows = land_ref.shape[0]
     cap = came_refs[0].shape[0]
@@ -299,7 +317,9 @@
             preferred_element_type=F32,
         ).astype(BF16)
     for s in range(ids_ref.shape[0]):
-        out_ref[s] = onehot_dot(rows_ref, ids_ref[s : s + 1, :], narrow).astype(BF16)
+        picked = onehot_dot(rows_ref, ids_ref[s : s + 1, :], narrow).astype(BF16)
+        gate_ref[s] = picked[:rows]
+        up_ref[s] = picked[rows:]
 
 
 def arrive_rows(land, ids, came):
@@ -310,10 +330,11 @@
         arrive_kernel,
         out_shape=(
             jax.ShapeDtypeStruct((2 * rows, narrow), BF16),
-            jax.ShapeDtypeStruct((turns, 2 * rows, width), BF16),
+            jax.ShapeDtypeStruct((turns, rows, width), BF16),
+            jax.ShapeDtypeStruct((turns, rows, width), BF16),
         ),
         in_specs=[VMEM, VMEM] + [HBM] * len(came),
-        out_specs=(VMEM,) * 2,
+        out_specs=(VMEM,) * 3,
         scratch_shapes=[
             pltpu.VMEM((slots, 2 * narrow), BF16),
             pltpu.SemaphoreType.DMA((len(came),)),
@@ -446,46 +467,44 @@
 
 
 def second_kernel(
-    rows_ref, near_ref, far_ref, ids_ref, gate_in, up_in, gate_out, up_out,
-    held_ref, base_sems, sems,
+    rows_ref, near_ref, far_ref, ids_ref, old_ref, out_ref, held_ref, base_sem, sems
 ):
-    rows, narrow = rows_ref.shape[0] // 2, rows_ref.shape[1]
-    outs = (gate_out, up_out)
-    layers = gate_out.shape[0]
-    copies = []
-    for side, out in enumerate(outs):
-        copies.append(
-            pltpu.make_async_copy(
-                rows_ref.at[pl.ds(side * rows, rows), :],
-                out.at[layers - 1, 1, :, pl.ds(0, narrow)],
-                base_sems.at[side],
-            )
-        )
-        copies[-1].start()
+    narrow = rows_ref.shape[1]
+    layers = out_ref.shape[0]
+    copies = [
+        pltpu.make_async_copy(rows_ref, out_ref.at[layers - 1, 1, :, pl.ds(0, narrow)], base_sem)
+    ]
+    copies[0].start()
 
     def near(start, size):
         return near_ref[:, start : start + size].astype(F32)
 
-    copies += put_extras(1, narrow, near, far_ref, ids_ref, outs, held_ref, sems)
+    copies += put_extras(1, narrow, near, far_ref, ids_ref, (out_ref,), held_ref, sems)
     for copy in copies:
         copy.wait()
 
 
-def second_half(rows, near, far, ids, gate_out, up_out):
-    count, narrow = rows.shape
+def second_half(rows, near, far, ids, out, side):
+    count, narrow = rows.shape[0] // 2, rows.shape[1]
     extra = near.shape[1]
-    layers = gate_out.shape[0]
-    out_type = jax.ShapeDtypeStruct(gate_out.shape, BF16)
+    layers = out.shape[0]
     return pl.pallas_call(
         second_kernel,
-        out_shape=(out_type, out_type),
-        in_specs=[VMEM] * 4 + [HBM] * 2,
-        out_specs=(HBM, HBM),
-        input_output_aliases={4: 0, 5: 1},
+        out_shape=jax.ShapeDtypeStruct(out.shape, BF16),
+        grid=(1,),
+        in_specs=[
+            pl.BlockSpec((count, narrow), lambda i: (side, 0)),
+            pl.BlockSpec((count, extra), lambda i: (side, 0)),
+            pl.BlockSpec(far.shape, lambda i: (0, 0, 0)),
+            pl.BlockSpec(ids.shape, lambda i: (0, 0)),
+            HBM,
+        ],
+        out_specs=HBM,
+        input_output_aliases={4: 0},
         scratch_shapes=[
             pltpu.VMEM((count, extra), BF16),
-            pltpu.SemaphoreType.DMA((2,)),
-            pltpu.SemaphoreType.DMA((len(column_tiles(extra)), layers, 2)),
+            pltpu.SemaphoreType.DMA(()),
+            pltpu.SemaphoreType.DMA((len(column_tiles(extra)), layers, 1)),
         ],
         compiler_params=PARAMS,
         cost_estimate=pl.CostEstimate(
@@ -493,39 +512,25 @@
             bytes_accessed=4 * count * (narrow + layers * extra),
             transcendentals=0,
         ),
-        name="second_half",
-    )(rows, near, far, ids, gate_out, up_out)
-
-
-def last_kernel(
-    land_ref, came_ref, gate_in, up_in, gate_out, up_out, in_ref, held_ref, in_sems, out_sems
-):
+    )(rows, near, far, ids, out)
+
+
+def last_kernel(land_ref, came_ref, gate_in, up_in, gate_out, up_out, held_ref, sems):
     narrow = came_ref.shape[1] // 2
-    steps = in_sems.shape[1]
+    steps = sems.shape[1]
     width = narrow // steps
-    loads, stores = [], []
-    for number in range(2 * steps):
-        columns = pl.ds(number * width, width)
-        loads.append(
-            pltpu.make_async_copy(
-                came_ref.at[:, columns],
-                in_ref.at[:, columns],
-                in_sems.at[number // steps, number % steps],
-            )
-        )
-        loads[-1].start()
+    stores = []
     for side, out in enumerate((gate_out, up_out)):
         for step in range(steps):
             at = side * narrow + step * width
-            loads[side * steps + step].wait()
             held_ref[:, at : at + width] = jnp.dot(
-                land_ref[...], in_ref[:, at : at + width], preferred_element_type=F32
+                land_ref[...], came_ref[:, at : at + width], preferred_element_type=F32
             ).astype(BF16)
             stores.append(
                 pltpu.make_async_copy(
                     held_ref.at[:, pl.ds(at, width)],
                     out.at[0, 1, :, pl.ds(step * width, width)],
-                    out_sems.at[side, step],
+                    sems.at[side, step],
                 )
             )
             stores[-1].start()
@@ -541,13 +546,11 @@
     return pl.pallas_call(
         last_kernel,
         out_shape=(out_type, out_type),
-        in_specs=[VMEM] + [HBM] * 3,
+        in_specs=[VMEM] * 2 + [HBM] * 2,
         out_specs=(HBM, HBM),
         input_output_aliases={2: 0, 3: 1},
         scratch_shapes=[
-            pltpu.VMEM((slots, 2 * narrow), BF16),
             pltpu.VMEM((rows, 2 * narrow), BF16),
-            pltpu.SemaphoreType.DMA((2, steps)),
             pltpu.SemaphoreType.DMA((2, steps)),
         ],
         compiler_params=PARAMS,
@@ -595,11 +598,14 @@
     own_far = turn_around(own_sent, splits)
     came_low = swap_rows(sent_low)
     land = land_rows(table, cap)
-    got, got_sent = arrive_rows(land, send_ids, came_top)
-    got_far = turn_around(got_sent, splits)
+    got, *got_sent = arrive_rows(land, send_ids, came_top)
+    got_far = [turn_around(got_sent[side], splits) for side in range(2)]
     outs = first_half(table, near_ids, own_far, far_ids, gate_weight, up_weight, out_type)
     got_near = near_columns(got, near_ids)
-    outs = second_half(got, got_near, got_far, far_ids, *outs)
+    outs = [
+        second_half(got, got_near, got_far[side], far_ids, outs[side], side)
+        for side in range(2)
+    ]
     return last_rows(land, came_low, *outs)
 
 

time: 109 us -> 110 us (level)
    pallas_call x1 -> x2, Pallas kernels: 3.83 us -> 4.57 us  [second_half(): pl.pallas_call(second_kernel, out_shape=jax.ShapeDtypeStruct(out.shape, B...]
    ppermute x2 -> x3, waiting for transfers between devices: 2.29 us -> 2.02 us  [turn_around(): lax.ppermute(sent[turn - 1], 'mp', [(i, (i + turn) % splits) for i in ran...]
    ppermute x2 -> x3, starting transfers between devices: 2.48 us -> 2.74 us  [turn_around(): lax.ppermute(sent[turn - 1], 'mp', [(i, (i + turn) % splits) for i in ran...]
  transfers between devices with their start and end apart: 18 -> 19, of which waited for: 12 -> 12; matrix products, arithmetic and copies ran while one was open for 0% -> 0% of each run, Pallas kernels for 24% -> 25%
where the time goes in v3:
time: 110 us; the launch traced here: 108 us
  starting transfers between devices  37.1 us (34%)
  Pallas kernels  34.9 us (32%)
  waiting for transfers between devices  34.3 us (31%)
    ppermute x15, waiting for transfers between devices, cross(): return lax.ppermute(sent, 'section', [(i, i ^ p) for i in range(blocks)])  32.2 us
    ppermute x15, starting transfers between devices, cross(): return lax.ppermute(sent, 'section', [(i, i ^ p) for i in range(blocks)])  27.7 us
    pallas_call x1, Pallas kernels, first_half(): pl.pallas_call(first_kernel, out_shape=(out_type, out_type), in_specs=[VM...  9.54 us
    all_to_all x1, starting transfers between devices, swap_rows(): lax.all_to_all(sent, 'section', split_axis=0, concat_axis=0, tiled=True)  6.67 us
    pallas_call x1, Pallas kernels, middle(): pl.pallas_call(functools.partial(middle_kernel, cap, splits), out_shape=(...  6.56 us
    pallas_call x1, Pallas kernels, arrive_rows(): pl.pallas_call(arrive_kernel, out_shape=(jax.ShapeDtypeStruct((2 * rows,...  4.94 us
    pallas_call x2, Pallas kernels, second_half(): pl.pallas_call(second_kernel, out_shape=jax.ShapeDtypeStruct(out.shape, B...  4.57 us
    pallas_call x1, Pallas kernels, near_columns(): pl.pallas_call(near_kernel, out_shape=jax.ShapeDtypeStruct((count, extra)...  4.49 us
  transfers between devices with their start and end apart: 19, of which 12 were waited for; matrix products, arithmetic and copies ran while one was open for 0% of the time, Pallas kernels for 25%

profile of v3, /device:TPU:13, one launch (start us, length us, event | category | flops | bytes accessed | tf_op | source)
XLA Modules:
  0.0 108.2 jit_solution(536104962528559268)
XLA Ops:
  0.6 0.0 copy-start.3
  0.6 6.6 %middle.1 = (bf16[1,256,1408]{2,1,0:T(8,128)(2,1)}, s32[1,2688]{1,0:T(1,128)}, s32[1,1408]{1,0:T(1,128)}, s32[1,2688]{1,0:T(1,128)}, bf16[128,5632]{1,0:T(8,128)(2,1)}) custom-call(s32[16,128]{1,0:T(8,128)} %bitcast.13, s32[42,128]{1,0:T(8,128)} %bitcast.22, bf16[2,128,2816]{2,1,0:T(8,128)(2,1)} %gate_ref.5, bf16[2,128,2816]{2,1,0:T(8,128)(2,1)} %up_ref.5), custom_call_target="tpu_custom_call" | custom-call | flops 2030043136 | bytes 5767168 | tf_op jit(solution)/shard_map/middle/pallas_call | solution.py:253
  7.2 0.0 copy-start.7
  7.2 0.0 copy-start.6
  7.2 6.7 %all-to-all-start = ((bf16[16,8,5632]{2,1,0:T(8,128)(2,1)}), bf16[16,8,5632]{2,1,0:T(8,128)(2,1)S(1)}, u32[]{:S(2)}, u32[]{:S(2)}) async-start(bf16[16,8,5632]{2,1,0:T(8,128)(2,1)} %bitcast.20), calls=%async_computation | async-start | bytes 2883584 | tf_op jit(solution)/shard_map/all_to_all | solution.py:587
  13.9 0.0 copy-start.5
  13.9 3.2 %send_rows.1 = (bf16[8,5632]{1,0:T(8,128)(2,1)}, bf16[8,5632]{1,0:T(8,128)(2,1)}, bf16[8,5632]{1,0:T(8,128)(2,1)}, bf16[8,5632]{1,0:T(8,128)(2,1)}, bf16[8,5632]...) custom-call(s32[16,128]{1,0:T(8,128)} %bitcast.14, ...), custom_call_target="tpu_custom_call" | custom-call | flops 184549376 | bytes 2883584 | tf_op jit(solution)/shard_map/send_rows/pallas_call | solution.py:132
  17.1 0.5 collective-permute-start
  17.6 0.3 collective-permute-start.1
  17.9 1.5 %collective-permute-start.2 = (bf16[8,5632]{1,0:T(8,128)(2,1)}, bf16[8,5632]{1,0:T(8,128)(2,1)S(1)}, u32[]{:S(2)}, u32[]{:S(2)}) collective-permute-start(bf16[8,5632]{1,0:T(8,128)(2,1)} %get-tuple-element.33), channel_id=1, source_target_pairs={{0,6},{2,4},{4,2},{6,0},{8,14},{10,12},{12,10},{14,8},{16,22},{18,... | collective-permute-start | bytes 270344 | tf_op jit(solution)/shard_map/ppermute | solution.py:590
  19.3 0.3 collective-permute-start.3
  19.6 1.5 %collective-permute-start.4 = (bf16[8,5632]{1,0:T(8,128)(2,1)}, bf16[8,5632]{1,0:T(8,128)(2,1)S(1)}, u32[]{:S(2)}, u32[]{:S(2)}) collective-permute-start(bf16[8,5632]{1,0:T(8,128)(2,1)} %get-tuple-element.35), channel_id=1, source_target_pairs={{0,10},{2,8},{4,14},{6,12},{8,2},{10,0},{12,6},{14,4},{16,26},{18,... | collective-permute-start | bytes 270344 | tf_op jit(solution)/shard_map/ppermute | solution.py:590
  21.1 0.0 collective-permute-done.refs_1_
  21.1 0.0 collective-permute-start.5
  21.1 1.7 %collective-permute-done.1.refs_2_ = bf16[8,5632]{1,0:T(8,128)(2,1)S(1)} collective-permute-done((bf16[8,5632]{1,0:T(8,128)(2,1)}, bf16[8,5632]{1,0:T(8,128)(2,1)S(1)}, u32[]{:S(2)}, u32[]{:S(2)}) %collective-permute-start.1) | collective-permute-done | bytes 90144 | tf_op jit(solution)/shard_map/ppermute | solution.py:590
  22.8 5.7 %collective-permute-start.6 = (bf16[8,5632]{1,0:T(8,128)(2,1)}, bf16[8,5632]{1,0:T(8,128)(2,1)S(1)}, u32[]{:S(2)}, u32[]{:S(2)}) collective-permute-start(bf16[8,5632]{1,0:T(8,128)(2,1)} %get-tuple-element.37), channel_id=1, source_target_pairs={{0,14},{2,12},{4,10},{6,8},{8,6},{10,4},{12,2},{14,0},{16,30},{18,... | collective-permute-start | bytes 270344 | tf_op jit(solution)/shard_map/ppermute | solution.py:590
  28.5 0.0 collective-permute-done.2.refs_3_
  28.5 2.7 %collective-permute-start.7 = (bf16[8,5632]{1,0:T(8,128)(2,1)}, bf16[8,5632]{1,0:T(8,128)(2,1)S(1)}, u32[]{:S(2)}, u32[]{:S(2)}) collective-permute-start(bf16[8,5632]{1,0:T(8,128)(2,1)} %get-tuple-element.38), channel_id=1, source_target_pairs={{0,16},{2,18},{4,20},{6,22},{8,24},{10,26},{12,28},{14,30},{16,0},... | collective-permute-start | bytes 270344 | tf_op jit(solution)/shard_map/ppermute | solution.py:590
  31.2 9.1 %collective-permute-done.3.refs_4_ = bf16[8,5632]{1,0:T(8,128)(2,1)S(1)} collective-permute-done((bf16[8,5632]{1,0:T(8,128)(2,1)}, bf16[8,5632]{1,0:T(8,128)(2,1)S(1)}, u32[]{:S(2)}, u32[]{:S(2)}) %collective-permute-start.3) | collective-permute-done | bytes 90144 | tf_op jit(solution)/shard_map/ppermute | solution.py:590
  40.3 2.6 %collective-permute-start.8 = (bf16[8,5632]{1,0:T(8,128)(2,1)}, bf16[8,5632]{1,0:T(8,128)(2,1)S(1)}, u32[]{:S(2)}, u32[]{:S(2)}) collective-permute-start(bf16[8,5632]{1,0:T(8,128)(2,1)} %get-tuple-element.39), channel_id=1, source_target_pairs={{0,18},{2,16},{4,22},{6,20},{8,26},{10,24},{12,30},{14,28},{16,2},... | collective-permute-start | bytes 270344 | tf_op jit(solution)/shard_map/ppermute | solution.py:590
  42.9 0.5 collective-permute-done.4.refs_5_
  43.4 0.3 collective-permute-start.9
  43.7 0.8 collective-permute-done.5.refs_6_
  44.5 3.8 %collective-permute-start.10 = (bf16[8,5632]{1,0:T(8,128)(2,1)}, bf16[8,5632]{1,0:T(8,128)(2,1)S(1)}, u32[]{:S(2)}, u32[]{:S(2)}) collective-permute-start(bf16[8,5632]{1,0:T(8,128)(2,1)} %get-tuple-element.41), channel_id=1, source_target_pairs={{0,22},{2,20},{4,18},{6,16},{8,30},{10,28},{12,26},{14,24},{16,6},... | collective-permute-start | bytes 270344 | tf_op jit(solution)/shard_map/ppermute | solution.py:590
  48.3 0.0 collective-permute-done.6.refs_7_
  48.3 0.0 copy-done.7
  48.3 1.2 %collective-permute-start.16 = (bf16[256,1408]{1,0:T(8,128)(2,1)S(1)}, bf16[256,1408]{1,0:T(8,128)(2,1)S(1)}, u32[]{:S(2)}, u32[]{:S(2)}) collective-permute-start(bf16[256,1408]{1,0:T(8,128)(2,1)S(1)} %bitcast.21), channel_id=1, source_target_pairs={{0,1},{1,0},{2,3},{3,2},{4,5},{5,4},{6,7},{7,6},{8,9},{9,8},{10,11... | collective-permute-start | bytes 2162696 | tf_op jit(solution)/shard_map/ppermute | solution.py:569
  49.5 1.7 %collective-permute-done.7.refs_8_ = bf16[8,5632]{1,0:T(8,128)(2,1)S(1)} collective-permute-done((bf16[8,5632]{1,0:T(8,128)(2,1)}, bf16[8,5632]{1,0:T(8,128)(2,1)S(1)}, u32[]{:S(2)}, u32[]{:S(2)}) %collective-permute-start.7) | collective-permute-done | bytes 90144 | tf_op jit(solution)/shard_map/ppermute | solution.py:590
  51.2 0.0 collective-permute-start.11
  51.2 5.8 %collective-permute-done.8.refs_9_ = bf16[8,5632]{1,0:T(8,128)(2,1)S(1)} collective-permute-done((bf16[8,5632]{1,0:T(8,128)(2,1)}, bf16[8,5632]{1,0:T(8,128)(2,1)S(1)}, u32[]{:S(2)}, u32[]{:S(2)}) %collective-permute-start.8) | collective-permute-done | bytes 90144 | tf_op jit(solution)/shard_map/ppermute | solution.py:590
  57.0 2.4 %collective-permute-start.12 = (bf16[8,5632]{1,0:T(8,128)(2,1)}, bf16[8,5632]{1,0:T(8,128)(2,1)S(1)}, u32[]{:S(2)}, u32[]{:S(2)}) collective-permute-start(bf16[8,5632]{1,0:T(8,128)(2,1)} %get-tuple-element.43), channel_id=1, source_target_pairs={{0,26},{2,24},{4,30},{6,28},{8,18},{10,16},{12,22},{14,20},{16,10}... | collective-permute-start | bytes 270344 | tf_op jit(solution)/shard_map/ppermute | solution.py:590
  59.5 0.0 collective-permute-done.9.refs_10_
  59.5 0.7 collective-permute-start.13
  60.2 1.6 %collective-permute-done.10.refs_11_ = bf16[8,5632]{1,0:T(8,128)(2,1)S(1)} collective-permute-done((bf16[8,5632]{1,0:T(8,128)(2,1)}, bf16[8,5632]{1,0:T(8,128)(2,1)S(1)}, u32[]{:S(2)}, u32[]{:S(2)}) %collective-permute-start.10) | collective-permute-done | bytes 90144 | tf_op jit(solution)/shard_map/ppermute | solution.py:590
  61.8 5.5 %collective-permute-start.14 = (bf16[8,5632]{1,0:T(8,128)(2,1)}, bf16[8,5632]{1,0:T(8,128)(2,1)S(1)}, u32[]{:S(2)}, u32[]{:S(2)}) collective-permute-start(bf16[8,5632]{1,0:T(8,128)(2,1)} %get-tuple-element.45), channel_id=1, source_target_pairs={{0,30},{2,28},{4,26},{6,24},{8,22},{10,20},{12,18},{14,16},{16,14}... | collective-permute-start | bytes 270344 | tf_op jit(solution)/shard_map/ppermute | solution.py:590
  67.3 0.0 copy-done.3
  67.3 0.2 land_rows.1.land_ref
  67.5 3.8 %collective-permute-done.11.refs_12_ = bf16[8,5632]{1,0:T(8,128)(2,1)S(1)} collective-permute-done((bf16[8,5632]{1,0:T(8,128)(2,1)}, bf16[8,5632]{1,0:T(8,128)(2,1)S(1)}, u32[]{:S(2)}, u32[]{:S(2)}) %collective-permute-start.11) | collective-permute-done | bytes 90144 | tf_op jit(solution)/shard_map/ppermute | solution.py:590
  71.3 2.8 %collective-permute-done.12.refs_13_ = bf16[8,5632]{1,0:T(8,128)(2,1)S(1)} collective-permute-done((bf16[8,5632]{1,0:T(8,128)(2,1)}, bf16[8,5632]{1,0:T(8,128)(2,1)S(1)}, u32[]{:S(2)}, u32[]{:S(2)}) %collective-permute-start.12) | collective-permute-done | bytes 90144 | tf_op jit(solution)/shard_map/ppermute | solution.py:590
  74.1 2.2 %collective-permute-done.13.refs_14_ = bf16[8,5632]{1,0:T(8,128)(2,1)S(1)} collective-permute-done((bf16[8,5632]{1,0:T(8,128)(2,1)}, bf16[8,5632]{1,0:T(8,128)(2,1)S(1)}, u32[]{:S(2)}, u32[]{:S(2)}) %collective-permute-start.13) | collective-permute-done | bytes 90144 | tf_op jit(solution)/shard_map/ppermute | solution.py:590
  76.3 2.2 %collective-permute-done.14.refs_15_ = bf16[8,5632]{1,0:T(8,128)(2,1)S(1)} collective-permute-done((bf16[8,5632]{1,0:T(8,128)(2,1)}, bf16[8,5632]{1,0:T(8,128)(2,1)S(1)}, u32[]{:S(2)}, u32[]{:S(2)}) %collective-permute-start.14) | collective-permute-done | bytes 90144 | tf_op jit(solution)/shard_map/ppermute | solution.py:590
  78.5 0.0 copy-done.6
  78.5 0.0 copy-start.4
  78.5 0.9 copy-done.4
  79.4 4.9 %arrive_rows.1 = (bf16[256,2816]{1,0:T(8,128)(2,1)S(1)}, bf16[1,128,1408]{2,1,0:T(8,128)(2,1)S(1)}, bf16[1,128,1408]{2,1,0:T(8,128)(2,1)S(1)}) custom-call(bf16[128,128]{1,0:T(8,128)(2,1)S(1)} %land_rows.1.land_ref, s32[1,1408]{1,0:T(1,128)S(1)} %copy-done.6, bf16[8,5632]{1,0:T(8,128)(2,1)S(1)} %copy-done.4, ...), custom_call_target="tpu_custom_call" | custom-call | flops 2030043136 | bytes 2883584 | tf_op jit(solution)/shard_map/arrive_rows/pallas_call | solution.py:329
  84.3 1.3 %collective-permute-start.17 = (bf16[128,1408]{1,0:T(8,128)(2,1)S(1)}, bf16[128,1408]{1,0:T(8,128)(2,1)S(1)}, u32[]{:S(2)}, u32[]{:S(2)}) collective-permute-start(bf16[128,1408]{1,0:T(8,128)(2,1)S(1)} %bitcast.18), channel_id=1, source_target_pairs={{0,1},{1,0},{2,3},{3,2},{4,5},{5,4},{6,7},{7,6},{8,9},{9,8},{10,11... | collective-permute-start | bytes 1081352 | tf_op jit(solution)/shard_map/ppermute | solution.py:569
  85.6 0.3 collective-permute-start.15
  85.9 0.0 copy-done.5
  85.9 0.0 copy-start
  85.9 0.0 copy-start.1
  85.9 0.0 copy-start.2
  85.9 4.5 %shard_map.59.near_ref = bf16[256,2688]{1,0:T(8,128)(2,1)S(1)} custom-call(bf16[256,2816]{1,0:T(8,128)(2,1)S(1)} %get-tuple-element.46.rows_ref, s32[1,2688]{1,0:T(1,128)S(1)} %copy-done.5), custom_call_target="tpu_custom_call" | custom-call | flops 3875536896 | bytes 2818048 | tf_op jit(solution)/shard_map/pallas_call | solution.py:362
  90.4 0.0 collective-permute-done.16
  90.4 0.0 copy-done
  90.4 0.0 copy-done.1
  90.4 0.0 copy-done.2
  90.4 9.5 %first_half.1 = (bf16[2,2,128,5504]{3,2,1,0:T(8,128)(2,1)}, bf16[2,2,128,5504]{3,2,1,0:T(8,128)(2,1)}) custom-call(s32[16,128]{1,0:T(8,128)S(1)} %bitcast.16, s32[1,2688]{1,0:T(1,128)S(1)} %copy-done.5, bf16[1,256,1408]{2,1,0:T(8,128)(2,1)S(1)} %bitcast.17, s32[1,2688]{1,0:T(1,128)S(1)} %copy-done.2, bf16[2,128,2816]{2,1,0:T(8,128)(2,1)S(1)} %copy-done, ...), custom_call_target="tpu_custom_call" | custom-call | flops 5813305344 | bytes 11272192 | tf_op jit(solution)/shard_map/first_half/pallas_call | solution.py:446
  100.0 2.0 %collective-permute-done.15 = bf16[128,1408]{1,0:T(8,128)(2,1)S(1)} collective-permute-done((bf16[128,1408]{1,0:T(8,128)(2,1)S(1)}, bf16[128,1408]{1,0:T(8,128)(2,1)S(1)}, u32[]{:S(2)}, u32[]{:S(2)}) %collective-permute-start.15) | collective-permute-done | bytes 360480 | tf_op jit(solution)/shard_map/ppermute | solution.py:569
  102.0 2.3 %shard_map.60.gate_in = bf16[2,2,128,5504]{3,2,1,0:T(8,128)(2,1)} custom-call(bf16[256,2816]{1,0:T(8,128)(2,1)S(1)} %get-tuple-element.46.rows_ref, bf16[256,2688]{1,0:T(8,128)(2,1)S(1)} %shard_map.59.near_ref, bf16[1,128,1408]{2,1,0:T(8,128)(2,1)S(1)} %bitcast.12, s32[1,2688]{1,0:T(1,128)S(1)} %copy-done.2, ...), custom_call_target="tpu_custom_call", output_to_operand_aliasing={{}: (4, {})} | custom-call | flops 968884224 | bytes 4194304 | tf_op jit(solution)/shard_map/pallas_call | solution.py:491
  104.3 0.0 collective-permute-done.17
  104.3 2.3 %shard_map.61.up_in = bf16[2,2,128,5504]{3,2,1,0:T(8,128)(2,1)} custom-call(bf16[256,2816]{1,0:T(8,128)(2,1)S(1)} %get-tuple-element.46.rows_ref, bf16[256,2688]{1,0:T(8,128)(2,1)S(1)} %shard_map.59.near_ref, bf16[1,128,1408]{2,1,0:T(8,128)(2,1)S(1)} %bitcast.11, s32[1,2688]{1,0:T(1,128)S(1)} %copy-done.2, ...), custom_call_target="tpu_custom_call", output_to_operand_aliasing={{}: (4, {})} | custom-call | flops 968884224 | bytes 4194304 | tf_op jit(solution)/shard_map/pallas_call | solution.py:491
  106.6 0.0 all-to-all-done
  106.6 1.4 %last_rows.1 = (bf16[2,2,128,5504]{3,2,1,0:T(8,128)(2,1)}, bf16[2,2,128,5504]{3,2,1,0:T(8,128)(2,1)}) custom-call(bf16[128,128]{1,0:T(8,128)(2,1)S(1)} %land_rows.1.land_ref, bf16[128,5632]{1,0:T(8,128)(2,1)S(1)} %bitcast.10, bf16[2,2,128,5504]{3,2,1,0:T(8,128)(2,1)} %shard_map.60.gate_in, ...), custom_call_target="tpu_custom_call", output_to_operand_aliasing={{0}: (2, {}), {1}: (3, {})} | custom-call | flops 184549376 | bytes 2883584 | tf_op jit(solution)/shard_map/last_rows/pallas_call | solution.py:546
Async XLA Ops:
  0.6 66.7 %copy-start.3 = (s32[2048]{0:T(1024)S(1)}, s32[2048]{0:T(1024)}, u32[]{:S(2)}) copy-start(s32[2048]{0:T(1024)} %param.6) | copy-start | bytes 24580
  7.2 41.1 %copy-start.7 = (bf16[1,256,1408]{2,1,0:T(8,128)(2,1)S(1)}, bf16[1,256,1408]{2,1,0:T(8,128)(2,1)}, u32[]{:S(2)}) copy-start(bf16[1,256,1408]{2,1,0:T(8,128)(2,1)} %get-tuple-element.50) | copy-start | bytes 2162692
  7.2 71.3 %copy-start.6 = (s32[1,1408]{1,0:T(1,128)S(1)}, s32[1,1408]{1,0:T(1,128)}, u32[]{:S(2)}) copy-start(s32[1,1408]{1,0:T(1,128)} %get-tuple-element.29.ids_ref) | copy-start | bytes 16900
  7.2 99.4 %all-to-all-start = ((bf16[16,8,5632]{2,1,0:T(8,128)(2,1)}), bf16[16,8,5632]{2,1,0:T(8,128)(2,1)S(1)}, u32[]{:S(2)}, u32[]{:S(2)}) async-start(bf16[16,8,5632]{2,1,0:T(8,128)(2,1)} %bitcast.20), calls=%async_computation | async-start | bytes 2883584 | tf_op jit(solution)/shard_map/all_to_all | solution.py:587
  13.9 72.0 %copy-start.5 = (s32[1,2688]{1,0:T(1,128)S(1)}, s32[1,2688]{1,0:T(1,128)}, u32[]{:S(2)}) copy-start(s32[1,2688]{1,0:T(1,128)} %get-tuple-element.47.ids_ref.near_ids_ref) | copy-start | bytes 32260
  17.1 4.0 %collective-permute-start = (bf16[8,5632]{1,0:T(8,128)(2,1)}, bf16[8,5632]{1,0:T(8,128)(2,1)S(1)}, u32[]{:S(2)}, u32[]{:S(2)}) collective-permute-start(bf16[8,5632]{1,0:T(8,128)(2,1)} %get-tuple-element.31), channel_id=1, source_target_pairs={{0,2},{2,0},{4,6},{6,4},{8,10},{10,8},{12,14},{14,12},{16,18},{18,... | collective-permute-start | bytes 270344 | tf_op jit(solution)/shard_map/ppermute | solution.py:590
  17.6 5.2 %collective-permute-start.1 = (bf16[8,5632]{1,0:T(8,128)(2,1)}, bf16[8,5632]{1,0:T(8,128)(2,1)S(1)}, u32[]{:S(2)}, u32[]{:S(2)}) collective-permute-start(bf16[8,5632]{1,0:T(8,128)(2,1)} %get-tuple-element.32), channel_id=1, source_target_pairs={{0,4},{2,6},{4,0},{6,2},{8,12},{10,14},{12,8},{14,10},{16,20},{18,... | collective-permute-start | bytes 270344 | tf_op jit(solution)/shard_map/ppermute | solution.py:590
  17.9 10.6 %collective-permute-start.2 = (bf16[8,5632]{1,0:T(8,128)(2,1)}, bf16[8,5632]{1,0:T(8,128)(2,1)S(1)}, u32[]{:S(2)}, u32[]{:S(2)}) collective-permute-start(bf16[8,5632]{1,0:T(8,128)(2,1)} %get-tuple-element.33), channel_id=1, source_target_pairs={{0,6},{2,4},{4,2},{6,0},{8,14},{10,12},{12,10},{14,8},{16,22},{18,... | collective-permute-start | bytes 270344 | tf_op jit(solution)/shard_map/ppermute | solution.py:590
  19.3 21.0 %collective-permute-start.3 = (bf16[8,5632]{1,0:T(8,128)(2,1)}, bf16[8,5632]{1,0:T(8,128)(2,1)S(1)}, u32[]{:S(2)}, u32[]{:S(2)}) collective-permute-start(bf16[8,5632]{1,0:T(8,128)(2,1)} %get-tuple-element.34), channel_id=1, source_target_pairs={{0,8},{2,10},{4,12},{6,14},{8,0},{10,2},{12,4},{14,6},{16,24},{18,... | collective-permute-start | bytes 270344 | tf_op jit(solution)/shard_map/ppermute | solution.py:590
  19.6 23.8 %collective-permute-start.4 = (bf16[8,5632]{1,0:T(8,128)(2,1)}, bf16[8,5632]{1,0:T(8,128)(2,1)S(1)}, u32[]{:S(2)}, u32[]{:S(2)}) collective-permute-start(bf16[8,5632]{1,0:T(8,128)(2,1)} %get-tuple-element.35), channel_id=1, source_target_pairs={{0,10},{2,8},{4,14},{6,12},{8,2},{10,0},{12,6},{14,4},{16,26},{18,... | collective-permute-start | bytes 270344 | tf_op jit(solution)/shard_map/ppermute | solution.py:590
  21.1 23.4 %collective-permute-start.5 = (bf16[8,5632]{1,0:T(8,128)(2,1)}, bf16[8,5632]{1,0:T(8,128)(2,1)S(1)}, u32[]{:S(2)}, u32[]{:S(2)}) collective-permute-start(bf16[8,5632]{1,0:T(8,128)(2,1)} %get-tuple-element.36), channel_id=1, source_target_pairs={{0,12},{2,14},{4,8},{6,10},{8,4},{10,6},{12,0},{14,2},{16,28},{18,... | collective-permute-start | bytes 270344 | tf_op jit(solution)/shard_map/ppermute | solution.py:590
  22.8 25.5 %collective-permute-start.6 = (bf16[8,5632]{1,0:T(8,128)(2,1)}, bf16[8,5632]{1,0:T(8,128)(2,1)S(1)}, u32[]{:S(2)}, u32[]{:S(2)}) collective-permute-start(bf16[8,5632]{1,0:T(8,128)(2,1)} %get-tuple-element.37), channel_id=1, source_target_pairs={{0,14},{2,12},{4,10},{6,8},{8,6},{10,4},{12,2},{14,0},{16,30},{18,... | collective-permute-start | bytes 270344 | tf_op jit(solution)/shard_map/ppermute | solution.py:590
  28.5 22.7 %collective-permute-start.7 = (bf16[8,5632]{1,0:T(8,128)(2,1)}, bf16[8,5632]{1,0:T(8,128)(2,1)S(1)}, u32[]{:S(2)}, u32[]{:S(2)}) collective-permute-start(bf16[8,5632]{1,0:T(8,128)(2,1)} %get-tuple-element.38), channel_id=1, source_target_pairs={{0,16},{2,18},{4,20},{6,22},{8,24},{10,26},{12,28},{14,30},{16,0},... | collective-permute-start | bytes 270344 | tf_op jit(solution)/shard_map/ppermute | solution.py:590
  40.3 16.7 %collective-permute-start.8 = (bf16[8,5632]{1,0:T(8,128)(2,1)}, bf16[8,5632]{1,0:T(8,128)(2,1)S(1)}, u32[]{:S(2)}, u32[]{:S(2)}) collective-permute-start(bf16[8,5632]{1,0:T(8,128)(2,1)} %get-tuple-element.39), channel_id=1, source_target_pairs={{0,18},{2,16},{4,22},{6,20},{8,26},{10,24},{12,30},{14,28},{16,2},... | collective-permute-start | bytes 270344 | tf_op jit(solution)/shard_map/ppermute | solution.py:590
  43.4 16.0 %collective-permute-start.9 = (bf16[8,5632]{1,0:T(8,128)(2,1)}, bf16[8,5632]{1,0:T(8,128)(2,1)S(1)}, u32[]{:S(2)}, u32[]{:S(2)}) collective-permute-start(bf16[8,5632]{1,0:T(8,128)(2,1)} %get-tuple-element.40), channel_id=1, source_target_pairs={{0,20},{2,22},{4,16},{6,18},{8,28},{10,30},{12,24},{14,26},{16,4},... | collective-permute-start | bytes 270344 | tf_op jit(solution)/shard_map/ppermute | solution.py:590
  44.5 17.3 %collective-permute-start.10 = (bf16[8,5632]{1,0:T(8,128)(2,1)}, bf16[8,5632]{1,0:T(8,128)(2,1)S(1)}, u32[]{:S(2)}, u32[]{:S(2)}) collective-permute-start(bf16[8,5632]{1,0:T(8,128)(2,1)} %get-tuple-element.41), channel_id=1, source_target_pairs={{0,22},{2,20},{4,18},{6,16},{8,30},{10,28},{12,26},{14,24},{16,6},... | collective-permute-start | bytes 270344 | tf_op jit(solution)/shard_map/ppermute | solution.py:590
  48.3 42.1 %collective-permute-start.16 = (bf16[256,1408]{1,0:T(8,128)(2,1)S(1)}, bf16[256,1408]{1,0:T(8,128)(2,1)S(1)}, u32[]{:S(2)}, u32[]{:S(2)}) collective-permute-start(bf16[256,1408]{1,0:T(8,128)(2,1)S(1)} %bitcast.21), channel_id=1, source_target_pairs={{0,1},{1,0},{2,3},{3,2},{4,5},{5,4},{6,7},{7,6},{8,9},{9,8},{10,11... | collective-permute-start | bytes 2162696 | tf_op jit(solution)/shard_map/ppermute | solution.py:569
  51.2 20.2 %collective-permute-start.11 = (bf16[8,5632]{1,0:T(8,128)(2,1)}, bf16[8,5632]{1,0:T(8,128)(2,1)S(1)}, u32[]{:S(2)}, u32[]{:S(2)}) collective-permute-start(bf16[8,5632]{1,0:T(8,128)(2,1)} %get-tuple-element.42), channel_id=1, source_target_pairs={{0,24},{2,26},{4,28},{6,30},{8,16},{10,18},{12,20},{14,22},{16,8},... | collective-permute-start | bytes 270344 | tf_op jit(solution)/shard_map/ppermute | solution.py:590
  57.0 17.1 %collective-permute-start.12 = (bf16[8,5632]{1,0:T(8,128)(2,1)}, bf16[8,5632]{1,0:T(8,128)(2,1)S(1)}, u32[]{:S(2)}, u32[]{:S(2)}) collective-permute-start(bf16[8,5632]{1,0:T(8,128)(2,1)} %get-tuple-element.43), channel_id=1, source_target_pairs={{0,26},{2,24},{4,30},{6,28},{8,18},{10,16},{12,22},{14,20},{16,10}... | collective-permute-start | bytes 270344 | tf_op jit(solution)/shard_map/ppermute | solution.py:590
  59.5 16.8 %collective-permute-start.13 = (bf16[8,5632]{1,0:T(8,128)(2,1)}, bf16[8,5632]{1,0:T(8,128)(2,1)S(1)}, u32[]{:S(2)}, u32[]{:S(2)}) collective-permute-start(bf16[8,5632]{1,0:T(8,128)(2,1)} %get-tuple-element.44), channel_id=1, source_target_pairs={{0,28},{2,30},{4,24},{6,26},{8,20},{10,22},{12,16},{14,18},{16,12}... | collective-permute-start | bytes 270344 | tf_op jit(solution)/shard_map/ppermute | solution.py:590
  61.8 16.6 %collective-permute-start.14 = (bf16[8,5632]{1,0:T(8,128)(2,1)}, bf16[8,5632]{1,0:T(8,128)(2,1)S(1)}, u32[]{:S(2)}, u32[]{:S(2)}) collective-permute-start(bf16[8,5632]{1,0:T(8,128)(2,1)} %get-tuple-element.45), channel_id=1, source_target_pairs={{0,30},{2,28},{4,26},{6,24},{8,22},{10,20},{12,18},{14,16},{16,14}... | collective-permute-start | bytes 270344 | tf_op jit(solution)/shard_map/ppermute | solution.py:590
  78.5 0.9 copy-start.4
  84.3 19.9 %collective-permute-start.17 = (bf16[128,1408]{1,0:T(8,128)(2,1)S(1)}, bf16[128,1408]{1,0:T(8,128)(2,1)S(1)}, u32[]{:S(2)}, u32[]{:S(2)}) collective-permute-start(bf16[128,1408]{1,0:T(8,128)(2,1)S(1)} %bitcast.18), channel_id=1, source_target_pairs={{0,1},{1,0},{2,3},{3,2},{4,5},{5,4},{6,7},{7,6},{8,9},{9,8},{10,11... | collective-permute-start | bytes 1081352 | tf_op jit(solution)/shard_map/ppermute | solution.py:569
  85.6 16.4 %collective-permute-start.15 = (bf16[128,1408]{1,0:T(8,128)(2,1)S(1)}, bf16[128,1408]{1,0:T(8,128)(2,1)S(1)}, u32[]{:S(2)}, u32[]{:S(2)}) collective-permute-start(bf16[128,1408]{1,0:T(8,128)(2,1)S(1)} %bitcast.19), channel_id=1, source_target_pairs={{0,1},{1,0},{2,3},{3,2},{4,5},{5,4},{6,7},{7,6},{8,9},{9,8},{10,11... | collective-permute-start | bytes 1081352 | tf_op jit(solution)/shard_map/ppermute | solution.py:569
  85.9 4.5 %copy-start = (bf16[2,128,2816]{2,1,0:T(8,128)(2,1)S(1)}, bf16[2,128,2816]{2,1,0:T(8,128)(2,1)}, u32[]{:S(2)}) copy-start(bf16[2,128,2816]{2,1,0:T(8,128)(2,1)} %gate_ref.5) | copy-start | bytes 4325380
  85.9 4.5 %copy-start.1 = (bf16[2,128,2816]{2,1,0:T(8,128)(2,1)S(1)}, bf16[2,128,2816]{2,1,0:T(8,128)(2,1)}, u32[]{:S(2)}) copy-start(bf16[2,128,2816]{2,1,0:T(8,128)(2,1)} %up_ref.5) | copy-start | bytes 4325380
  85.9 4.5 %copy-start.2 = (s32[1,2688]{1,0:T(1,128)S(1)}, s32[1,2688]{1,0:T(1,128)}, u32[]{:S(2)}) copy-start(s32[1,2688]{1,0:T(1,128)} %get-tuple-element.49.far_ids_ref.ids_ref) | copy-start | bytes 32260

commit v4 on v3

--- a/solution.py
+++ b/solution.py
@@ -14,6 +14,7 @@
 VMEM = pl.BlockSpec(memory_space=pltpu.VMEM)
 HBM = pl.BlockSpec(memory_space=pl.ANY)
 K_CHUNK = 256
+MOVED_TILES = 2
 PARAMS = pltpu.CompilerParams(vmem_limit_bytes=32 << 20)
 
 
@@ -89,13 +90,12 @@
     return loads
 
 
-def put_slots(loads, pick, scale, in_ref, held_ref, sent_refs, sems):
-    width = held_ref.shape[1] // len(loads)
+def put_slots(parts, pick, scale, held_ref, sent_refs, sems):
     stores = []
-    for side, load in enumerate(loads):
-        columns = pl.ds(side * width, width)
+    for number, (load, source, start) in enumerate(parts):
+        columns = pl.ds(start, source.shape[1])
         load.wait()
-        rows = jnp.dot(pick, in_ref[:, columns], preferred_element_type=F32)
+        rows = jnp.dot(pick, source[...], preferred_element_type=F32)
         held_ref[:, columns] = (rows * scale).astype(BF16)
         first = 0
         for piece, ref in enumerate(sent_refs):
@@ -104,7 +104,7 @@
                 pltpu.make_async_copy(
                     held_ref.at[pl.ds(first, count), columns],
                     ref.at[:, columns],
-                    sems.at[side, piece],
+                    sems.at[number, piece],
                 )
             )
             stores[-1].start()
@@ -113,36 +113,46 @@
 
 
 def send_kernel(layer, cap, table_ref, gate_ref, up_ref, *refs):
-    *sent_refs, map_ref, in_ref, held_ref, key_ref, within_ref, map_sem, in_sems, out_sems = refs
+    *sent_refs, map_ref, in_ref, rest_ref, held_ref, key_ref, within_ref = refs[:-4]
+    map_sem, in_sems, rest_sem, out_sems = refs[-4:]
+    narrow, moved = gate_ref.shape[2], rest_ref.shape[1]
     map_load = pltpu.make_async_copy(table_ref, map_ref, map_sem)
     map_load.start()
     loads = load_weights([layer], gate_ref, up_ref, in_ref, in_sems)
+    rest = pltpu.make_async_copy(up_ref.at[0, :, pl.ds(narrow - moved, moved)], rest_ref, rest_sem)
+    rest.start()
     me = lax.axis_index("section")
     targets = [me ^ p for p in range(map_ref.shape[0])]
     map_load.wait()
     pick, count = pick_matrix(map_ref[...], me, cap, key_ref, within_ref, targets)
-    stores = put_slots(loads, pick, 1.0 / count, in_ref.at[0], held_ref, sent_refs, out_sems)
-    for store in stores:
+    parts = [
+        (loads[0], in_ref.at[0, :, pl.ds(0, narrow)], 0),
+        (loads[1], in_ref.at[0, :, pl.ds(narrow, narrow)], narrow),
+        (rest, rest_ref, 2 * narrow),
+    ]
+    for store in put_slots(parts, pick, 1.0 / count, held_ref, sent_refs, out_sems):
         store.wait()
 
 
-def send_rows(table, gate, up, layer, cap):
+def send_rows(table, gate, up, layer, cap, moved):
     _, rows, narrow = gate.shape
     blocks = table.shape[0]
     return pl.pallas_call(
         functools.partial(send_kernel, layer, cap),
-        out_shape=[jax.ShapeDtypeStruct((cap, 2 * narrow), BF16)] * blocks,
+        out_shape=[jax.ShapeDtypeStruct((cap, 2 * narrow + moved), BF16)] * blocks,
         in_specs=[HBM] * 3,
         out_specs=[HBM] * blocks,
         scratch_shapes=[
             pltpu.VMEM((blocks, rows), I32),
             pltpu.VMEM((1, rows, 2 * narrow), BF16),
-            pltpu.VMEM((blocks * cap, 2 * narrow), BF16),
+            pltpu.VMEM((rows, moved), BF16),
+            pltpu.VMEM((blocks * cap, 2 * narrow + moved), BF16),
             pltpu.VMEM((blocks, rows), I32),
             pltpu.VMEM((blocks, rows), I32),
             pltpu.SemaphoreType.DMA(()),
             pltpu.SemaphoreType.DMA((1, 2)),
-            pltpu.SemaphoreType.DMA((2, blocks)),
+            pltpu.SemaphoreType.DMA(()),
+            pltpu.SemaphoreType.DMA((3, blocks)),
         ],
         cost_estimate=pl.CostEstimate(
             flops=4 * blocks * cap * rows * narrow,
@@ -227,18 +237,20 @@
     in_ref, own_ref, held_ref, key_ref, within_ref, in_sems, out_sems,
 ):
     layers, rows, narrow = gate_ref.shape
-    loads = load_weights([layers - 1, 0], gate_ref, up_ref, in_ref, in_sems)
+    loads = load_weights([0, layers - 1], gate_ref, up_ref, in_ref, in_sems)
     me = lax.axis_index("section")
     table = table_ref[...]
     column_plan(narrow, map_ref, near_ref, send_ref, far_ref, splits)
     scale = 1.0 / count_of(table, iota((rows, 1), 0) + me * rows)
     pick, count = pick_matrix(table, me, cap, key_ref, within_ref, list(range(table.shape[0])))
-    stores = put_slots(
-        loads[2:], pick, 1.0 / count, in_ref.at[1], held_ref, (sent_ref,), out_sems
-    )
-    for side, load in enumerate(loads[:2]):
+    parts = [
+        (loads[0], in_ref.at[0, :, pl.ds(0, narrow)], 0),
+        (loads[1], in_ref.at[0, :, pl.ds(narrow, sent_ref.shape[1] - narrow)], narrow),
+    ]
+    stores = put_slots(parts, pick, 1.0 / count, held_ref, (sent_ref,), out_sems)
+    for side, load in enumerate(loads[2:]):
         load.wait()
-        columns = in_ref[0, :, side * narrow : (side + 1) * narrow]
+        columns = in_ref[1, :, side * narrow : (side + 1) * narrow]
         own_ref[side * rows : (side + 1) * rows] = (columns.astype(F32) * scale).astype(BF16)
     for s in range(splits - 1):
         turn_ref[s] = onehot_dot(own_ref, send_ref[s : s + 1, :], narrow).astype(BF16)
@@ -246,7 +258,7 @@
         store.wait()
 
 
-def middle(table, columns, gate, up, cap, splits, width):
+def middle(table, columns, gate, up, cap, splits, width, moved):
     _, rows, narrow = gate.shape
     blocks = table.shape[0]
     extra = columns.size // splits
@@ -257,14 +269,14 @@
             jax.ShapeDtypeStruct((1, extra), I32),
             jax.ShapeDtypeStruct((splits - 1, width), I32),
             jax.ShapeDtypeStruct((splits - 1, extra), I32),
-            jax.ShapeDtypeStruct((blocks * cap, 2 * narrow), BF16),
+            jax.ShapeDtypeStruct((blocks * cap, 2 * narrow - moved), BF16),
         ),
         in_specs=[VMEM, VMEM, HBM, HBM],
         out_specs=(VMEM, VMEM, VMEM, VMEM, HBM),
         scratch_shapes=[
             pltpu.VMEM((2, rows, 2 * narrow), BF16),
             pltpu.VMEM((2 * rows, narrow), BF16),
-            pltpu.VMEM((blocks * cap, 2 * narrow), BF16),
+            pltpu.VMEM((blocks * cap, 2 * narrow - moved), BF16),
             pltpu.VMEM((blocks, rows), I32),
             pltpu.VMEM((blocks, rows), I32),
             pltpu.SemaphoreType.DMA((2, 2)),
@@ -297,7 +309,7 @@
 
 
 def arrive_kernel(land_ref, ids_ref, *refs):
-    *came_refs, rows_ref, gate_ref, up_ref, held_ref, sems = refs
+    *came_refs, rows_ref, rest_ref, gate_ref, up_ref, held_ref, sems = refs
     narrow = rows_ref.shape[1]
     rows = land_ref.shape[0]
     cap = came_refs[0].shape[0]
@@ -320,23 +332,27 @@
         picked = onehot_dot(rows_ref, ids_ref[s : s + 1, :], narrow).astype(BF16)
         gate_ref[s] = picked[:rows]
         up_ref[s] = picked[rows:]
-
-
-def arrive_rows(land, ids, came):
+    rest_ref[...] = jnp.dot(
+        land_ref[...], held_ref[:, 2 * narrow :], preferred_element_type=F32
+    ).astype(BF16)
+
+
+def arrive_rows(land, ids, came, moved):
     rows, slots = land.shape
-    narrow = came[0].shape[1] // 2
+    narrow = (came[0].shape[1] - moved) // 2
     turns, width = ids.shape
     return pl.pallas_call(
         arrive_kernel,
         out_shape=(
             jax.ShapeDtypeStruct((2 * rows, narrow), BF16),
+            jax.ShapeDtypeStruct((rows, moved), BF16),
             jax.ShapeDtypeStruct((turns, rows, width), BF16),
             jax.ShapeDtypeStruct((turns, rows, width), BF16),
         ),
         in_specs=[VMEM, VMEM] + [HBM] * len(came),
-        out_specs=(VMEM,) * 3,
+        out_specs=(VMEM,) * 4,
         scratch_shapes=[
-            pltpu.VMEM((slots, 2 * narrow), BF16),
+            pltpu.VMEM((slots, 2 * narrow + moved), BF16),
             pltpu.SemaphoreType.DMA((len(came),)),
         ],
         compiler_params=PARAMS,
@@ -466,15 +482,24 @@
     )(table, near_ids, far, far_ids, gate, up)
 
 
-def second_kernel(
-    rows_ref, near_ref, far_ref, ids_ref, old_ref, out_ref, held_ref, base_sem, sems
-):
+def second_kernel(with_rest, rows_ref, near_ref, far_ref, ids_ref, *refs):
+    rest_ref, _, out_ref, held_ref, base_sems, sems = refs if with_rest else (None, *refs)
     narrow = rows_ref.shape[1]
     layers = out_ref.shape[0]
     copies = [
-        pltpu.make_async_copy(rows_ref, out_ref.at[layers - 1, 1, :, pl.ds(0, narrow)], base_sem)
+        pltpu.make_async_copy(
+            rows_ref, out_ref.at[layers - 1, 1, :, pl.ds(0, narrow)], base_sems.at[0]
+        )
     ]
-    copies[0].start()
+    if with_rest:
+        moved = rest_ref.shape[1]
+        copies.append(
+            pltpu.make_async_copy(
+                rest_ref, out_ref.at[0, 1, :, pl.ds(narrow - moved, moved)], base_sems.at[1]
+            )
+        )
+    for copy in copies:
+        copy.start()
 
     def near(start, size):
         return near_ref[:, start : start + size].astype(F32)
@@ -484,12 +509,13 @@
         copy.wait()
 
 
-def second_half(rows, near, far, ids, out, side):
+def second_half(rows, near, far, ids, rest, out, side):
     count, narrow = rows.shape[0] // 2, rows.shape[1]
     extra = near.shape[1]
     layers = out.shape[0]
+    rests = [] if rest is None else [rest]
     return pl.pallas_call(
-        second_kernel,
+        functools.partial(second_kernel, bool(rests)),
         out_shape=jax.ShapeDtypeStruct(out.shape, BF16),
         grid=(1,),
         in_specs=[
@@ -497,13 +523,14 @@
             pl.BlockSpec((count, extra), lambda i: (side, 0)),
             pl.BlockSpec(far.shape, lambda i: (0, 0, 0)),
             pl.BlockSpec(ids.shape, lambda i: (0, 0)),
+            *[pl.BlockSpec(array.shape, lambda i: (0, 0)) for array in rests],
             HBM,
         ],
         out_specs=HBM,
-        input_output_aliases={4: 0},
+        input_output_aliases={4 + len(rests): 0},
         scratch_shapes=[
             pltpu.VMEM((count, extra), BF16),
-            pltpu.SemaphoreType.DMA(()),
+            pltpu.SemaphoreType.DMA((2,)),
             pltpu.SemaphoreType.DMA((len(column_tiles(extra)), layers, 1)),
         ],
         compiler_params=PARAMS,
@@ -512,51 +539,54 @@
             bytes_accessed=4 * count * (narrow + layers * extra),
             transcendentals=0,
         ),
-    )(rows, near, far, ids, out)
-
-
-def last_kernel(land_ref, came_ref, gate_in, up_in, gate_out, up_out, held_ref, sems):
-    narrow = came_ref.shape[1] // 2
-    steps = sems.shape[1]
-    width = narrow // steps
+    )(rows, near, far, ids, *rests, out)
+
+
+def last_pieces(narrow, total):
+    return [
+        (side, side * narrow + start, start, size)
+        for side, extent in enumerate((narrow, total - narrow))
+        for start, size in column_tiles(extent)
+    ]
+
+
+def last_kernel(narrow, land_ref, came_ref, gate_in, up_in, gate_out, up_out, held_ref, sems):
+    outs = (gate_out, up_out)
     stores = []
-    for side, out in enumerate((gate_out, up_out)):
-        for step in range(steps):
-            at = side * narrow + step * width
-            held_ref[:, at : at + width] = jnp.dot(
-                land_ref[...], came_ref[:, at : at + width], preferred_element_type=F32
-            ).astype(BF16)
-            stores.append(
-                pltpu.make_async_copy(
-                    held_ref.at[:, pl.ds(at, width)],
-                    out.at[0, 1, :, pl.ds(step * width, width)],
-                    sems.at[side, step],
-                )
+    for number, (side, at, start, size) in enumerate(last_pieces(narrow, came_ref.shape[1])):
+        held_ref[:, at : at + size] = jnp.dot(
+            land_ref[...], came_ref[:, at : at + size], preferred_element_type=F32
+        ).astype(BF16)
+        stores.append(
+            pltpu.make_async_copy(
+                held_ref.at[:, pl.ds(at, size)],
+                outs[side].at[0, 1, :, pl.ds(start, size)],
+                sems.at[number],
             )
-            stores[-1].start()
+        )
+        stores[-1].start()
     for store in stores:
         store.wait()
 
 
-def last_rows(land, came, gate_out, up_out):
+def last_rows(land, came, gate_out, up_out, narrow):
     rows, slots = land.shape
-    narrow = came.shape[1] // 2
-    steps = 2
+    total = came.shape[1]
     out_type = jax.ShapeDtypeStruct(gate_out.shape, BF16)
     return pl.pallas_call(
-        last_kernel,
+        functools.partial(last_kernel, narrow),
         out_shape=(out_type, out_type),
         in_specs=[VMEM] * 2 + [HBM] * 2,
         out_specs=(HBM, HBM),
         input_output_aliases={2: 0, 3: 1},
         scratch_shapes=[
-            pltpu.VMEM((rows, 2 * narrow), BF16),
-            pltpu.SemaphoreType.DMA((2, steps)),
+            pltpu.VMEM((rows, total), BF16),
+            pltpu.SemaphoreType.DMA((len(last_pieces(narrow, total)),)),
         ],
         compiler_params=PARAMS,
         cost_estimate=pl.CostEstimate(
-            flops=4 * rows * slots * narrow,
-            bytes_accessed=8 * rows * narrow,
+            flops=2 * rows * slots * total,
+            bytes_accessed=4 * rows * total,
             transcendentals=0,
         ),
         name="last_rows",
@@ -580,6 +610,7 @@
     cap = rows // blocks
     column_cap = extra // splits
     width = -(-column_cap // 128) * 128
+    moved = min(MOVED_TILES, narrow // 256) * 128
     table = hidden_map.reshape(blocks, rows)
     out_type = jax.ShapeDtypeStruct((layers, 2, rows, narrow + extra), BF16)
 
@@ -589,24 +620,27 @@
     def cross(sent, p):
         return lax.ppermute(sent, "section", [(i, i ^ p) for i in range(blocks)])
 
-    sent_top = send_rows(table, gate_weight, up_weight, layers - 1, cap)
+    sent_top = send_rows(table, gate_weight, up_weight, layers - 1, cap, moved)
     came_top = [sent_top[0]] + [cross(sent_top[p], p) for p in range(1, blocks)]
     columns = ffn_map.reshape(-1, 128)
     own_sent, near_ids, send_ids, far_ids, sent_low = middle(
-        table, columns, gate_weight, up_weight, cap, splits, width
+        table, columns, gate_weight, up_weight, cap, splits, width, moved
     )
     own_far = turn_around(own_sent, splits)
     came_low = swap_rows(sent_low)
     land = land_rows(table, cap)
-    got, *got_sent = arrive_rows(land, send_ids, came_top)
+    got, rest, *got_sent = arrive_rows(land, send_ids, came_top, moved)
     got_far = [turn_around(got_sent[side], splits) for side in range(2)]
     outs = first_half(table, near_ids, own_far, far_ids, gate_weight, up_weight, out_type)
     got_near = near_columns(got, near_ids)
     outs = [
-        second_half(got, got_near, got_far[side], far_ids, outs[side], side)
+        second_half(
+            got, got_near, got_far[side], far_ids,
+            rest if side else None, outs[side], side,
+        )
         for side in range(2)
     ]
-    return last_rows(land, came_low, *outs)
+    return last_rows(land, came_low, *outs, narrow)
 
 
 def plain_local(gate_weight, up_weight, hidden_map, ffn_map):

time: 110 us -> 109 us (level)
  waiting for transfers between devices: 34.3 us -> 32.7 us
  starting transfers between devices: 37.1 us -> 38.5 us
    ppermute x15, waiting for transfers between devices: 32.2 us -> 30.5 us  [cross(): return lax.ppermute(sent, 'section', [(i, i ^ p) for i in range(blocks)])]
    ppermute x15, starting transfers between devices: 27.7 us -> 29.1 us  [cross(): return lax.ppermute(sent, 'section', [(i, i ^ p) for i in range(blocks)])]
where the time goes in v4:
time: 109 us; the launch traced here: 108 us
  starting transfers between devices  38.5 us (35%)
  Pallas kernels  34.6 us (32%)
  waiting for transfers between devices  32.7 us (30%)
    ppermute x15, waiting for transfers between devices, cross(): return lax.ppermute(sent, 'section', [(i, i ^ p) for i in range(blocks)])  30.5 us
    ppermute x15, starting transfers between devices, cross(): return lax.ppermute(sent, 'section', [(i, i ^ p) for i in range(blocks)])  29.1 us
    pallas_call x1, Pallas kernels, first_half(): pl.pallas_call(first_kernel, out_shape=(out_type, out_type), in_specs=[VM...  9.5 us
    all_to_all x1, starting transfers between devices, swap_rows(): lax.all_to_all(sent, 'section', split_axis=0, concat_axis=0, tiled=True)  6.67 us
    pallas_call x1, Pallas kernels, middle(): pl.pallas_call(functools.partial(middle_kernel, cap, splits), out_shape=(...  6.08 us
    pallas_call x1, Pallas kernels, arrive_rows(): pl.pallas_call(arrive_kernel, out_shape=(jax.ShapeDtypeStruct((2 * rows,...  5.03 us
    pallas_call x2, Pallas kernels, second_half(): pl.pallas_call(functools.partial(second_kernel, bool(rests)), out_shape=j...  4.59 us
    pallas_call x1, Pallas kernels, near_columns(): pl.pallas_call(near_kernel, out_shape=jax.ShapeDtypeStruct((count, extra)...  4.4 us
  transfers between devices with their start and end apart: 19, of which 12 were waited for; matrix products, arithmetic and copies ran while one was open for 0% of the time, Pallas kernels for 25%

profile of v4, /device:TPU:13, one launch (start us, length us, event | category | flops | bytes accessed | tf_op | source)
XLA Modules:
  0.0 107.7 jit_solution(9687038272938628651)
XLA Ops:
  0.6 0.0 copy-start.3
  0.6 6.1 %middle.1 = (bf16[1,256,1408]{2,1,0:T(8,128)(2,1)}, s32[1,2688]{1,0:T(1,128)}, s32[1,1408]{1,0:T(1,128)}, s32[1,2688]{1,0:T(1,128)}, bf16[128,5376]{1,0:T(8,128)(2,1)}) custom-call(s32[16,128]{1,0:T(8,128)} %bitcast.13, s32[42,128]{1,0:T(8,128)} %bitcast.22, bf16[2,128,2816]{2,1,0:T(8,128)(2,1)} %gate_ref.5, bf16[2,128,2816]{2,1,0:T(8,128)(2,1)} %up_ref.5), custom_call_target="tpu_custom_call" | custom-call | flops 2030043136 | bytes 5767168 | tf_op jit(solution)/shard_map/middle/pallas_call | solution.py:265
  6.7 0.0 copy-start.7
  6.7 0.0 copy-start.6
  6.8 6.7 %all-to-all-start = ((bf16[16,8,5376]{2,1,0:T(8,128)(2,1)}), bf16[16,8,5376]{2,1,0:T(8,128)(2,1)S(1)}, u32[]{:S(2)}, u32[]{:S(2)}) async-start(bf16[16,8,5376]{2,1,0:T(8,128)(2,1)} %bitcast.20), calls=%async_computation | async-start | bytes 2752512 | tf_op jit(solution)/shard_map/all_to_all | solution.py:618
  13.4 0.0 copy-start.5
  13.4 3.4 %send_rows.1 = (bf16[8,5888]{1,0:T(8,128)(2,1)}, bf16[8,5888]{1,0:T(8,128)(2,1)}, bf16[8,5888]{1,0:T(8,128)(2,1)}, bf16[8,5888]{1,0:T(8,128)(2,1)}, bf16[8,5888]...) custom-call(s32[16,128]{1,0:T(8,128)} %bitcast.14, ...), custom_call_target="tpu_custom_call" | custom-call | flops 184549376 | bytes 2883584 | tf_op jit(solution)/shard_map/send_rows/pallas_call | solution.py:140
  16.9 0.5 collective-permute-start
  17.3 0.3 collective-permute-start.1
  17.6 1.5 %collective-permute-start.2 = (bf16[8,5888]{1,0:T(8,128)(2,1)}, bf16[8,5888]{1,0:T(8,128)(2,1)S(1)}, u32[]{:S(2)}, u32[]{:S(2)}) collective-permute-start(bf16[8,5888]{1,0:T(8,128)(2,1)} %get-tuple-element.34), channel_id=1, source_target_pairs={{0,6},{2,4},{4,2},{6,0},{8,14},{10,12},{12,10},{14,8},{16,22},{18,... | collective-permute-start | bytes 282632 | tf_op jit(solution)/shard_map/ppermute | solution.py:621
  19.1 0.3 collective-permute-start.3
  19.3 1.5 %collective-permute-start.4 = (bf16[8,5888]{1,0:T(8,128)(2,1)}, bf16[8,5888]{1,0:T(8,128)(2,1)S(1)}, u32[]{:S(2)}, u32[]{:S(2)}) collective-permute-start(bf16[8,5888]{1,0:T(8,128)(2,1)} %get-tuple-element.36), channel_id=1, source_target_pairs={{0,10},{2,8},{4,14},{6,12},{8,2},{10,0},{12,6},{14,4},{16,26},{18,... | collective-permute-start | bytes 282632 | tf_op jit(solution)/shard_map/ppermute | solution.py:621
  20.8 0.0 collective-permute-done.refs_1_
  20.8 0.0 collective-permute-start.5
  20.8 1.6 %collective-permute-done.1.refs_2_ = bf16[8,5888]{1,0:T(8,128)(2,1)S(1)} collective-permute-done((bf16[8,5888]{1,0:T(8,128)(2,1)}, bf16[8,5888]{1,0:T(8,128)(2,1)S(1)}, u32[]{:S(2)}, u32[]{:S(2)}) %collective-permute-start.1) | collective-permute-done | bytes 94240 | tf_op jit(solution)/shard_map/ppermute | solution.py:621
  22.4 5.4 %collective-permute-start.6 = (bf16[8,5888]{1,0:T(8,128)(2,1)}, bf16[8,5888]{1,0:T(8,128)(2,1)S(1)}, u32[]{:S(2)}, u32[]{:S(2)}) collective-permute-start(bf16[8,5888]{1,0:T(8,128)(2,1)} %get-tuple-element.38), channel_id=1, source_target_pairs={{0,14},{2,12},{4,10},{6,8},{8,6},{10,4},{12,2},{14,0},{16,30},{18,... | collective-permute-start | bytes 282632 | tf_op jit(solution)/shard_map/ppermute | solution.py:621
  27.9 0.0 collective-permute-done.2.refs_3_
  27.9 2.9 %collective-permute-start.7 = (bf16[8,5888]{1,0:T(8,128)(2,1)}, bf16[8,5888]{1,0:T(8,128)(2,1)S(1)}, u32[]{:S(2)}, u32[]{:S(2)}) collective-permute-start(bf16[8,5888]{1,0:T(8,128)(2,1)} %get-tuple-element.39), channel_id=1, source_target_pairs={{0,16},{2,18},{4,20},{6,22},{8,24},{10,26},{12,28},{14,30},{16,0},... | collective-permute-start | bytes 282632 | tf_op jit(solution)/shard_map/ppermute | solution.py:621
  30.8 8.1 %collective-permute-done.3.refs_4_ = bf16[8,5888]{1,0:T(8,128)(2,1)S(1)} collective-permute-done((bf16[8,5888]{1,0:T(8,128)(2,1)}, bf16[8,5888]{1,0:T(8,128)(2,1)S(1)}, u32[]{:S(2)}, u32[]{:S(2)}) %collective-permute-start.3) | collective-permute-done | bytes 94240 | tf_op jit(solution)/shard_map/ppermute | solution.py:621
  38.9 2.6 %collective-permute-start.8 = (bf16[8,5888]{1,0:T(8,128)(2,1)}, bf16[8,5888]{1,0:T(8,128)(2,1)S(1)}, u32[]{:S(2)}, u32[]{:S(2)}) collective-permute-start(bf16[8,5888]{1,0:T(8,128)(2,1)} %get-tuple-element.40), channel_id=1, source_target_pairs={{0,18},{2,16},{4,22},{6,20},{8,26},{10,24},{12,30},{14,28},{16,2},... | collective-permute-start | bytes 282632 | tf_op jit(solution)/shard_map/ppermute | solution.py:621
  41.5 0.6 collective-permute-done.4.refs_5_
  42.1 0.2 collective-permute-start.9
  42.2 1.0 collective-permute-done.5.refs_6_
  43.2 3.9 %collective-permute-start.10 = (bf16[8,5888]{1,0:T(8,128)(2,1)}, bf16[8,5888]{1,0:T(8,128)(2,1)S(1)}, u32[]{:S(2)}, u32[]{:S(2)}) collective-permute-start(bf16[8,5888]{1,0:T(8,128)(2,1)} %get-tuple-element.42), channel_id=1, source_target_pairs={{0,22},{2,20},{4,18},{6,16},{8,30},{10,28},{12,26},{14,24},{16,6},... | collective-permute-start | bytes 282632 | tf_op jit(solution)/shard_map/ppermute | solution.py:621
  47.2 0.0 collective-permute-done.6.refs_7_
  47.2 0.0 copy-done.7
  47.2 1.2 %collective-permute-start.16 = (bf16[256,1408]{1,0:T(8,128)(2,1)S(1)}, bf16[256,1408]{1,0:T(8,128)(2,1)S(1)}, u32[]{:S(2)}, u32[]{:S(2)}) collective-permute-start(bf16[256,1408]{1,0:T(8,128)(2,1)S(1)} %bitcast.21), channel_id=1, source_target_pairs={{0,1},{1,0},{2,3},{3,2},{4,5},{5,4},{6,7},{7,6},{8,9},{9,8},{10,11... | collective-permute-start | bytes 2162696 | tf_op jit(solution)/shard_map/ppermute | solution.py:599
  48.4 1.9 %collective-permute-done.7.refs_8_ = bf16[8,5888]{1,0:T(8,128)(2,1)S(1)} collective-permute-done((bf16[8,5888]{1,0:T(8,128)(2,1)}, bf16[8,5888]{1,0:T(8,128)(2,1)S(1)}, u32[]{:S(2)}, u32[]{:S(2)}) %collective-permute-start.7) | collective-permute-done | bytes 94240 | tf_op jit(solution)/shard_map/ppermute | solution.py:621
  50.3 0.0 collective-permute-start.11
  50.3 6.2 %collective-permute-done.8.refs_9_ = bf16[8,5888]{1,0:T(8,128)(2,1)S(1)} collective-permute-done((bf16[8,5888]{1,0:T(8,128)(2,1)}, bf16[8,5888]{1,0:T(8,128)(2,1)S(1)}, u32[]{:S(2)}, u32[]{:S(2)}) %collective-permute-start.8) | collective-permute-done | bytes 94240 | tf_op jit(solution)/shard_map/ppermute | solution.py:621
  56.4 2.6 %collective-permute-start.12 = (bf16[8,5888]{1,0:T(8,128)(2,1)}, bf16[8,5888]{1,0:T(8,128)(2,1)S(1)}, u32[]{:S(2)}, u32[]{:S(2)}) collective-permute-start(bf16[8,5888]{1,0:T(8,128)(2,1)} %get-tuple-element.44), channel_id=1, source_target_pairs={{0,26},{2,24},{4,30},{6,28},{8,18},{10,16},{12,22},{14,20},{16,10}... | collective-permute-start | bytes 282632 | tf_op jit(solution)/shard_map/ppermute | solution.py:621
  59.0 0.0 collective-permute-done.9.refs_10_
  59.0 0.8 collective-permute-start.13
  59.8 0.6 collective-permute-done.10.refs_11_
  60.5 6.7 %collective-permute-start.14 = (bf16[8,5888]{1,0:T(8,128)(2,1)}, bf16[8,5888]{1,0:T(8,128)(2,1)S(1)}, u32[]{:S(2)}, u32[]{:S(2)}) collective-permute-start(bf16[8,5888]{1,0:T(8,128)(2,1)} %get-tuple-element.46), channel_id=1, source_target_pairs={{0,30},{2,28},{4,26},{6,24},{8,22},{10,20},{12,18},{14,16},{16,14}... | collective-permute-start | bytes 282632 | tf_op jit(solution)/shard_map/ppermute | solution.py:621
  67.2 0.0 copy-done.3
  67.2 0.2 land_rows.1.land_ref
  67.4 0.9 collective-permute-done.11.refs_12_
  68.3 5.9 %collective-permute-done.12.refs_13_ = bf16[8,5888]{1,0:T(8,128)(2,1)S(1)} collective-permute-done((bf16[8,5888]{1,0:T(8,128)(2,1)}, bf16[8,5888]{1,0:T(8,128)(2,1)S(1)}, u32[]{:S(2)}, u32[]{:S(2)}) %collective-permute-start.12) | collective-permute-done | bytes 94240 | tf_op jit(solution)/shard_map/ppermute | solution.py:621
  74.2 1.4 %collective-permute-done.13.refs_14_ = bf16[8,5888]{1,0:T(8,128)(2,1)S(1)} collective-permute-done((bf16[8,5888]{1,0:T(8,128)(2,1)}, bf16[8,5888]{1,0:T(8,128)(2,1)S(1)}, u32[]{:S(2)}, u32[]{:S(2)}) %collective-permute-start.13) | collective-permute-done | bytes 94240 | tf_op jit(solution)/shard_map/ppermute | solution.py:621
  75.6 2.3 %collective-permute-done.14.refs_15_ = bf16[8,5888]{1,0:T(8,128)(2,1)S(1)} collective-permute-done((bf16[8,5888]{1,0:T(8,128)(2,1)}, bf16[8,5888]{1,0:T(8,128)(2,1)S(1)}, u32[]{:S(2)}, u32[]{:S(2)}) %collective-permute-start.14) | collective-permute-done | bytes 94240 | tf_op jit(solution)/shard_map/ppermute | solution.py:621
  77.9 0.0 copy-done.6
  77.9 0.0 copy-start.4
  77.9 0.9 copy-done.4
  78.8 5.0 %arrive_rows.1 = (bf16[256,2816]{1,0:T(8,128)(2,1)S(1)}, bf16[128,256]{1,0:T(8,128)(2,1)S(1)}, bf16[1,128,1408]{2,1,0:T(8,128)(2,1)S(1)}, bf16[1,128,1408]{2,1,0:T(8,128)(2,1)S(1)}) custom-call(bf16[128,128]{1,0:T(8,128)(2,1)S(1)} %land_rows.1.land_ref, s32[1,1408]{1,0:T(1,128)S(1)} %copy-done.6, bf16[8,5888]{1,0:T(8,128)(2,1)S(1)} %copy-done.4, ...), custom_call_target="tpu_custom_call" | custom-call | flops 2030043136 | bytes 2883584 | tf_op jit(solution)/shard_map/arrive_rows/pallas_call | solution.py:344
  83.9 1.3 %collective-permute-start.17 = (bf16[128,1408]{1,0:T(8,128)(2,1)S(1)}, bf16[128,1408]{1,0:T(8,128)(2,1)S(1)}, u32[]{:S(2)}, u32[]{:S(2)}) collective-permute-start(bf16[128,1408]{1,0:T(8,128)(2,1)S(1)} %bitcast.18), channel_id=1, source_target_pairs={{0,1},{1,0},{2,3},{3,2},{4,5},{5,4},{6,7},{7,6},{8,9},{9,8},{10,11... | collective-permute-start | bytes 1081352 | tf_op jit(solution)/shard_map/ppermute | solution.py:599
  85.1 0.3 collective-permute-start.15
  85.4 0.0 copy-done.5
  85.4 0.0 copy-start
  85.4 0.0 copy-start.1
  85.4 0.0 copy-start.2
  85.4 4.4 %shard_map.59.near_ref = bf16[256,2688]{1,0:T(8,128)(2,1)S(1)} custom-call(bf16[256,2816]{1,0:T(8,128)(2,1)S(1)} %get-tuple-element.47.rows_ref, s32[1,2688]{1,0:T(1,128)S(1)} %copy-done.5), custom_call_target="tpu_custom_call" | custom-call | flops 3875536896 | bytes 2818048 | tf_op jit(solution)/shard_map/pallas_call | solution.py:378
  89.8 0.0 collective-permute-done.16
  89.8 0.0 copy-done
  89.8 0.0 copy-done.1
  89.8 0.0 copy-done.2
  89.8 9.5 %first_half.1 = (bf16[2,2,128,5504]{3,2,1,0:T(8,128)(2,1)}, bf16[2,2,128,5504]{3,2,1,0:T(8,128)(2,1)}) custom-call(s32[16,128]{1,0:T(8,128)S(1)} %bitcast.16, s32[1,2688]{1,0:T(1,128)S(1)} %copy-done.5, bf16[1,256,1408]{2,1,0:T(8,128)(2,1)S(1)} %bitcast.17, s32[1,2688]{1,0:T(1,128)S(1)} %copy-done.2, bf16[2,128,2816]{2,1,0:T(8,128)(2,1)S(1)} %copy-done, ...), custom_call_target="tpu_custom_call" | custom-call | flops 5813305344 | bytes 11272192 | tf_op jit(solution)/shard_map/first_half/pallas_call | solution.py:462
  99.3 2.2 %collective-permute-done.15 = bf16[128,1408]{1,0:T(8,128)(2,1)S(1)} collective-permute-done((bf16[128,1408]{1,0:T(8,128)(2,1)S(1)}, bf16[128,1408]{1,0:T(8,128)(2,1)S(1)}, u32[]{:S(2)}, u32[]{:S(2)}) %collective-permute-start.15) | collective-permute-done | bytes 360480 | tf_op jit(solution)/shard_map/ppermute | solution.py:599
  101.5 2.3 %shard_map.60.gate_in = bf16[2,2,128,5504]{3,2,1,0:T(8,128)(2,1)} custom-call(bf16[256,2816]{1,0:T(8,128)(2,1)S(1)} %get-tuple-element.47.rows_ref, bf16[256,2688]{1,0:T(8,128)(2,1)S(1)} %shard_map.59.near_ref, bf16[1,128,1408]{2,1,0:T(8,128)(2,1)S(1)} %bitcast.12, s32[1,2688]{1,0:T(1,128)S(1)} %copy-done.2, ...), custom_call_target="tpu_custom_call", output_to_operand_aliasing={{}: (4, {})} | custom-call | flops 968884224 | bytes 4194304 | tf_op jit(solution)/shard_map/pallas_call | solution.py:517
  103.8 0.0 collective-permute-done.17
  103.8 2.3 %shard_map.61.up_in = bf16[2,2,128,5504]{3,2,1,0:T(8,128)(2,1)} custom-call(bf16[256,2816]{1,0:T(8,128)(2,1)S(1)} %get-tuple-element.47.rows_ref, bf16[256,2688]{1,0:T(8,128)(2,1)S(1)} %shard_map.59.near_ref, bf16[1,128,1408]{2,1,0:T(8,128)(2,1)S(1)} %bitcast.11, s32[1,2688]{1,0:T(1,128)S(1)} %copy-done.2, ...), custom_call_target="tpu_custom_call", output_to_operand_aliasing={{}: (5, {})} | custom-call | flops 968884224 | bytes 4194304 | tf_op jit(solution)/shard_map/pallas_call | solution.py:517
  106.1 0.0 all-to-all-done
  106.1 1.3 %last_rows.1 = (bf16[2,2,128,5504]{3,2,1,0:T(8,128)(2,1)}, bf16[2,2,128,5504]{3,2,1,0:T(8,128)(2,1)}) custom-call(bf16[128,128]{1,0:T(8,128)(2,1)S(1)} %land_rows.1.land_ref, bf16[128,5376]{1,0:T(8,128)(2,1)S(1)} %bitcast.10, bf16[2,2,128,5504]{3,2,1,0:T(8,128)(2,1)} %shard_map.60.gate_in, ...), custom_call_target="tpu_custom_call", output_to_operand_aliasing={{0}: (2, {}), {1}: (3, {})} | custom-call | flops 176160768 | bytes 2752512 | tf_op jit(solution)/shard_map/last_rows/pallas_call | solution.py:576
Async XLA Ops:
  0.6 66.6 %copy-start.3 = (s32[2048]{0:T(1024)S(1)}, s32[2048]{0:T(1024)}, u32[]{:S(2)}) copy-start(s32[2048]{0:T(1024)} %param.6) | copy-start | bytes 24580
  6.7 40.4 %copy-start.7 = (bf16[1,256,1408]{2,1,0:T(8,128)(2,1)S(1)}, bf16[1,256,1408]{2,1,0:T(8,128)(2,1)}, u32[]{:S(2)}) copy-start(bf16[1,256,1408]{2,1,0:T(8,128)(2,1)} %get-tuple-element.51) | copy-start | bytes 2162692
  6.7 71.2 %copy-start.6 = (s32[1,1408]{1,0:T(1,128)S(1)}, s32[1,1408]{1,0:T(1,128)}, u32[]{:S(2)}) copy-start(s32[1,1408]{1,0:T(1,128)} %get-tuple-element.30.ids_ref) | copy-start | bytes 16900
  6.8 99.4 %all-to-all-start = ((bf16[16,8,5376]{2,1,0:T(8,128)(2,1)}), bf16[16,8,5376]{2,1,0:T(8,128)(2,1)S(1)}, u32[]{:S(2)}, u32[]{:S(2)}) async-start(bf16[16,8,5376]{2,1,0:T(8,128)(2,1)} %bitcast.20), calls=%async_computation | async-start | bytes 2752512 | tf_op jit(solution)/shard_map/all_to_all | solution.py:618
  13.4 72.0 %copy-start.5 = (s32[1,2688]{1,0:T(1,128)S(1)}, s32[1,2688]{1,0:T(1,128)}, u32[]{:S(2)}) copy-start(s32[1,2688]{1,0:T(1,128)} %get-tuple-element.48.ids_ref.near_ids_ref) | copy-start | bytes 32260
  16.9 4.0 %collective-permute-start = (bf16[8,5888]{1,0:T(8,128)(2,1)}, bf16[8,5888]{1,0:T(8,128)(2,1)S(1)}, u32[]{:S(2)}, u32[]{:S(2)}) collective-permute-start(bf16[8,5888]{1,0:T(8,128)(2,1)} %get-tuple-element.32), channel_id=1, source_target_pairs={{0,2},{2,0},{4,6},{6,4},{8,10},{10,8},{12,14},{14,12},{16,18},{18,... | collective-permute-start | bytes 282632 | tf_op jit(solution)/shard_map/ppermute | solution.py:621
  17.3 5.1 %collective-permute-start.1 = (bf16[8,5888]{1,0:T(8,128)(2,1)}, bf16[8,5888]{1,0:T(8,128)(2,1)S(1)}, u32[]{:S(2)}, u32[]{:S(2)}) collective-permute-start(bf16[8,5888]{1,0:T(8,128)(2,1)} %get-tuple-element.33), channel_id=1, source_target_pairs={{0,4},{2,6},{4,0},{6,2},{8,12},{10,14},{12,8},{14,10},{16,20},{18,... | collective-permute-start | bytes 282632 | tf_op jit(solution)/shard_map/ppermute | solution.py:621
  17.6 10.3 %collective-permute-start.2 = (bf16[8,5888]{1,0:T(8,128)(2,1)}, bf16[8,5888]{1,0:T(8,128)(2,1)S(1)}, u32[]{:S(2)}, u32[]{:S(2)}) collective-permute-start(bf16[8,5888]{1,0:T(8,128)(2,1)} %get-tuple-element.34), channel_id=1, source_target_pairs={{0,6},{2,4},{4,2},{6,0},{8,14},{10,12},{12,10},{14,8},{16,22},{18,... | collective-permute-start | bytes 282632 | tf_op jit(solution)/shard_map/ppermute | solution.py:621
  19.1 19.8 %collective-permute-start.3 = (bf16[8,5888]{1,0:T(8,128)(2,1)}, bf16[8,5888]{1,0:T(8,128)(2,1)S(1)}, u32[]{:S(2)}, u32[]{:S(2)}) collective-permute-start(bf16[8,5888]{1,0:T(8,128)(2,1)} %get-tuple-element.35), channel_id=1, source_target_pairs={{0,8},{2,10},{4,12},{6,14},{8,0},{10,2},{12,4},{14,6},{16,24},{18,... | collective-permute-start | bytes 282632 | tf_op jit(solution)/shard_map/ppermute | solution.py:621
  19.3 22.7 %collective-permute-start.4 = (bf16[8,5888]{1,0:T(8,128)(2,1)}, bf16[8,5888]{1,0:T(8,128)(2,1)S(1)}, u32[]{:S(2)}, u32[]{:S(2)}) collective-permute-start(bf16[8,5888]{1,0:T(8,128)(2,1)} %get-tuple-element.36), channel_id=1, source_target_pairs={{0,10},{2,8},{4,14},{6,12},{8,2},{10,0},{12,6},{14,4},{16,26},{18,... | collective-permute-start | bytes 282632 | tf_op jit(solution)/shard_map/ppermute | solution.py:621
  20.8 22.4 %collective-permute-start.5 = (bf16[8,5888]{1,0:T(8,128)(2,1)}, bf16[8,5888]{1,0:T(8,128)(2,1)S(1)}, u32[]{:S(2)}, u32[]{:S(2)}) collective-permute-start(bf16[8,5888]{1,0:T(8,128)(2,1)} %get-tuple-element.37), channel_id=1, source_target_pairs={{0,12},{2,14},{4,8},{6,10},{8,4},{10,6},{12,0},{14,2},{16,28},{18,... | collective-permute-start | bytes 282632 | tf_op jit(solution)/shard_map/ppermute | solution.py:621
  22.4 24.7 %collective-permute-start.6 = (bf16[8,5888]{1,0:T(8,128)(2,1)}, bf16[8,5888]{1,0:T(8,128)(2,1)S(1)}, u32[]{:S(2)}, u32[]{:S(2)}) collective-permute-start(bf16[8,5888]{1,0:T(8,128)(2,1)} %get-tuple-element.38), channel_id=1, source_target_pairs={{0,14},{2,12},{4,10},{6,8},{8,6},{10,4},{12,2},{14,0},{16,30},{18,... | collective-permute-start | bytes 282632 | tf_op jit(solution)/shard_map/ppermute | solution.py:621
  27.9 22.4 %collective-permute-start.7 = (bf16[8,5888]{1,0:T(8,128)(2,1)}, bf16[8,5888]{1,0:T(8,128)(2,1)S(1)}, u32[]{:S(2)}, u32[]{:S(2)}) collective-permute-start(bf16[8,5888]{1,0:T(8,128)(2,1)} %get-tuple-element.39), channel_id=1, source_target_pairs={{0,16},{2,18},{4,20},{6,22},{8,24},{10,26},{12,28},{14,30},{16,0},... | collective-permute-start | bytes 282632 | tf_op jit(solution)/shard_map/ppermute | solution.py:621
  38.9 17.6 %collective-permute-start.8 = (bf16[8,5888]{1,0:T(8,128)(2,1)}, bf16[8,5888]{1,0:T(8,128)(2,1)S(1)}, u32[]{:S(2)}, u32[]{:S(2)}) collective-permute-start(bf16[8,5888]{1,0:T(8,128)(2,1)} %get-tuple-element.40), channel_id=1, source_target_pairs={{0,18},{2,16},{4,22},{6,20},{8,26},{10,24},{12,30},{14,28},{16,2},... | collective-permute-start | bytes 282632 | tf_op jit(solution)/shard_map/ppermute | solution.py:621
  42.1 17.0 %collective-permute-start.9 = (bf16[8,5888]{1,0:T(8,128)(2,1)}, bf16[8,5888]{1,0:T(8,128)(2,1)S(1)}, u32[]{:S(2)}, u32[]{:S(2)}) collective-permute-start(bf16[8,5888]{1,0:T(8,128)(2,1)} %get-tuple-element.41), channel_id=1, source_target_pairs={{0,20},{2,22},{4,16},{6,18},{8,28},{10,30},{12,24},{14,26},{16,4},... | collective-permute-start | bytes 282632 | tf_op jit(solution)/shard_map/ppermute | solution.py:621
  43.2 17.2 %collective-permute-start.10 = (bf16[8,5888]{1,0:T(8,128)(2,1)}, bf16[8,5888]{1,0:T(8,128)(2,1)S(1)}, u32[]{:S(2)}, u32[]{:S(2)}) collective-permute-start(bf16[8,5888]{1,0:T(8,128)(2,1)} %get-tuple-element.42), channel_id=1, source_target_pairs={{0,22},{2,20},{4,18},{6,16},{8,30},{10,28},{12,26},{14,24},{16,6},... | collective-permute-start | bytes 282632 | tf_op jit(solution)/shard_map/ppermute | solution.py:621
  47.2 42.6 %collective-permute-start.16 = (bf16[256,1408]{1,0:T(8,128)(2,1)S(1)}, bf16[256,1408]{1,0:T(8,128)(2,1)S(1)}, u32[]{:S(2)}, u32[]{:S(2)}) collective-permute-start(bf16[256,1408]{1,0:T(8,128)(2,1)S(1)} %bitcast.21), channel_id=1, source_target_pairs={{0,1},{1,0},{2,3},{3,2},{4,5},{5,4},{6,7},{7,6},{8,9},{9,8},{10,11... | collective-permute-start | bytes 2162696 | tf_op jit(solution)/shard_map/ppermute | solution.py:599
  50.3 18.1 %collective-permute-start.11 = (bf16[8,5888]{1,0:T(8,128)(2,1)}, bf16[8,5888]{1,0:T(8,128)(2,1)S(1)}, u32[]{:S(2)}, u32[]{:S(2)}) collective-permute-start(bf16[8,5888]{1,0:T(8,128)(2,1)} %get-tuple-element.43), channel_id=1, source_target_pairs={{0,24},{2,26},{4,28},{6,30},{8,16},{10,18},{12,20},{14,22},{16,8},... | collective-permute-start | bytes 282632 | tf_op jit(solution)/shard_map/ppermute | solution.py:621
  56.4 17.8 %collective-permute-start.12 = (bf16[8,5888]{1,0:T(8,128)(2,1)}, bf16[8,5888]{1,0:T(8,128)(2,1)S(1)}, u32[]{:S(2)}, u32[]{:S(2)}) collective-permute-start(bf16[8,5888]{1,0:T(8,128)(2,1)} %get-tuple-element.44), channel_id=1, source_target_pairs={{0,26},{2,24},{4,30},{6,28},{8,18},{10,16},{12,22},{14,20},{16,10}... | collective-permute-start | bytes 282632 | tf_op jit(solution)/shard_map/ppermute | solution.py:621
  59.0 16.6 %collective-permute-start.13 = (bf16[8,5888]{1,0:T(8,128)(2,1)}, bf16[8,5888]{1,0:T(8,128)(2,1)S(1)}, u32[]{:S(2)}, u32[]{:S(2)}) collective-permute-start(bf16[8,5888]{1,0:T(8,128)(2,1)} %get-tuple-element.45), channel_id=1, source_target_pairs={{0,28},{2,30},{4,24},{6,26},{8,20},{10,22},{12,16},{14,18},{16,12}... | collective-permute-start | bytes 282632 | tf_op jit(solution)/shard_map/ppermute | solution.py:621
  60.5 17.4 %collective-permute-start.14 = (bf16[8,5888]{1,0:T(8,128)(2,1)}, bf16[8,5888]{1,0:T(8,128)(2,1)S(1)}, u32[]{:S(2)}, u32[]{:S(2)}) collective-permute-start(bf16[8,5888]{1,0:T(8,128)(2,1)} %get-tuple-element.46), channel_id=1, source_target_pairs={{0,30},{2,28},{4,26},{6,24},{8,22},{10,20},{12,18},{14,16},{16,14}... | collective-permute-start | bytes 282632 | tf_op jit(solution)/shard_map/ppermute | solution.py:621
  77.9 0.9 copy-start.4
  83.9 19.9 %collective-permute-start.17 = (bf16[128,1408]{1,0:T(8,128)(2,1)S(1)}, bf16[128,1408]{1,0:T(8,128)(2,1)S(1)}, u32[]{:S(2)}, u32[]{:S(2)}) collective-permute-start(bf16[128,1408]{1,0:T(8,128)(2,1)S(1)} %bitcast.18), channel_id=1, source_target_pairs={{0,1},{1,0},{2,3},{3,2},{4,5},{5,4},{6,7},{7,6},{8,9},{9,8},{10,11... | collective-permute-start | bytes 1081352 | tf_op jit(solution)/shard_map/ppermute | solution.py:599
  85.1 16.4 %collective-permute-start.15 = (bf16[128,1408]{1,0:T(8,128)(2,1)S(1)}, bf16[128,1408]{1,0:T(8,128)(2,1)S(1)}, u32[]{:S(2)}, u32[]{:S(2)}) collective-permute-start(bf16[128,1408]{1,0:T(8,128)(2,1)S(1)} %bitcast.19), channel_id=1, source_target_pairs={{0,1},{1,0},{2,3},{3,2},{4,5},{5,4},{6,7},{7,6},{8,9},{9,8},{10,11... | collective-permute-start | bytes 1081352 | tf_op jit(solution)/shard_map/ppermute | solution.py:599
  85.4 4.4 %copy-start = (bf16[2,128,2816]{2,1,0:T(8,128)(2,1)S(1)}, bf16[2,128,2816]{2,1,0:T(8,128)(2,1)}, u32[]{:S(2)}) copy-start(bf16[2,128,2816]{2,1,0:T(8,128)(2,1)} %gate_ref.5) | copy-start | bytes 4325380
  85.4 4.4 %copy-start.1 = (bf16[2,128,2816]{2,1,0:T(8,128)(2,1)S(1)}, bf16[2,128,2816]{2,1,0:T(8,128)(2,1)}, u32[]{:S(2)}) copy-start(bf16[2,128,2816]{2,1,0:T(8,128)(2,1)} %up_ref.5) | copy-start | bytes 4325380
  85.4 4.4 %copy-start.2 = (s32[1,2688]{1,0:T(1,128)S(1)}, s32[1,2688]{1,0:T(1,128)}, u32[]{:S(2)}) copy-start(s32[1,2688]{1,0:T(1,128)} %get-tuple-element.50.far_ids_ref.ids_ref) | copy-start | bytes 32260

commit v5 on v4

--- a/solution.py
+++ b/solution.py
@@ -44,7 +44,12 @@
         parts.append(jnp.where(key_ref[line, :] == slot, within_ref[line, :], 0).astype(F32))
     row_of = jnp.sum(jnp.concatenate(parts, axis=0), axis=1, keepdims=True).astype(I32)
     pick = (iota((blocks * cap, rows), 1) == row_of).astype(F32).astype(BF16)
-    return pick, count_of(table, row_of + me * rows)
+    own = count_of(table, iota((rows, 1), 0) + me * rows)
+    high = jnp.floor(own * (1.0 / 64.0))
+    low = own - high * 64.0
+    spread = [jnp.broadcast_to(part, (rows, 128)).astype(BF16) for part in (high, low)]
+    high, low = [jnp.dot(pick, part, preferred_element_type=F32)[:, :1] for part in spread]
+    return pick, high * 64.0 + low, own
 
 
 def land_matrix(mine, blocks, cap):
@@ -124,7 +129,7 @@
     me = lax.axis_index("section")
     targets = [me ^ p for p in range(map_ref.shape[0])]
     map_load.wait()
-    pick, count = pick_matrix(map_ref[...], me, cap, key_ref, within_ref, targets)
+    pick, count, _ = pick_matrix(map_ref[...], me, cap, key_ref, within_ref, targets)
     parts = [
         (loads[0], in_ref.at[0, :, pl.ds(0, narrow)], 0),
         (loads[1], in_ref.at[0, :, pl.ds(narrow, narrow)], narrow),
@@ -241,8 +246,8 @@
     me = lax.axis_index("section")
     table = table_ref[...]
     column_plan(narrow, map_ref, near_ref, send_ref, far_ref, splits)
-    scale = 1.0 / count_of(table, iota((rows, 1), 0) + me * rows)
-    pick, count = pick_matrix(table, me, cap, key_ref, within_ref, list(range(table.shape[0])))
+    pick, count, own = pick_matrix(table, me, cap, key_ref, within_ref, list(range(table.shape[0])))
+    scale = 1.0 / own
     parts = [
         (loads[0], in_ref.at[0, :, pl.ds(0, narrow)], 0),
         (loads[1], in_ref.at[0, :, pl.ds(narrow, sent_ref.shape[1] - narrow)], narrow),

time: 109 us -> 109 us (level)
  no operation moved by 1% of the time
where the time goes in v5:
time: 109 us; the launch traced here: 108 us
  starting transfers between devices  38.6 us (35%)
  Pallas kernels  34.5 us (32%)
  waiting for transfers between devices  32.6 us (30%)
    ppermute x15, waiting for transfers between devices, cross(): return lax.ppermute(sent, 'section', [(i, i ^ p) for i in range(blocks)])  30.5 us
    ppermute x15, starting transfers between devices, cross(): return lax.ppermute(sent, 'section', [(i, i ^ p) for i in range(blocks)])  29.2 us
    pallas_call x1, Pallas kernels, first_half(): pl.pallas_call(first_kernel, out_shape=(out_type, out_type), in_specs=[VM...  9.5 us
    all_to_all x1, starting transfers between devices, swap_rows(): lax.all_to_all(sent, 'section', split_axis=0, concat_axis=0, tiled=True)  6.67 us
    pallas_call x1, Pallas kernels, middle(): pl.pallas_call(functools.partial(middle_kernel, cap, splits), out_shape=(...  6.09 us
    pallas_call x1, Pallas kernels, arrive_rows(): pl.pallas_call(arrive_kernel, out_shape=(jax.ShapeDtypeStruct((2 * rows,...  5.03 us
    pallas_call x2, Pallas kernels, second_half(): pl.pallas_call(functools.partial(second_kernel, bool(rests)), out_shape=j...  4.59 us
    pallas_call x1, Pallas kernels, near_columns(): pl.pallas_call(near_kernel, out_shape=jax.ShapeDtypeStruct((count, extra)...  4.4 us
  transfers between devices with their start and end apart: 19, of which 12 were waited for; matrix products, arithmetic and copies ran while one was open for 0% of the time, Pallas kernels for 25%

profile of v5, /device:TPU:13, one launch (start us, length us, event | category | flops | bytes accessed | tf_op | source)
XLA Modules:
  0.0 107.7 jit_solution(10319608873966151944)
XLA Ops:
  0.6 0.0 copy-start.3
  0.6 6.1 %middle.1 = (bf16[1,256,1408]{2,1,0:T(8,128)(2,1)}, s32[1,2688]{1,0:T(1,128)}, s32[1,1408]{1,0:T(1,128)}, s32[1,2688]{1,0:T(1,128)}, bf16[128,5376]{1,0:T(8,128)(2,1)}) custom-call(s32[16,128]{1,0:T(8,128)} %bitcast.13, s32[42,128]{1,0:T(8,128)} %bitcast.22, bf16[2,128,2816]{2,1,0:T(8,128)(2,1)} %gate_ref.5, bf16[2,128,2816]{2,1,0:T(8,128)(2,1)} %up_ref.5), custom_call_target="tpu_custom_call" | custom-call | flops 2030043136 | bytes 5767168 | tf_op jit(solution)/shard_map/middle/pallas_call | solution.py:270
  6.7 0.0 copy-start.7
  6.7 0.0 copy-start.6
  6.8 6.7 %all-to-all-start = ((bf16[16,8,5376]{2,1,0:T(8,128)(2,1)}), bf16[16,8,5376]{2,1,0:T(8,128)(2,1)S(1)}, u32[]{:S(2)}, u32[]{:S(2)}) async-start(bf16[16,8,5376]{2,1,0:T(8,128)(2,1)} %bitcast.20), calls=%async_computation | async-start | bytes 2752512 | tf_op jit(solution)/shard_map/all_to_all | solution.py:623
  13.4 0.0 copy-start.5
  13.4 3.4 %send_rows.1 = (bf16[8,5888]{1,0:T(8,128)(2,1)}, bf16[8,5888]{1,0:T(8,128)(2,1)}, bf16[8,5888]{1,0:T(8,128)(2,1)}, bf16[8,5888]{1,0:T(8,128)(2,1)}, bf16[8,5888]...) custom-call(s32[16,128]{1,0:T(8,128)} %bitcast.14, ...), custom_call_target="tpu_custom_call" | custom-call | flops 184549376 | bytes 2883584 | tf_op jit(solution)/shard_map/send_rows/pallas_call | solution.py:145
  16.8 0.5 collective-permute-start
  17.3 0.3 collective-permute-start.1
  17.6 1.5 %collective-permute-start.2 = (bf16[8,5888]{1,0:T(8,128)(2,1)}, bf16[8,5888]{1,0:T(8,128)(2,1)S(1)}, u32[]{:S(2)}, u32[]{:S(2)}) collective-permute-start(bf16[8,5888]{1,0:T(8,128)(2,1)} %get-tuple-element.34), channel_id=1, source_target_pairs={{0,6},{2,4},{4,2},{6,0},{8,14},{10,12},{12,10},{14,8},{16,22},{18,... | collective-permute-start | bytes 282632 | tf_op jit(solution)/shard_map/ppermute | solution.py:626
  19.0 0.3 collective-permute-start.3
  19.3 1.5 %collective-permute-start.4 = (bf16[8,5888]{1,0:T(8,128)(2,1)}, bf16[8,5888]{1,0:T(8,128)(2,1)S(1)}, u32[]{:S(2)}, u32[]{:S(2)}) collective-permute-start(bf16[8,5888]{1,0:T(8,128)(2,1)} %get-tuple-element.36), channel_id=1, source_target_pairs={{0,10},{2,8},{4,14},{6,12},{8,2},{10,0},{12,6},{14,4},{16,26},{18,... | collective-permute-start | bytes 282632 | tf_op jit(solution)/shard_map/ppermute | solution.py:626
  20.8 0.0 collective-permute-done.refs_1_
  20.8 0.0 collective-permute-start.5
  20.8 1.6 %collective-permute-done.1.refs_2_ = bf16[8,5888]{1,0:T(8,128)(2,1)S(1)} collective-permute-done((bf16[8,5888]{1,0:T(8,128)(2,1)}, bf16[8,5888]{1,0:T(8,128)(2,1)S(1)}, u32[]{:S(2)}, u32[]{:S(2)}) %collective-permute-start.1) | collective-permute-done | bytes 94240 | tf_op jit(solution)/shard_map/ppermute | solution.py:626
  22.4 5.5 %collective-permute-start.6 = (bf16[8,5888]{1,0:T(8,128)(2,1)}, bf16[8,5888]{1,0:T(8,128)(2,1)S(1)}, u32[]{:S(2)}, u32[]{:S(2)}) collective-permute-start(bf16[8,5888]{1,0:T(8,128)(2,1)} %get-tuple-element.38), channel_id=1, source_target_pairs={{0,14},{2,12},{4,10},{6,8},{8,6},{10,4},{12,2},{14,0},{16,30},{18,... | collective-permute-start | bytes 282632 | tf_op jit(solution)/shard_map/ppermute | solution.py:626
  27.9 0.0 collective-permute-done.2.refs_3_
  27.9 2.9 %collective-permute-start.7 = (bf16[8,5888]{1,0:T(8,128)(2,1)}, bf16[8,5888]{1,0:T(8,128)(2,1)S(1)}, u32[]{:S(2)}, u32[]{:S(2)}) collective-permute-start(bf16[8,5888]{1,0:T(8,128)(2,1)} %get-tuple-element.39), channel_id=1, source_target_pairs={{0,16},{2,18},{4,20},{6,22},{8,24},{10,26},{12,28},{14,30},{16,0},... | collective-permute-start | bytes 282632 | tf_op jit(solution)/shard_map/ppermute | solution.py:626
  30.8 8.1 %collective-permute-done.3.refs_4_ = bf16[8,5888]{1,0:T(8,128)(2,1)S(1)} collective-permute-done((bf16[8,5888]{1,0:T(8,128)(2,1)}, bf16[8,5888]{1,0:T(8,128)(2,1)S(1)}, u32[]{:S(2)}, u32[]{:S(2)}) %collective-permute-start.3) | collective-permute-done | bytes 94240 | tf_op jit(solution)/shard_map/ppermute | solution.py:626
  38.9 2.6 %collective-permute-start.8 = (bf16[8,5888]{1,0:T(8,128)(2,1)}, bf16[8,5888]{1,0:T(8,128)(2,1)S(1)}, u32[]{:S(2)}, u32[]{:S(2)}) collective-permute-start(bf16[8,5888]{1,0:T(8,128)(2,1)} %get-tuple-element.40), channel_id=1, source_target_pairs={{0,18},{2,16},{4,22},{6,20},{8,26},{10,24},{12,30},{14,28},{16,2},... | collective-permute-start | bytes 282632 | tf_op jit(solution)/shard_map/ppermute | solution.py:626
  41.5 0.6 collective-permute-done.4.refs_5_
  42.1 0.2 collective-permute-start.9
  42.2 1.0 collective-permute-done.5.refs_6_
  43.2 3.9 %collective-permute-start.10 = (bf16[8,5888]{1,0:T(8,128)(2,1)}, bf16[8,5888]{1,0:T(8,128)(2,1)S(1)}, u32[]{:S(2)}, u32[]{:S(2)}) collective-permute-start(bf16[8,5888]{1,0:T(8,128)(2,1)} %get-tuple-element.42), channel_id=1, source_target_pairs={{0,22},{2,20},{4,18},{6,16},{8,30},{10,28},{12,26},{14,24},{16,6},... | collective-permute-start | bytes 282632 | tf_op jit(solution)/shard_map/ppermute | solution.py:626
  47.2 0.0 collective-permute-done.6.refs_7_
  47.2 0.0 copy-done.7
  47.2 1.2 %collective-permute-start.16 = (bf16[256,1408]{1,0:T(8,128)(2,1)S(1)}, bf16[256,1408]{1,0:T(8,128)(2,1)S(1)}, u32[]{:S(2)}, u32[]{:S(2)}) collective-permute-start(bf16[256,1408]{1,0:T(8,128)(2,1)S(1)} %bitcast.21), channel_id=1, source_target_pairs={{0,1},{1,0},{2,3},{3,2},{4,5},{5,4},{6,7},{7,6},{8,9},{9,8},{10,11... | collective-permute-start | bytes 2162696 | tf_op jit(solution)/shard_map/ppermute | solution.py:604
  48.4 1.9 %collective-permute-done.7.refs_8_ = bf16[8,5888]{1,0:T(8,128)(2,1)S(1)} collective-permute-done((bf16[8,5888]{1,0:T(8,128)(2,1)}, bf16[8,5888]{1,0:T(8,128)(2,1)S(1)}, u32[]{:S(2)}, u32[]{:S(2)}) %collective-permute-start.7) | collective-permute-done | bytes 94240 | tf_op jit(solution)/shard_map/ppermute | solution.py:626
  50.3 0.0 collective-permute-start.11
  50.3 6.2 %collective-permute-done.8.refs_9_ = bf16[8,5888]{1,0:T(8,128)(2,1)S(1)} collective-permute-done((bf16[8,5888]{1,0:T(8,128)(2,1)}, bf16[8,5888]{1,0:T(8,128)(2,1)S(1)}, u32[]{:S(2)}, u32[]{:S(2)}) %collective-permute-start.8) | collective-permute-done | bytes 94240 | tf_op jit(solution)/shard_map/ppermute | solution.py:626
  56.5 2.6 %collective-permute-start.12 = (bf16[8,5888]{1,0:T(8,128)(2,1)}, bf16[8,5888]{1,0:T(8,128)(2,1)S(1)}, u32[]{:S(2)}, u32[]{:S(2)}) collective-permute-start(bf16[8,5888]{1,0:T(8,128)(2,1)} %get-tuple-element.44), channel_id=1, source_target_pairs={{0,26},{2,24},{4,30},{6,28},{8,18},{10,16},{12,22},{14,20},{16,10}... | collective-permute-start | bytes 282632 | tf_op jit(solution)/shard_map/ppermute | solution.py:626
  59.0 0.0 collective-permute-done.9.refs_10_
  59.0 0.8 collective-permute-start.13
  59.9 0.6 collective-permute-done.10.refs_11_
  60.5 6.7 %collective-permute-start.14 = (bf16[8,5888]{1,0:T(8,128)(2,1)}, bf16[8,5888]{1,0:T(8,128)(2,1)S(1)}, u32[]{:S(2)}, u32[]{:S(2)}) collective-permute-start(bf16[8,5888]{1,0:T(8,128)(2,1)} %get-tuple-element.46), channel_id=1, source_target_pairs={{0,30},{2,28},{4,26},{6,24},{8,22},{10,20},{12,18},{14,16},{16,14}... | collective-permute-start | bytes 282632 | tf_op jit(solution)/shard_map/ppermute | solution.py:626
  67.2 0.0 copy-done.3
  67.2 0.2 land_rows.1.land_ref
  67.4 0.9 collective-permute-done.11.refs_12_
  68.3 5.9 %collective-permute-done.12.refs_13_ = bf16[8,5888]{1,0:T(8,128)(2,1)S(1)} collective-permute-done((bf16[8,5888]{1,0:T(8,128)(2,1)}, bf16[8,5888]{1,0:T(8,128)(2,1)S(1)}, u32[]{:S(2)}, u32[]{:S(2)}) %collective-permute-start.12) | collective-permute-done | bytes 94240 | tf_op jit(solution)/shard_map/ppermute | solution.py:626
  74.2 1.4 %collective-permute-done.13.refs_14_ = bf16[8,5888]{1,0:T(8,128)(2,1)S(1)} collective-permute-done((bf16[8,5888]{1,0:T(8,128)(2,1)}, bf16[8,5888]{1,0:T(8,128)(2,1)S(1)}, u32[]{:S(2)}, u32[]{:S(2)}) %collective-permute-start.13) | collective-permute-done | bytes 94240 | tf_op jit(solution)/shard_map/ppermute | solution.py:626
  75.6 2.3 %collective-permute-done.14.refs_15_ = bf16[8,5888]{1,0:T(8,128)(2,1)S(1)} collective-permute-done((bf16[8,5888]{1,0:T(8,128)(2,1)}, bf16[8,5888]{1,0:T(8,128)(2,1)S(1)}, u32[]{:S(2)}, u32[]{:S(2)}) %collective-permute-start.14) | collective-permute-done | bytes 94240 | tf_op jit(solution)/shard_map/ppermute | solution.py:626
  77.9 0.0 copy-done.6
  77.9 0.0 copy-start.4
  77.9 0.9 copy-done.4
  78.8 5.0 %arrive_rows.1 = (bf16[256,2816]{1,0:T(8,128)(2,1)S(1)}, bf16[128,256]{1,0:T(8,128)(2,1)S(1)}, bf16[1,128,1408]{2,1,0:T(8,128)(2,1)S(1)}, bf16[1,128,1408]{2,1,0:T(8,128)(2,1)S(1)}) custom-call(bf16[128,128]{1,0:T(8,128)(2,1)S(1)} %land_rows.1.land_ref, s32[1,1408]{1,0:T(1,128)S(1)} %copy-done.6, bf16[8,5888]{1,0:T(8,128)(2,1)S(1)} %copy-done.4, ...), custom_call_target="tpu_custom_call" | custom-call | flops 2030043136 | bytes 2883584 | tf_op jit(solution)/shard_map/arrive_rows/pallas_call | solution.py:349
  83.9 1.3 %collective-permute-start.17 = (bf16[128,1408]{1,0:T(8,128)(2,1)S(1)}, bf16[128,1408]{1,0:T(8,128)(2,1)S(1)}, u32[]{:S(2)}, u32[]{:S(2)}) collective-permute-start(bf16[128,1408]{1,0:T(8,128)(2,1)S(1)} %bitcast.18), channel_id=1, source_target_pairs={{0,1},{1,0},{2,3},{3,2},{4,5},{5,4},{6,7},{7,6},{8,9},{9,8},{10,11... | collective-permute-start | bytes 1081352 | tf_op jit(solution)/shard_map/ppermute | solution.py:604
  85.1 0.3 collective-permute-start.15
  85.4 0.0 copy-done.5
  85.4 0.0 copy-start
  85.4 0.0 copy-start.1
  85.4 0.0 copy-start.2
  85.4 4.4 %shard_map.59.near_ref = bf16[256,2688]{1,0:T(8,128)(2,1)S(1)} custom-call(bf16[256,2816]{1,0:T(8,128)(2,1)S(1)} %get-tuple-element.47.rows_ref, s32[1,2688]{1,0:T(1,128)S(1)} %copy-done.5), custom_call_target="tpu_custom_call" | custom-call | flops 3875536896 | bytes 2818048 | tf_op jit(solution)/shard_map/pallas_call | solution.py:383
  89.8 0.0 collective-permute-done.16
  89.8 0.0 copy-done
  89.8 0.0 copy-done.1
  89.8 0.0 copy-done.2
  89.8 9.5 %first_half.1 = (bf16[2,2,128,5504]{3,2,1,0:T(8,128)(2,1)}, bf16[2,2,128,5504]{3,2,1,0:T(8,128)(2,1)}) custom-call(s32[16,128]{1,0:T(8,128)S(1)} %bitcast.16, s32[1,2688]{1,0:T(1,128)S(1)} %copy-done.5, bf16[1,256,1408]{2,1,0:T(8,128)(2,1)S(1)} %bitcast.17, s32[1,2688]{1,0:T(1,128)S(1)} %copy-done.2, bf16[2,128,2816]{2,1,0:T(8,128)(2,1)S(1)} %copy-done, ...), custom_call_target="tpu_custom_call" | custom-call | flops 5813305344 | bytes 11272192 | tf_op jit(solution)/shard_map/first_half/pallas_call | solution.py:467
  99.4 2.2 %collective-permute-done.15 = bf16[128,1408]{1,0:T(8,128)(2,1)S(1)} collective-permute-done((bf16[128,1408]{1,0:T(8,128)(2,1)S(1)}, bf16[128,1408]{1,0:T(8,128)(2,1)S(1)}, u32[]{:S(2)}, u32[]{:S(2)}) %collective-permute-start.15) | collective-permute-done | bytes 360480 | tf_op jit(solution)/shard_map/ppermute | solution.py:604
  101.5 2.3 %shard_map.60.gate_in = bf16[2,2,128,5504]{3,2,1,0:T(8,128)(2,1)} custom-call(bf16[256,2816]{1,0:T(8,128)(2,1)S(1)} %get-tuple-element.47.rows_ref, bf16[256,2688]{1,0:T(8,128)(2,1)S(1)} %shard_map.59.near_ref, bf16[1,128,1408]{2,1,0:T(8,128)(2,1)S(1)} %bitcast.12, s32[1,2688]{1,0:T(1,128)S(1)} %copy-done.2, ...), custom_call_target="tpu_custom_call", output_to_operand_aliasing={{}: (4, {})} | custom-call | flops 968884224 | bytes 4194304 | tf_op jit(solution)/shard_map/pallas_call | solution.py:522
  103.8 0.0 collective-permute-done.17
  103.8 2.3 %shard_map.61.up_in = bf16[2,2,128,5504]{3,2,1,0:T(8,128)(2,1)} custom-call(bf16[256,2816]{1,0:T(8,128)(2,1)S(1)} %get-tuple-element.47.rows_ref, bf16[256,2688]{1,0:T(8,128)(2,1)S(1)} %shard_map.59.near_ref, bf16[1,128,1408]{2,1,0:T(8,128)(2,1)S(1)} %bitcast.11, s32[1,2688]{1,0:T(1,128)S(1)} %copy-done.2, ...), custom_call_target="tpu_custom_call", output_to_operand_aliasing={{}: (5, {})} | custom-call | flops 968884224 | bytes 4194304 | tf_op jit(solution)/shard_map/pallas_call | solution.py:522
  106.1 0.0 all-to-all-done
  106.1 1.3 %last_rows.1 = (bf16[2,2,128,5504]{3,2,1,0:T(8,128)(2,1)}, bf16[2,2,128,5504]{3,2,1,0:T(8,128)(2,1)}) custom-call(bf16[128,128]{1,0:T(8,128)(2,1)S(1)} %land_rows.1.land_ref, bf16[128,5376]{1,0:T(8,128)(2,1)S(1)} %bitcast.10, bf16[2,2,128,5504]{3,2,1,0:T(8,128)(2,1)} %shard_map.60.gate_in, ...), custom_call_target="tpu_custom_call", output_to_operand_aliasing={{0}: (2, {}), {1}: (3, {})} | custom-call | flops 176160768 | bytes 2752512 | tf_op jit(solution)/shard_map/last_rows/pallas_call | solution.py:581
Async XLA Ops:
  0.6 66.6 %copy-start.3 = (s32[2048]{0:T(1024)S(1)}, s32[2048]{0:T(1024)}, u32[]{:S(2)}) copy-start(s32[2048]{0:T(1024)} %param.6) | copy-start | bytes 24580
  6.7 40.4 %copy-start.7 = (bf16[1,256,1408]{2,1,0:T(8,128)(2,1)S(1)}, bf16[1,256,1408]{2,1,0:T(8,128)(2,1)}, u32[]{:S(2)}) copy-start(bf16[1,256,1408]{2,1,0:T(8,128)(2,1)} %get-tuple-element.51) | copy-start | bytes 2162692
  6.7 71.2 %copy-start.6 = (s32[1,1408]{1,0:T(1,128)S(1)}, s32[1,1408]{1,0:T(1,128)}, u32[]{:S(2)}) copy-start(s32[1,1408]{1,0:T(1,128)} %get-tuple-element.30.ids_ref) | copy-start | bytes 16900
  6.8 99.4 %all-to-all-start = ((bf16[16,8,5376]{2,1,0:T(8,128)(2,1)}), bf16[16,8,5376]{2,1,0:T(8,128)(2,1)S(1)}, u32[]{:S(2)}, u32[]{:S(2)}) async-start(bf16[16,8,5376]{2,1,0:T(8,128)(2,1)} %bitcast.20), calls=%async_computation | async-start | bytes 2752512 | tf_op jit(solution)/shard_map/all_to_all | solution.py:623
  13.4 72.0 %copy-start.5 = (s32[1,2688]{1,0:T(1,128)S(1)}, s32[1,2688]{1,0:T(1,128)}, u32[]{:S(2)}) copy-start(s32[1,2688]{1,0:T(1,128)} %get-tuple-element.48.ids_ref.near_ids_ref) | copy-start | bytes 32260
  16.8 4.0 %collective-permute-start = (bf16[8,5888]{1,0:T(8,128)(2,1)}, bf16[8,5888]{1,0:T(8,128)(2,1)S(1)}, u32[]{:S(2)}, u32[]{:S(2)}) collective-permute-start(bf16[8,5888]{1,0:T(8,128)(2,1)} %get-tuple-element.32), channel_id=1, source_target_pairs={{0,2},{2,0},{4,6},{6,4},{8,10},{10,8},{12,14},{14,12},{16,18},{18,... | collective-permute-start | bytes 282632 | tf_op jit(solution)/shard_map/ppermute | solution.py:626
  17.3 5.1 %collective-permute-start.1 = (bf16[8,5888]{1,0:T(8,128)(2,1)}, bf16[8,5888]{1,0:T(8,128)(2,1)S(1)}, u32[]{:S(2)}, u32[]{:S(2)}) collective-permute-start(bf16[8,5888]{1,0:T(8,128)(2,1)} %get-tuple-element.33), channel_id=1, source_target_pairs={{0,4},{2,6},{4,0},{6,2},{8,12},{10,14},{12,8},{14,10},{16,20},{18,... | collective-permute-start | bytes 282632 | tf_op jit(solution)/shard_map/ppermute | solution.py:626
  17.6 10.3 %collective-permute-start.2 = (bf16[8,5888]{1,0:T(8,128)(2,1)}, bf16[8,5888]{1,0:T(8,128)(2,1)S(1)}, u32[]{:S(2)}, u32[]{:S(2)}) collective-permute-start(bf16[8,5888]{1,0:T(8,128)(2,1)} %get-tuple-element.34), channel_id=1, source_target_pairs={{0,6},{2,4},{4,2},{6,0},{8,14},{10,12},{12,10},{14,8},{16,22},{18,... | collective-permute-start | bytes 282632 | tf_op jit(solution)/shard_map/ppermute | solution.py:626
  19.0 19.9 %collective-permute-start.3 = (bf16[8,5888]{1,0:T(8,128)(2,1)}, bf16[8,5888]{1,0:T(8,128)(2,1)S(1)}, u32[]{:S(2)}, u32[]{:S(2)}) collective-permute-start(bf16[8,5888]{1,0:T(8,128)(2,1)} %get-tuple-element.35), channel_id=1, source_target_pairs={{0,8},{2,10},{4,12},{6,14},{8,0},{10,2},{12,4},{14,6},{16,24},{18,... | collective-permute-start | bytes 282632 | tf_op jit(solution)/shard_map/ppermute | solution.py:626
  19.3 22.7 %collective-permute-start.4 = (bf16[8,5888]{1,0:T(8,128)(2,1)}, bf16[8,5888]{1,0:T(8,128)(2,1)S(1)}, u32[]{:S(2)}, u32[]{:S(2)}) collective-permute-start(bf16[8,5888]{1,0:T(8,128)(2,1)} %get-tuple-element.36), channel_id=1, source_target_pairs={{0,10},{2,8},{4,14},{6,12},{8,2},{10,0},{12,6},{14,4},{16,26},{18,... | collective-permute-start | bytes 282632 | tf_op jit(solution)/shard_map/ppermute | solution.py:626
  20.8 22.5 %collective-permute-start.5 = (bf16[8,5888]{1,0:T(8,128)(2,1)}, bf16[8,5888]{1,0:T(8,128)(2,1)S(1)}, u32[]{:S(2)}, u32[]{:S(2)}) collective-permute-start(bf16[8,5888]{1,0:T(8,128)(2,1)} %get-tuple-element.37), channel_id=1, source_target_pairs={{0,12},{2,14},{4,8},{6,10},{8,4},{10,6},{12,0},{14,2},{16,28},{18,... | collective-permute-start | bytes 282632 | tf_op jit(solution)/shard_map/ppermute | solution.py:626
  22.4 24.8 %collective-permute-start.6 = (bf16[8,5888]{1,0:T(8,128)(2,1)}, bf16[8,5888]{1,0:T(8,128)(2,1)S(1)}, u32[]{:S(2)}, u32[]{:S(2)}) collective-permute-start(bf16[8,5888]{1,0:T(8,128)(2,1)} %get-tuple-element.38), channel_id=1, source_target_pairs={{0,14},{2,12},{4,10},{6,8},{8,6},{10,4},{12,2},{14,0},{16,30},{18,... | collective-permute-start | bytes 282632 | tf_op jit(solution)/shard_map/ppermute | solution.py:626
  27.9 22.4 %collective-permute-start.7 = (bf16[8,5888]{1,0:T(8,128)(2,1)}, bf16[8,5888]{1,0:T(8,128)(2,1)S(1)}, u32[]{:S(2)}, u32[]{:S(2)}) collective-permute-start(bf16[8,5888]{1,0:T(8,128)(2,1)} %get-tuple-element.39), channel_id=1, source_target_pairs={{0,16},{2,18},{4,20},{6,22},{8,24},{10,26},{12,28},{14,30},{16,0},... | collective-permute-start | bytes 282632 | tf_op jit(solution)/shard_map/ppermute | solution.py:626
  38.9 17.6 %collective-permute-start.8 = (bf16[8,5888]{1,0:T(8,128)(2,1)}, bf16[8,5888]{1,0:T(8,128)(2,1)S(1)}, u32[]{:S(2)}, u32[]{:S(2)}) collective-permute-start(bf16[8,5888]{1,0:T(8,128)(2,1)} %get-tuple-element.40), channel_id=1, source_target_pairs={{0,18},{2,16},{4,22},{6,20},{8,26},{10,24},{12,30},{14,28},{16,2},... | collective-permute-start | bytes 282632 | tf_op jit(solution)/shard_map/ppermute | solution.py:626
  42.1 17.0 %collective-permute-start.9 = (bf16[8,5888]{1,0:T(8,128)(2,1)}, bf16[8,5888]{1,0:T(8,128)(2,1)S(1)}, u32[]{:S(2)}, u32[]{:S(2)}) collective-permute-start(bf16[8,5888]{1,0:T(8,128)(2,1)} %get-tuple-element.41), channel_id=1, source_target_pairs={{0,20},{2,22},{4,16},{6,18},{8,28},{10,30},{12,24},{14,26},{16,4},... | collective-permute-start | bytes 282632 | tf_op jit(solution)/shard_map/ppermute | solution.py:626
  43.2 17.2 %collective-permute-start.10 = (bf16[8,5888]{1,0:T(8,128)(2,1)}, bf16[8,5888]{1,0:T(8,128)(2,1)S(1)}, u32[]{:S(2)}, u32[]{:S(2)}) collective-permute-start(bf16[8,5888]{1,0:T(8,128)(2,1)} %get-tuple-element.42), channel_id=1, source_target_pairs={{0,22},{2,20},{4,18},{6,16},{8,30},{10,28},{12,26},{14,24},{16,6},... | collective-permute-start | bytes 282632 | tf_op jit(solution)/shard_map/ppermute | solution.py:626
  47.2 42.6 %collective-permute-start.16 = (bf16[256,1408]{1,0:T(8,128)(2,1)S(1)}, bf16[256,1408]{1,0:T(8,128)(2,1)S(1)}, u32[]{:S(2)}, u32[]{:S(2)}) collective-permute-start(bf16[256,1408]{1,0:T(8,128)(2,1)S(1)} %bitcast.21), channel_id=1, source_target_pairs={{0,1},{1,0},{2,3},{3,2},{4,5},{5,4},{6,7},{7,6},{8,9},{9,8},{10,11... | collective-permute-start | bytes 2162696 | tf_op jit(solution)/shard_map/ppermute | solution.py:604
  50.3 18.1 %collective-permute-start.11 = (bf16[8,5888]{1,0:T(8,128)(2,1)}, bf16[8,5888]{1,0:T(8,128)(2,1)S(1)}, u32[]{:S(2)}, u32[]{:S(2)}) collective-permute-start(bf16[8,5888]{1,0:T(8,128)(2,1)} %get-tuple-element.43), channel_id=1, source_target_pairs={{0,24},{2,26},{4,28},{6,30},{8,16},{10,18},{12,20},{14,22},{16,8},... | collective-permute-start | bytes 282632 | tf_op jit(solution)/shard_map/ppermute | solution.py:626
  56.5 17.8 %collective-permute-start.12 = (bf16[8,5888]{1,0:T(8,128)(2,1)}, bf16[8,5888]{1,0:T(8,128)(2,1)S(1)}, u32[]{:S(2)}, u32[]{:S(2)}) collective-permute-start(bf16[8,5888]{1,0:T(8,128)(2,1)} %get-tuple-element.44), channel_id=1, source_target_pairs={{0,26},{2,24},{4,30},{6,28},{8,18},{10,16},{12,22},{14,20},{16,10}... | collective-permute-start | bytes 282632 | tf_op jit(solution)/shard_map/ppermute | solution.py:626
  59.0 16.6 %collective-permute-start.13 = (bf16[8,5888]{1,0:T(8,128)(2,1)}, bf16[8,5888]{1,0:T(8,128)(2,1)S(1)}, u32[]{:S(2)}, u32[]{:S(2)}) collective-permute-start(bf16[8,5888]{1,0:T(8,128)(2,1)} %get-tuple-element.45), channel_id=1, source_target_pairs={{0,28},{2,30},{4,24},{6,26},{8,20},{10,22},{12,16},{14,18},{16,12}... | collective-permute-start | bytes 282632 | tf_op jit(solution)/shard_map/ppermute | solution.py:626
  60.5 17.4 %collective-permute-start.14 = (bf16[8,5888]{1,0:T(8,128)(2,1)}, bf16[8,5888]{1,0:T(8,128)(2,1)S(1)}, u32[]{:S(2)}, u32[]{:S(2)}) collective-permute-start(bf16[8,5888]{1,0:T(8,128)(2,1)} %get-tuple-element.46), channel_id=1, source_target_pairs={{0,30},{2,28},{4,26},{6,24},{8,22},{10,20},{12,18},{14,16},{16,14}... | collective-permute-start | bytes 282632 | tf_op jit(solution)/shard_map/ppermute | solution.py:626
  77.9 0.9 copy-start.4
  83.9 19.9 %collective-permute-start.17 = (bf16[128,1408]{1,0:T(8,128)(2,1)S(1)}, bf16[128,1408]{1,0:T(8,128)(2,1)S(1)}, u32[]{:S(2)}, u32[]{:S(2)}) collective-permute-start(bf16[128,1408]{1,0:T(8,128)(2,1)S(1)} %bitcast.18), channel_id=1, source_target_pairs={{0,1},{1,0},{2,3},{3,2},{4,5},{5,4},{6,7},{7,6},{8,9},{9,8},{10,11... | collective-permute-start | bytes 1081352 | tf_op jit(solution)/shard_map/ppermute | solution.py:604
  85.1 16.4 %collective-permute-start.15 = (bf16[128,1408]{1,0:T(8,128)(2,1)S(1)}, bf16[128,1408]{1,0:T(8,128)(2,1)S(1)}, u32[]{:S(2)}, u32[]{:S(2)}) collective-permute-start(bf16[128,1408]{1,0:T(8,128)(2,1)S(1)} %bitcast.19), channel_id=1, source_target_pairs={{0,1},{1,0},{2,3},{3,2},{4,5},{5,4},{6,7},{7,6},{8,9},{9,8},{10,11... | collective-permute-start | bytes 1081352 | tf_op jit(solution)/shard_map/ppermute | solution.py:604
  85.4 4.4 %copy-start = (bf16[2,128,2816]{2,1,0:T(8,128)(2,1)S(1)}, bf16[2,128,2816]{2,1,0:T(8,128)(2,1)}, u32[]{:S(2)}) copy-start(bf16[2,128,2816]{2,1,0:T(8,128)(2,1)} %gate_ref.5) | copy-start | bytes 4325380
  85.4 4.4 %copy-start.1 = (bf16[2,128,2816]{2,1,0:T(8,128)(2,1)S(1)}, bf16[2,128,2816]{2,1,0:T(8,128)(2,1)}, u32[]{:S(2)}) copy-start(bf16[2,128,2816]{2,1,0:T(8,128)(2,1)} %up_ref.5) | copy-start | bytes 4325380
  85.4 4.4 %copy-start.2 = (s32[1,2688]{1,0:T(1,128)S(1)}, s32[1,2688]{1,0:T(1,128)}, u32[]{:S(2)}) copy-start(s32[1,2688]{1,0:T(1,128)} %get-tuple-element.50.far_ids_ref.ids_ref) | copy-start | bytes 32260
